TPU v7x, 32 devices: a whole 2x2x4 slice. The times are simulated.
32 devices in a mesh: groups: 2 (over x), slab: 16 (over z, y, core).
Axes of the slice: x: 2, y: 2, z: 4, core: 2. Of those that a mesh axis runs over, the one named last changes fastest.
Arguments:
- latents: bfloat16 [32768, 512], P(('groups', 'slab')), parts along dimension 0, may hold values from -6 to 6
- positions: float32 [3, 32768], P(None, ('groups', 'slab')), parts along dimension 1, may hold values from -5 to 5
- counts: int32 [32], P(('groups', 'slab')), parts along dimension 0, may hold values from 1 to 1024, 12288 in all
- send_rows: int32 [32, 2, 256], P(('groups', 'slab')), parts along dimension 0, may hold values from 0 to 1023, as said below
- tiles: int32 [32, 8, 4], P(('groups', 'slab')), parts along dimension 0, may hold values from 0 to 11, as said below
- w_msg: bfloat16 [2, 512, 512], replicated, may hold values from -0.25 to 0.25
- w_in: bfloat16 [2, 2, 512, 1024], replicated, may hold values from -0.1875 to 0.1875
- w_out: bfloat16 [2, 1024, 512], replicated, may hold values from -0.1875 to 0.1875
- cotangent: bfloat16 [32768, 512], P(('groups', 'slab')), parts along dimension 0, may hold values from -6 to 6
Outputs:
- final_latents: bfloat16 [32768, 512], P(('groups', 'slab')), parts along dimension 0
- grad_latents: float32 [32768, 512], P(('groups', 'slab')), parts along dimension 0
- grad_msg: float32 [4, 512, 512], P('groups', 'slab'), parts along dimension 0
- grad_in: float32 [4, 2, 512, 1024], P('groups', None, 'slab'), parts along dimension 0
- grad_out: float32 [4, 1024, 512], P('groups', 'slab'), parts along dimension 0
There are 2 independent parts, one for each index of `groups`. A program takes and returns all parts, laid end to end along the dimension named above; an argument that names none is the same for every part. Nothing has to cross between parts.
Inputs may be any that keep to these rules, and one draw needn't show every extreme that they name: Each list send_rows[s, d] holds 256 different rows and always includes rows 0 and 1023. tiles[s, t, 0] = t + 2; the 4 entries of a row differ; the first local tile lists extended tile 0 and the last local tile lists the last extended tile.
All inputs are finite; a program needn't handle non-finite values. No bound on the sum of `counts` on one device may be relied on, other than what follows from the above.
Results may differ from a plain program's by a relative error of at most 0.025.
Values may be sent and summed in bfloat16 or wider, within the bound.
No kernel may reach another device: no remote copies, remote signals or barrier semaphores. Data moves between devices by JAX's collectives and lax.ppermute only.
A program may use at most 128 MiB of HBM per device.

v0:
```python
import functools
import math

import jax
import jax.numpy as jnp
from jax import lax
from jax.experimental import pallas as pl
from jax.experimental.pallas import tpu as pltpu
from jax.sharding import PartitionSpec as P


LAYERS = 2
TILE = 128
HALO = 256
GEO = 16
BLOCK = 256
LIMIT = 24
GHOST_TILES = HALO // TILE
F32 = jnp.float32
BF16 = jnp.bfloat16


def dg(a, b, ca, cb):
    return lax.dot_general(a, b, (((ca,), (cb,)), ((), ())), preferred_element_type=F32)


def blocks(n):
    return [slice(r, r + BLOCK) for r in range(0, n, BLOCK)]


def alive_rows(count_ref, rows, start=0):
    index = lax.broadcasted_iota(jnp.int32, (rows, 1), 0) + start
    return jnp.where(index < count_ref[0], 1.0, 0.0).astype(F32)


def picks(rows_ref, d, n):
    index = lax.broadcasted_iota(jnp.int32, (n, HALO), 0)
    return jnp.where(index == rows_ref[d : d + 1, :], 1.0, 0.0).astype(BF16)


def send_kernel(count, rows, latents, positions, up, down, geo):
    n = latents.shape[0]
    x = positions[...]
    high = x.astype(BF16).astype(F32)
    rest = x - high
    middle = rest.astype(BF16).astype(F32)
    geo[...] = jnp.zeros_like(geo)
    geo[0:3, :] = high
    geo[3:6, :] = middle
    geo[6:9, :] = rest - middle
    lane = lax.broadcasted_iota(jnp.int32, (1, n), 1)
    geo[9:10, :] = jnp.where(lane < count[0], 1.0, 0.0).astype(F32)
    fields = geo[...].astype(BF16)
    for d, out in ((0, down), (1, up)):
        pick = picks(rows, d, n)
        out[0:HALO, :] = dg(pick, latents[...], 0, 0).astype(BF16)
        out[HALO : HALO + GEO, :] = jnp.zeros((GEO, out.shape[1]), BF16)
        out[HALO : HALO + GEO, 0:HALO] = dg(fields, pick, 1, 0).astype(BF16)


def pair_weight(x_column, geo):
    total = None
    for c in range(3):
        offset = x_column[:, c : c + 1] - geo[c : c + 1, :]
        total = offset * offset if total is None else total + offset * offset
    return geo[3:4, :] / (1.0 + total)


def own_kernel(
    count, tiles, latents, positions, cotangent, w_msg, w_in, w_out,
    a_own, squares, columns, update, partial, pre_part, grad_hidden,
    wide, geo,
):
    n = latents.shape[0]
    tile_count = n // TILE
    wide[...] = jnp.zeros_like(wide)
    wide[0:3, :] = positions[...]
    lane = lax.broadcasted_iota(jnp.int32, (1, n), 1)
    wide[3:4, :] = jnp.where(lane < count[0], 1.0, 0.0).astype(F32)
    for t in range(tile_count):
        part = wide[:, t * TILE : (t + 1) * TILE]
        geo[t] = part[0:8]
        columns[t * TILE : (t + 1) * TILE, :] = part.T
    a_own[...] = jnp.zeros_like(a_own)
    squares[...] = jnp.zeros_like(squares)

    def tile_step(t, _):
        rows = pl.ds(pl.multiple_of(t * TILE, TILE), TILE)
        for k in range(tiles.shape[2]):
            near = tiles[0, t, k] - GHOST_TILES

            @pl.when((near >= 0) & (near < tile_count))
            def _():
                weight = pair_weight(columns[rows, :], geo[near])
                squares[rows, :] += weight * weight
                a_own[rows, pl.ds(pl.multiple_of(near * TILE, TILE), TILE)] = weight.astype(BF16)

        return 0

    lax.fori_loop(0, tile_count, tile_step, 0)
    update[...] = dg(latents[...], w_msg[0], 1, 0).astype(BF16)
    partial[...] = dg(a_own[...], update[...], 1, 0)
    pre_part[...] = dg(latents[...], w_in[0, 0], 1, 0).astype(BF16)
    grad_delta = (cotangent[...].astype(F32) * alive_rows(count, n)).astype(BF16)
    grad_hidden[...] = dg(grad_delta, w_out[LAYERS - 1], 1, 1).astype(BF16)


def first_kernel(
    count, tiles, rows, latents, lower, upper, squares, columns, partial, pre_part, w_msg, w_in, w_out,
    a_ghost, inverse, message, hidden, slope, current, update, up, down,
    geo, sums,
):
    n = latents.shape[0]
    tile_count = n // TILE
    for side, ghost in enumerate((lower, upper)):
        fields = ghost[HALO : HALO + GEO, :].astype(F32)
        place = fields[0:3] + fields[3:6] + fields[6:9]
        for g in range(GHOST_TILES):
            cut = slice(g * TILE, (g + 1) * TILE)
            geo[side * GHOST_TILES + g, 0:3, :] = place[:, cut]
            geo[side * GHOST_TILES + g, 3:4, :] = fields[9:10, cut]
    a_ghost[...] = jnp.zeros_like(a_ghost)
    sums[...] = squares[...]

    def tile_step(t, _):
        own = pl.ds(pl.multiple_of(t * TILE, TILE), TILE)
        for k in range(tiles.shape[2]):
            index = tiles[0, t, k]
            near = jnp.where(index < GHOST_TILES, index, index - tile_count)

            @pl.when((index < GHOST_TILES) | (index >= GHOST_TILES + tile_count))
            def _():
                weight = pair_weight(columns[own, :], geo[near])
                sums[own, :] += weight * weight
                a_ghost[own, pl.ds(pl.multiple_of(near * TILE, TILE), TILE)] = weight.astype(BF16)

        return 0

    lax.fori_loop(0, tile_count, tile_step, 0)
    update_lower = dg(lower[0:HALO, :], w_msg[0], 1, 0).astype(BF16)
    update_upper = dg(upper[0:HALO, :], w_msg[0], 1, 0).astype(BF16)
    for r in blocks(n):
        inv = 1.0 / jnp.sqrt(1.0 + jnp.sum(sums[r, :], axis=1, keepdims=True))
        inverse[r, :] = jnp.broadcast_to(inv, (BLOCK, TILE))
        total = partial[r, :] + dg(a_ghost[r, 0:HALO], update_lower, 1, 0)
        total = total + dg(a_ghost[r, HALO : 2 * HALO], update_upper, 1, 0)
        mess = (total * inv).astype(BF16)
        message[r, :] = mess
        pre = pre_part[r, :].astype(F32) + dg(mess, w_in[0, 1], 1, 0)
        sigma = 1.0 / (1.0 + jnp.exp(-pre))
        hid = (pre * sigma).astype(BF16)
        hidden[r, :] = hid
        slope[r, :] = (sigma * (1.0 + pre * (1.0 - sigma))).astype(BF16)
        delta = dg(hid, w_out[0], 1, 0)
        live = alive_rows(count, BLOCK, r.start)
        cur = (latents[r, :].astype(F32) + live * delta).astype(BF16)
        current[r, :] = cur
        update[r, :] = dg(cur, w_msg[1], 1, 0).astype(BF16)
    down[...] = dg(picks(rows, 0, n), update[...], 0, 0).astype(BF16)
    up[...] = dg(picks(rows, 1, n), update[...], 0, 0).astype(BF16)


def middle_kernel(current, update, a_own, w_in, partial, pre_part):
    partial[...] = dg(a_own[...], update[...], 1, 0)
    pre_part[...] = dg(current[...], w_in[1, 0], 1, 0).astype(BF16)


def last_kernel(
    lower, upper, a_ghost, inverse, partial, pre_part, grad_hidden, w_in,
    message, hidden, grad_pre, scaled, back_lower, back_upper,
):
    n = partial.shape[0]
    for r in blocks(n):
        inv = inverse[r, 0:1]
        total = partial[r, :] + dg(a_ghost[r, 0:HALO], lower[...], 1, 0)
        total = total + dg(a_ghost[r, HALO : 2 * HALO], upper[...], 1, 0)
        mess = (total * inv).astype(BF16)
        message[r, :] = mess
        pre = pre_part[r, :].astype(F32) + dg(mess, w_in[1, 1], 1, 0)
        sigma = 1.0 / (1.0 + jnp.exp(-pre))
        hidden[r, :] = (pre * sigma).astype(BF16)
        slope = sigma * (1.0 + pre * (1.0 - sigma))
        gpre = (grad_hidden[r, :].astype(F32) * slope).astype(BF16)
        grad_pre[r, :] = gpre
        scaled[r, :] = (dg(gpre, w_in[1, 1], 1, 1) * inv).astype(BF16)
    back_lower[...] = dg(a_ghost[:, 0:HALO], scaled[...], 0, 0).astype(BF16)
    back_upper[...] = dg(a_ghost[:, HALO : 2 * HALO], scaled[...], 0, 0).astype(BF16)


def pack_rows(core, stage, value, keep, give, at, slabs):
    height, columns = value.shape
    rows, width, rest = height // slabs, keep.shape[-1], slabs // 4
    stage[0:height, 0:columns] = value
    for h in range(columns // width):
        for side in range(2):
            for far in range(rest):
                pair = (far * 2 + side) * 2
                for out, which in ((keep, core), (give, 1 - core)):
                    source = pl.ds(pl.multiple_of((pair + which) * rows, rows), rows)
                    out[side * rest + far, at : at + rows, :] = stage[source, h * width : (h + 1) * width]
        at += rows
    return at


def terms_kernel(layer, slabs, norm, *refs):
    if layer == 1:
        (count, core, before, message, hidden, grad_pre, scaled, vector, a_own, w_in, w_out,
         grad_own, direct, keep, give, final, stage, tall) = refs
    else:
        (count, core, before, message, hidden, grad_pre, scaled, vector, later, later_update, a_own, w_in,
         grad_own, direct, keep, give, stage, tall) = refs
    n = before.shape[0]
    live = alive_rows(count, n)
    grad_delta = (vector[...].astype(F32) * live).astype(BF16)
    at = 0
    if layer == 0:
        value = dg(later[...], later_update[...], 0, 0)
        at = pack_rows(core[0], tall, (value * norm).astype(BF16), keep, give, at, slabs)
    value = dg(hidden[...], grad_delta, 0, 0)
    at = pack_rows(core[0], tall, (value * norm).astype(BF16), keep, give, at, slabs)
    for left in (before, message):
        value = dg(left[...], grad_pre[...], 0, 0)
        at = pack_rows(core[0], stage, (value * norm).astype(BF16), keep, give, at, slabs)
    grad_own[...] = dg(a_own[...], scaled[...], 0, 0)
    direct[...] = vector[...].astype(F32) + dg(grad_pre[...], w_in[layer, 0], 1, 1)
    if layer == 1:
        delta = dg(hidden[...], w_out[layer], 1, 0)
        final[...] = (before[...].astype(F32) + live * delta).astype(BF16)


def turn_kernel(
    count, rows, grad_own, from_above, from_below, direct, slope, inverse, a_ghost, w_msg, w_in, w_out,
    grad_update, gradient, grad_pre, scaled, back_lower, back_upper,
):
    n = direct.shape[0]
    pick_down = picks(rows, 0, n)
    pick_up = picks(rows, 1, n)
    for r in blocks(n):
        total = grad_own[r, :] + dg(pick_up[r, :], from_above[...], 1, 0)
        total = total + dg(pick_down[r, :], from_below[...], 1, 0)
        gup = total.astype(BF16)
        grad_update[r, :] = gup
        grad = direct[r, :] + dg(gup, w_msg[1], 1, 1)
        gradient[r, :] = grad
        gdelta = (grad * alive_rows(count, BLOCK, r.start)).astype(BF16)
        gpre = (dg(gdelta, w_out[0], 1, 1) * slope[r, :].astype(F32)).astype(BF16)
        grad_pre[r, :] = gpre
        scaled[r, :] = (dg(gpre, w_in[0, 1], 1, 1) * inverse[r, 0:1]).astype(BF16)
    back_lower[...] = dg(a_ghost[:, 0:HALO], scaled[...], 0, 0).astype(BF16)
    back_upper[...] = dg(a_ghost[:, HALO : 2 * HALO], scaled[...], 0, 0).astype(BF16)


def end_kernel(
    slabs, norm, core, rows, grad_own, from_above, from_below, direct, latents, w_msg,
    gradient, keep, give, gup_all, tall,
):
    n = direct.shape[0]
    pick_down = picks(rows, 0, n)
    pick_up = picks(rows, 1, n)
    total = grad_own[...] + dg(pick_up, from_above[...], 1, 0)
    total = total + dg(pick_down, from_below[...], 1, 0)
    gup_all[...] = total.astype(BF16)
    value = dg(latents[...], gup_all[...], 0, 0)
    pack_rows(core[0], tall, (value * norm).astype(BF16), keep, give, 0, slabs)
    gradient[...] = direct[...] + dg(gup_all[...], w_msg[0], 1, 1)


VMEM = pl.BlockSpec(memory_space=pltpu.VMEM)
SMEM = pl.BlockSpec(memory_space=pltpu.SMEM)


def call(kernel, where, outs, scratch, gflops):
    def run(*args):
        return pl.pallas_call(
            kernel,
            in_specs=where,
            out_specs=[VMEM] * len(outs),
            out_shape=[jax.ShapeDtypeStruct(s, d) for s, d in outs],
            scratch_shapes=scratch,
            compiler_params=pltpu.CompilerParams(vmem_limit_bytes=LIMIT << 20),
            cost_estimate=pl.CostEstimate(flops=int(gflops * 1e9), transcendentals=0, bytes_accessed=int(gflops * 2e6)),
        )(*args)

    return run


def reduce_rows(keep, give, slabs):
    rest = slabs // 4
    me = lax.axis_index("slab")
    side, far = (me // 2) % 2, me // 4

    def take(x, i):
        return lax.dynamic_index_in_dim(x, i, 0, keepdims=False)

    def swap(x, bit):
        return lax.ppermute(x, "slab", [(i, i ^ bit) for i in range(slabs)])

    mine = (keep.astype(F32) + swap(give, 1).astype(F32)).astype(BF16)
    half = mine.reshape(2, rest, *keep.shape[1:])
    mine = (take(half, side).astype(F32) + swap(take(half, 1 - side), 2).astype(F32)).astype(BF16)
    total = take(mine, far).astype(F32)
    for d in range(1, rest):
        total = total + swap(take(mine, far ^ d), 4 * d).astype(F32)
    return total


def body(latents, positions, counts, send_rows, tiles, w_msg, w_in, w_out, cotangent):
    n, width = latents.shape
    hidden_width = w_out.shape[1]
    slabs = lax.axis_size("slab")
    norm = 1.0 / math.sqrt(slabs * n)
    rows = send_rows[0]
    core = (lax.axis_index("slab") % 2).astype(jnp.int32).reshape(1)
    up_pairs = [(i, i + 1) for i in range(slabs - 1)]
    down_pairs = [(i + 1, i) for i in range(slabs - 1)]

    def trade(up, down):
        lower = lax.ppermute(up, "slab", up_pairs)
        upper = lax.ppermute(down, "slab", down_pairs)
        return lower, upper

    row_b, row_f = ((n, width), BF16), ((n, width), F32)
    hid_b = ((n, hidden_width), BF16)
    halo_b = ((HALO, width), BF16)
    stage = pltpu.VMEM((width, hidden_width), BF16)
    tall = pltpu.VMEM((hidden_width, width), BF16)

    up, down = call(
        send_kernel, [SMEM, VMEM, VMEM, VMEM],
        [((HALO + GEO, width), BF16)] * 2, [pltpu.VMEM((GEO, n), F32)], 0.5,
    )(counts, rows, latents, positions)
    lower, upper = trade(up, down)

    a_own, squares, columns, _, partial, pre_part, grad_hidden = call(
        own_kernel, [SMEM, SMEM] + [VMEM] * 6,
        [((n, n), BF16), ((n, TILE), F32), ((n, TILE), F32), row_b, row_f, hid_b, hid_b],
        [pltpu.VMEM((TILE, n), F32), pltpu.VMEM((n // TILE, 8, TILE), F32)], 5,
    )(counts, tiles, latents, positions, cotangent, w_msg, w_in, w_out)

    a_ghost, inverse, message0, hidden0, slope0, current1, update1, up, down = call(
        first_kernel, [SMEM, SMEM] + [VMEM] * 11,
        [((n, 2 * HALO), BF16), ((n, TILE), F32), row_b, hid_b, hid_b, row_b, row_b, halo_b, halo_b],
        [pltpu.VMEM((2 * GHOST_TILES, 8, TILE), F32), pltpu.VMEM((n, TILE), F32)], 5,
    )(counts, tiles, rows, latents, lower, upper, squares, columns, partial, pre_part, w_msg, w_in, w_out)
    lower, upper = trade(up, down)

    partial, pre_part = call(middle_kernel, [VMEM] * 4, [row_f, hid_b], [], 2)(current1, update1, a_own, w_in)

    message1, hidden1, grad_pre1, scaled1, back_lower, back_upper = call(
        last_kernel, [VMEM] * 8, [row_b, hid_b, hid_b, row_b, halo_b, halo_b], [], 4,
    )(lower, upper, a_ghost, inverse, partial, pre_part, grad_hidden, w_in)
    from_below, from_above = trade(back_upper, back_lower)

    out_rows, msg_rows = hidden_width // slabs, width // slabs
    in_rows = 2 * msg_rows * (hidden_width // width)
    half = ((slabs // 2, out_rows + in_rows, width), BF16)
    grad_own, direct, keep, give, final = call(
        functools.partial(terms_kernel, 1, slabs, norm), [SMEM] * 2 + [VMEM] * 9,
        [row_f, row_f, half, half, row_b], [stage, tall], 6,
    )(counts, core, current1, message1, hidden1, grad_pre1, scaled1, cotangent, a_own, w_in, w_out)
    share1 = reduce_rows(keep, give, slabs)

    grad_update1, gradient1, grad_pre0, scaled0, back_lower, back_upper = call(
        turn_kernel, [SMEM] + [VMEM] * 11, [row_b, row_f, hid_b, row_b, halo_b, halo_b], [], 4,
    )(counts, rows, grad_own, from_above, from_below, direct, slope0, inverse, a_ghost, w_msg, w_in, w_out)
    from_below, from_above = trade(back_upper, back_lower)

    half = ((slabs // 2, msg_rows + out_rows + in_rows, width), BF16)
    grad_own, direct, keep, give = call(
        functools.partial(terms_kernel, 0, slabs, norm), [SMEM] * 2 + [VMEM] * 10,
        [row_f, row_f, half, half], [stage, tall], 6,
    )(counts, core, latents, message0, hidden0, grad_pre0, scaled0, gradient1, current1, grad_update1, a_own, w_in)
    share0 = reduce_rows(keep, give, slabs)

    half = ((slabs // 2, msg_rows, width), BF16)
    gradient, keep, give = call(
        functools.partial(end_kernel, slabs, norm), [SMEM] + [VMEM] * 7, [row_f, half, half],
        [pltpu.VMEM((n, width), BF16), tall], 2,
    )(core, rows, grad_own, from_above, from_below, direct, latents, w_msg)
    share_msg0 = reduce_rows(keep, give, slabs)

    def unpack_in(share):
        parts = share.reshape(2, hidden_width // width, msg_rows, width)
        return jnp.concatenate([parts[:, h] for h in range(hidden_width // width)], axis=-1)

    grad_msg = jnp.stack([share_msg0, share0[:msg_rows]])
    grad_out = jnp.stack([share0[msg_rows : msg_rows + out_rows], share1[:out_rows]])
    grad_in = jnp.stack([unpack_in(share0[msg_rows + out_rows :]), unpack_in(share1[out_rows:])])
    return (final, gradient, grad_msg, grad_in, grad_out)


def solution(mesh):
    placed = (
        P(("groups", "slab"), None),
        P(None, ("groups", "slab")),
        P(("groups", "slab")),
        P(("groups", "slab"), None, None),
        P(("groups", "slab"), None, None),
        P(),
        P(),
        P(),
        P(("groups", "slab"), None),
    )
    return jax.shard_map(
        body,
        mesh=mesh,
        in_specs=placed,
        out_specs=(
            P(("groups", "slab"), None),
            P(("groups", "slab"), None),
            P("groups", "slab", None),
            P("groups", None, "slab", None),
            P("groups", "slab", None),
        ),
        check_vma=False,
    )
```

profile of v0, /device:TPU:0, one launch (start us, length us, event | category | flops | bytes accessed | tf_op | source)
XLA Modules:
  0.0 178.2 jit_solution(7726124743542549978)
XLA Ops:
  3.9 1.7 shard_map.128
  5.6 2.4 %collective-permute-start = (bf16[272,512]{1,0:T(8,128)(2,1)}, bf16[272,512]{1,0:T(8,128)(2,1)S(1)}, u32[]{:S(2)}, u32[]{:S(2)}) collective-permute-start(bf16[272,512]{1,0:T(8,128)(2,1)} %get-tuple-element.48), channel_id=1, source_target_pairs={{0,1},{1,2},{2,3},{3,4},{4,5},{5,6},{6,7},{7,8},{8,9},{9,10},{10,1... | collective-permute-start | bytes 835592 | tf_op jit(solution)/shard_map/ppermute | solution.py:318
  10.0 2.2 %copy-done = bf16[2,2,512,1024]{3,2,1,0:T(8,128)(2,1)S(1)} copy-done((bf16[2,2,512,1024]{3,2,1,0:T(8,128)(2,1)S(1)}, bf16[2,2,512,1024]{3,2,1,0:T(8,128)(2,1)}, u32[]{:S(2)}) %copy-start) | copy-done | bytes 4194328
  18.2 8.5 %shard_map.129 = (bf16[1024,1024]{1,0:T(8,128)(2,1)S(1)}, f32[1024,128]{1,0:T(8,128)S(1)}, f32[1024,128]{1,0:T(8,128)S(1)}, bf16[1024,512]{1,0:T(8,128)(2,1)}, f...) custom-call(s32[1]{0:T(128)S(6)} %copy.24.count.refs_0_, ...), custom_call_target="tpu_custom_call" | custom-call | flops 5000000000 | bytes 10000000 | tf_op jit(solution)/shard_map/pallas_call | solution.py:274
  32.7 8.5 %shard_map.130 = (bf16[1024,512]{1,0:T(8,128)(2,1)S(1)}, f32[1024,128]{1,0:T(8,128)S(1)}, bf16[1024,512]{1,0:T(8,128)(2,1)S(1)}, bf16[1024,1024]{1,0:T(8,128)(2,...) custom-call(s32[1]{0:T(128)S(6)} %copy.24.count.refs_0_, ...), custom_call_target="tpu_custom_call" | custom-call | flops 5000000000 | bytes 10000000 | tf_op jit(solution)/shard_map/pallas_call | solution.py:274
  47.7 5.1 %collective-permute-start.2 = (bf16[256,512]{1,0:T(8,128)(2,1)}, bf16[256,512]{1,0:T(8,128)(2,1)S(1)}, u32[]{:S(2)}, u32[]{:S(2)}) collective-permute-start(bf16[256,512]{1,0:T(8,128)(2,1)} %get-tuple-element.55), channel_id=1, source_target_pairs={{0,1},{1,2},{2,3},{3,4},{4,5},{5,6},{6,7},{7,8},{8,9},{9,10},{10,1... | collective-permute-start | bytes 786440 | tf_op jit(solution)/shard_map/ppermute | solution.py:318
  54.4 2.2 %copy-done.2 = bf16[2,2,512,1024]{3,2,1,0:T(8,128)(2,1)S(1)} copy-done((bf16[2,2,512,1024]{3,2,1,0:T(8,128)(2,1)S(1)}, bf16[2,2,512,1024]{3,2,1,0:T(8,128)(2,1)}, u32[]{:S(2)}) %copy-start.2) | copy-done | bytes 4194328
  60.6 2.3 %shard_map.131 = (f32[1024,512]{1,0:T(8,128)S(1)}, bf16[1024,1024]{1,0:T(8,128)(2,1)S(1)}) custom-call(bf16[1024,512]{1,0:T(8,128)(2,1)S(1)} %copy-done.16, bf16[1024,512]{1,0:T(8,128)(2,1)S(1)} %copy-done.18, bf16[1024,1024]{1,0:T(8,128)(2,1)S(1)} %copy-done.9, bf16[2,2,512,1024]{3,2,1,0:T(8,128)(2,1)S(1)} %copy-done.2), custom_call_target="tpu_custom_call" | custom-call | flops 2000000000 | bytes 4000000 | tf_op jit(solution)/shard_map/pallas_call | solution.py:274
  63.0 6.2 %shard_map.132 = (bf16[1024,512]{1,0:T(8,128)(2,1)S(1)}, bf16[1024,1024]{1,0:T(8,128)(2,1)S(1)}, bf16[1024,1024]{1,0:T(8,128)(2,1)S(1)}, bf16[1024,512]{1,0:T(8,...) custom-call(bf16[256,512]{1,0:T(8,128)(2,1)S(1)} %collective-permute-done.2.lower, ...), custom_call_target="tpu_custom_call" | custom-call | flops 4000000000 | bytes 8000000 | tf_op jit(solution)/shard_map/pallas_call | solution.py:274
  70.5 5.1 %collective-permute-start.5 = (bf16[256,512]{1,0:T(8,128)(2,1)S(1)}, bf16[256,512]{1,0:T(8,128)(2,1)S(1)}, u32[]{:S(2)}, u32[]{:S(2)}) collective-permute-start(bf16[256,512]{1,0:T(8,128)(2,1)S(1)} %get-tuple-element.73), channel_id=1, source_target_pairs={{0,1},{1,2},{2,3},{3,4},{4,5},{5,6},{6,7},{7,8},{8,9},{9,10},{10,1... | collective-permute-start | bytes 786440 | tf_op jit(solution)/shard_map/ppermute | solution.py:318
  75.7 7.8 %shard_map.133 = (f32[1024,512]{1,0:T(8,128)S(1)}, f32[1024,512]{1,0:T(8,128)S(1)}, bf16[8,192,512]{2,1,0:T(8,128)(2,1)S(1)}, bf16[8,192,512]{2,1,0:T(8,128)(2,1)}, bf16[1024,512]{1,0:T(8,128)(2,1)}) custom-call(s32[1]{0:T(128)S(6)} %copy.24.count.refs_0_, s32[1]{0:T(128)} %bitcast.refs_1_.core, bf16[1024,512]{1,0:T(8,128)(2,1)S(1)} %copy-done.16, ...), custom_call_target="tpu_custom_call" | custom-call | flops 6000000000 | bytes 12000000 | tf_op jit(solution)/shard_map/pallas_call | solution.py:274
  83.5 1.7 collective-permute-start.18
  85.3 4.6 %shard_map.134 = (bf16[1024,512]{1,0:T(8,128)(2,1)S(1)}, f32[1024,512]{1,0:T(8,128)S(1)}, bf16[1024,1024]{1,0:T(8,128)(2,1)S(1)}, bf16[1024,512]{1,0:T(8,128)(2,...) custom-call(s32[1]{0:T(128)S(6)} %copy.24.count.refs_0_, s32[2,256]{1,0:T(2,128)S(1)} %bitcast.79, ...), custom_call_target="tpu_custom_call" | custom-call | flops 4000000000 | bytes 8000000 | tf_op jit(solution)/shard_map/pallas_call | solution.py:274
  91.2 3.3 %collective-permute-start.7 = (bf16[256,512]{1,0:T(8,128)(2,1)S(1)}, bf16[256,512]{1,0:T(8,128)(2,1)S(1)}, u32[]{:S(2)}, u32[]{:S(2)}) collective-permute-start(bf16[256,512]{1,0:T(8,128)(2,1)S(1)} %get-tuple-element.82), channel_id=1, source_target_pairs={{0,1},{1,2},{2,3},{3,4},{4,5},{5,6},{6,7},{7,8},{8,9},{9,10},{10,1... | collective-permute-start | bytes 786440 | tf_op jit(solution)/shard_map/ppermute | solution.py:318
  94.6 6.3 %shard_map.135 = (f32[1024,512]{1,0:T(8,128)S(1)}, f32[1024,512]{1,0:T(8,128)S(1)}, bf16[8,224,512]{2,1,0:T(8,128)(2,1)S(1)}, bf16[8,224,512]{2,1,0:T(8,128)(2,1)}) custom-call(s32[1]{0:T(128)S(6)} %copy.24.count.refs_0_, s32[1]{0:T(128)} %bitcast.refs_1_.core, bf16[1024,512]{1,0:T(8,128)(2,1)S(1)} %copy-done.29, bf16[1024,512]{1,0:T(8,128)(2,1)S(1)} %copy-done.41, ...), custom_call_target="tpu_custom_call" | custom-call | flops 6000000000 | bytes 12000000 | tf_op jit(solution)/shard_map/pallas_call | solution.py:274
  100.9 3.0 %collective-permute-start.13 = (bf16[8,224,512]{2,1,0:T(8,128)(2,1)}, bf16[8,224,512]{2,1,0:T(8,128)(2,1)}, u32[]{:S(2)}, u32[]{:S(2)}) collective-permute-start(bf16[8,224,512]{2,1,0:T(8,128)(2,1)} %get-tuple-element.88), channel_id=1, source_target_pairs={{0,1},{1,0},{2,3},{3,2},{4,5},{5,4},{6,7},{7,6},{8,9},{9,8},{10,11... | collective-permute-start | bytes 5505032 | tf_op jit(solution)/shard_map/ppermute | solution.py:296
  103.9 3.1 %shard_map.136 = (f32[1024,512]{1,0:T(8,128)}, bf16[8,32,512]{2,1,0:T(8,128)(2,1)S(1)}, bf16[8,32,512]{2,1,0:T(8,128)(2,1)}) custom-call(s32[1]{0:T(128)} %bitcast.refs_1_.core, s32[2,256]{1,0:T(2,128)S(1)} %bitcast.80, f32[1024,512]{1,0:T(8,128)S(1)} %get-tuple-element.80.grad_own, bf16[256,512]{1,0:T(8,128)(2,1)S(1)} %collective-permute-done.6.from_above, ...), custom_call_target="tpu_custom_call" | custom-call | flops 2000000000 | bytes 4000000 | tf_op jit(solution)/shard_map/pallas_call | solution.py:274
  107.8 1.8 %collective-permute-done.8 = bf16[8,32,512]{2,1,0:T(8,128)(2,1)} collective-permute-done((bf16[8,32,512]{2,1,0:T(8,128)(2,1)}, bf16[8,32,512]{2,1,0:T(8,128)(2,1)}, u32[]{:S(2)}, u32[]{:S(2)}) %collective-permute-start.8) | collective-permute-done | bytes 262176 | tf_op jit(solution)/shard_map/ppermute | solution.py:296
  110.7 2.6 %collective-permute-start.9 = (bf16[4,32,512]{2,1,0:T(8,128)(2,1)S(1)}, bf16[4,32,512]{2,1,0:T(8,128)(2,1)S(1)}, u32[]{:S(2)}, u32[]{:S(2)}) collective-permute-start(bf16[4,32,512]{2,1,0:T(8,128)(2,1)S(1)} %dynamic-slice_bitcast_fusion.8), channel_id=1, source_target_pairs={{0,2},{1,3},{2,0},{3,1},{4,6},{5,7},{6,4},{7,5},{8,10},{9,11},{10,... | collective-permute-start | bytes 393224 | tf_op jit(solution)/shard_map/ppermute | solution.py:296
  113.3 1.8 %add_convert_fusion.1 = bf16[8,192,512]{2,1,0:T(8,128)(2,1)S(1)} fusion(bf16[8,192,512]{2,1,0:T(8,128)(2,1)} %collective-permute-done.18, bf16[8,192,512]{2,1,0:T(8,128)(2,1)S(1)} %copy-done.12), kind=kLoop, calls=%fused_computation.1 | loop fusion | flops 3145728 | bytes 4718592 | tf_op jit(solution)/shard_map/convert_element_type | solution.py:298
  115.4 1.8 %collective-permute-done.9 = bf16[4,32,512]{2,1,0:T(8,128)(2,1)S(1)} collective-permute-done((bf16[4,32,512]{2,1,0:T(8,128)(2,1)S(1)}, bf16[4,32,512]{2,1,0:T(8,128)(2,1)S(1)}, u32[]{:S(2)}, u32[]{:S(2)}) %collective-permute-start.9) | collective-permute-done | bytes 131104 | tf_op jit(solution)/shard_map/ppermute | solution.py:296
  117.2 1.6 collective-permute-start.10
  118.9 2.1 %collective-permute-start.11 = (bf16[32,512]{1,0:T(8,128)(2,1)S(1)}, bf16[32,512]{1,0:T(8,128)(2,1)S(1)}, u32[]{:S(2)}, u32[]{:S(2)}) collective-permute-start(bf16[32,512]{1,0:T(8,128)(2,1)S(1)} %get-tuple-element.103), channel_id=1, source_target_pairs={{0,8},{1,9},{2,10},{3,11},{4,12},{5,13},{6,14},{7,15},{8,0},{9,1},... | collective-permute-start | bytes 98312 | tf_op jit(solution)/shard_map/ppermute | solution.py:296
  121.7 2.0 %add_convert_fusion = bf16[8,224,512]{2,1,0:T(8,128)(2,1)S(1)} fusion(bf16[8,224,512]{2,1,0:T(8,128)(2,1)} %collective-permute-done.13, bf16[8,224,512]{2,1,0:T(8,128)(2,1)S(1)} %get-tuple-element.87), kind=kLoop, calls=%fused_computation | loop fusion | flops 3670016 | bytes 5505024 | tf_op jit(solution)/shard_map/convert_element_type | solution.py:298
  123.8 2.5 %collective-permute-start.14 = (bf16[4,224,512]{2,1,0:T(8,128)(2,1)S(1)}, bf16[4,224,512]{2,1,0:T(8,128)(2,1)S(1)}, u32[]{:S(2)}, u32[]{:S(2)}) collective-permute-start(bf16[4,224,512]{2,1,0:T(8,128)(2,1)S(1)} %dynamic-slice_bitcast_fusion), channel_id=1, source_target_pairs={{0,2},{1,3},{2,0},{3,1},{4,6},{5,7},{6,4},{7,5},{8,10},{9,11},{10,... | collective-permute-start | bytes 2752520 | tf_op jit(solution)/shard_map/ppermute | solution.py:296
  126.3 9.4 %collective-permute-done.19 = bf16[4,192,512]{2,1,0:T(8,128)(2,1)S(1)} collective-permute-done((bf16[4,192,512]{2,1,0:T(8,128)(2,1)S(1)}, bf16[4,192,512]{2,1,0:T(8,128)(2,1)S(1)}, u32[]{:S(2)}, u32[]{:S(2)}) %collective-permute-start.19) | collective-permute-done | bytes 786464 | tf_op jit(solution)/shard_map/ppermute | solution.py:296
  138.8 1.7 collective-permute-start.22
  140.5 2.8 %collective-permute-done.20 = bf16[192,512]{1,0:T(8,128)(2,1)S(1)} collective-permute-done((bf16[192,512]{1,0:T(8,128)(2,1)S(1)}, bf16[192,512]{1,0:T(8,128)(2,1)S(1)}, u32[]{:S(2)}, u32[]{:S(2)}) %collective-permute-start.20) | collective-permute-done | bytes 196640 | tf_op jit(solution)/shard_map/ppermute | solution.py:296
  143.3 10.2 %collective-permute-done.21 = bf16[192,512]{1,0:T(8,128)(2,1)S(1)} collective-permute-done((bf16[192,512]{1,0:T(8,128)(2,1)S(1)}, bf16[192,512]{1,0:T(8,128)(2,1)S(1)}, u32[]{:S(2)}, u32[]{:S(2)}) %collective-permute-start.21) | collective-permute-done | bytes 196640 | tf_op jit(solution)/shard_map/ppermute | solution.py:296
  154.6 2.2 %collective-permute-start.15 = (bf16[224,512]{1,0:T(8,128)(2,1)S(1)}, bf16[224,512]{1,0:T(8,128)(2,1)S(1)}, u32[]{:S(2)}, u32[]{:S(2)}) collective-permute-start(bf16[224,512]{1,0:T(8,128)(2,1)S(1)} %get-tuple-element.91), channel_id=1, source_target_pairs={{0,4},{1,5},{2,6},{3,7},{4,0},{5,1},{6,2},{7,3},{8,12},{9,13},{10,... | collective-permute-start | bytes 688136 | tf_op jit(solution)/shard_map/ppermute | solution.py:296
  159.3 5.2 %collective-permute-done.15 = bf16[224,512]{1,0:T(8,128)(2,1)S(1)} collective-permute-done((bf16[224,512]{1,0:T(8,128)(2,1)S(1)}, bf16[224,512]{1,0:T(8,128)(2,1)S(1)}, u32[]{:S(2)}, u32[]{:S(2)}) %collective-permute-start.15) | collective-permute-done | bytes 229408 | tf_op jit(solution)/shard_map/ppermute | solution.py:296
  164.5 11.3 %collective-permute-done.16 = bf16[224,512]{1,0:T(8,128)(2,1)S(1)} collective-permute-done((bf16[224,512]{1,0:T(8,128)(2,1)S(1)}, bf16[224,512]{1,0:T(8,128)(2,1)S(1)}, u32[]{:S(2)}, u32[]{:S(2)}) %collective-permute-start.16) | collective-permute-done | bytes 229408 | tf_op jit(solution)/shard_map/ppermute | solution.py:296
  (135 shorter events, 43.1 us)
Async XLA Ops:
  5.6 23.8 %collective-permute-start = (bf16[272,512]{1,0:T(8,128)(2,1)}, bf16[272,512]{1,0:T(8,128)(2,1)S(1)}, u32[]{:S(2)}, u32[]{:S(2)}) collective-permute-start(bf16[272,512]{1,0:T(8,128)(2,1)} %get-tuple-element.48), channel_id=1, source_target_pairs={{0,1},{1,2},{2,3},{3,4},{4,5},{5,6},{6,7},{7,8},{8,9},{9,10},{10,1... | collective-permute-start | bytes 835592 | tf_op jit(solution)/shard_map/ppermute | solution.py:318
  8.0 22.1 %collective-permute-start.1 = (bf16[272,512]{1,0:T(8,128)(2,1)S(1)}, bf16[272,512]{1,0:T(8,128)(2,1)S(1)}, u32[]{:S(2)}, u32[]{:S(2)}) collective-permute-start(bf16[272,512]{1,0:T(8,128)(2,1)S(1)} %get-tuple-element.49), channel_id=1, source_target_pairs={{1,0},{2,1},{3,2},{4,3},{5,4},{6,5},{7,6},{8,7},{9,8},{10,9},{11,1... | collective-permute-start | bytes 835592 | tf_op jit(solution)/shard_map/ppermute | solution.py:319
  18.2 12.6 %copy-start.1 = (bf16[2,2,512,1024]{3,2,1,0:T(8,128)(2,1)S(1)}, bf16[2,2,512,1024]{3,2,1,0:T(8,128)(2,1)}, u32[]{:S(2)}) copy-start(bf16[2,2,512,1024]{3,2,1,0:T(8,128)(2,1)} %refs_11_.1) | copy-start | bytes 12582916
  18.2 12.6 %copy-start.5 = (bf16[2,1024,512]{2,1,0:T(8,128)(2,1)S(1)}, bf16[2,1024,512]{2,1,0:T(8,128)(2,1)}, u32[]{:S(2)}) copy-start(bf16[2,1024,512]{2,1,0:T(8,128)(2,1)} %w_out.5) | copy-start | bytes 6291460
  18.2 12.6 %copy-start.23 = (s32[1,2,256]{2,1,0:T(2,128)S(1)}, s32[1,2,256]{2,1,0:T(2,128)}, u32[]{:S(2)}) copy-start(s32[1,2,256]{2,1,0:T(2,128)} %param.12) | copy-start | bytes 6148
  18.2 12.6 %copy-start.28 = (bf16[1024,512]{1,0:T(8,128)(2,1)S(1)}, bf16[1024,512]{1,0:T(8,128)(2,1)}, u32[]{:S(2)}) copy-start(bf16[1024,512]{1,0:T(8,128)(2,1)} %latents.7) | copy-start | bytes 3145732
  47.7 15.2 %collective-permute-start.2 = (bf16[256,512]{1,0:T(8,128)(2,1)}, bf16[256,512]{1,0:T(8,128)(2,1)S(1)}, u32[]{:S(2)}, u32[]{:S(2)}) collective-permute-start(bf16[256,512]{1,0:T(8,128)(2,1)} %get-tuple-element.55), channel_id=1, source_target_pairs={{0,1},{1,2},{2,3},{3,4},{4,5},{5,6},{6,7},{7,8},{8,9},{9,10},{10,1... | collective-permute-start | bytes 786440 | tf_op jit(solution)/shard_map/ppermute | solution.py:318
  52.8 10.1 %collective-permute-start.3 = (bf16[256,512]{1,0:T(8,128)(2,1)}, bf16[256,512]{1,0:T(8,128)(2,1)}, u32[]{:S(2)}, u32[]{:S(2)}) collective-permute-start(bf16[256,512]{1,0:T(8,128)(2,1)} %get-tuple-element.56), channel_id=1, source_target_pairs={{1,0},{2,1},{3,2},{4,3},{5,4},{6,5},{7,6},{8,7},{9,8},{10,9},{11,1... | collective-permute-start | bytes 786440 | tf_op jit(solution)/shard_map/ppermute | solution.py:319
  63.0 12.7 %copy-start.3 = (bf16[2,2,512,1024]{3,2,1,0:T(8,128)(2,1)S(1)}, bf16[2,2,512,1024]{3,2,1,0:T(8,128)(2,1)}, u32[]{:S(2)}) copy-start(bf16[2,2,512,1024]{3,2,1,0:T(8,128)(2,1)} %refs_11_.1) | copy-start | bytes 12582916
  63.0 12.7 %copy-start.10 = (bf16[1024,1024]{1,0:T(8,128)(2,1)S(1)}, bf16[1024,1024]{1,0:T(8,128)(2,1)}, u32[]{:S(2)}) copy-start(bf16[1024,1024]{1,0:T(8,128)(2,1)} %copy-done.8) | copy-start | bytes 6291460
  63.0 12.7 %copy-start.25 = (bf16[1024,512]{1,0:T(8,128)(2,1)S(1)}, bf16[1024,512]{1,0:T(8,128)(2,1)}, u32[]{:S(2)}) copy-start(bf16[1024,512]{1,0:T(8,128)(2,1)} %refs_7_.1) | copy-start | bytes 3145732
  69.2 16.0 %collective-permute-start.4 = (bf16[256,512]{1,0:T(8,128)(2,1)S(1)}, bf16[256,512]{1,0:T(8,128)(2,1)S(1)}, u32[]{:S(2)}, u32[]{:S(2)}) collective-permute-start(bf16[256,512]{1,0:T(8,128)(2,1)S(1)} %get-tuple-element.72), channel_id=1, source_target_pairs={{1,0},{2,1},{3,2},{4,3},{5,4},{6,5},{7,6},{8,7},{9,8},{10,9},{11,1... | collective-permute-start | bytes 786440 | tf_op jit(solution)/shard_map/ppermute | solution.py:319
  70.5 14.7 %collective-permute-start.5 = (bf16[256,512]{1,0:T(8,128)(2,1)S(1)}, bf16[256,512]{1,0:T(8,128)(2,1)S(1)}, u32[]{:S(2)}, u32[]{:S(2)}) collective-permute-start(bf16[256,512]{1,0:T(8,128)(2,1)S(1)} %get-tuple-element.73), channel_id=1, source_target_pairs={{0,1},{1,2},{2,3},{3,4},{4,5},{5,6},{6,7},{7,8},{8,9},{9,10},{10,1... | collective-permute-start | bytes 786440 | tf_op jit(solution)/shard_map/ppermute | solution.py:318
  75.7 9.6 %copy-start.7 = (bf16[1024,1024]{1,0:T(8,128)(2,1)S(1)}, bf16[1024,1024]{1,0:T(8,128)(2,1)}, u32[]{:S(2)}) copy-start(bf16[1024,1024]{1,0:T(8,128)(2,1)} %copy-done.6) | copy-start | bytes 6291460
  75.7 9.6 %copy-start.14 = (bf16[2,512,512]{2,1,0:T(8,128)(2,1)S(1)}, bf16[2,512,512]{2,1,0:T(8,128)(2,1)}, u32[]{:S(2)}) copy-start(bf16[2,512,512]{2,1,0:T(8,128)(2,1)} %w_msg.7) | copy-start | bytes 3145732
  83.5 29.8 %collective-permute-start.18 = (bf16[8,192,512]{2,1,0:T(8,128)(2,1)}, bf16[8,192,512]{2,1,0:T(8,128)(2,1)}, u32[]{:S(2)}, u32[]{:S(2)}) collective-permute-start(bf16[8,192,512]{2,1,0:T(8,128)(2,1)} %get-tuple-element.90), channel_id=1, source_target_pairs={{0,1},{1,0},{2,3},{3,2},{4,5},{5,4},{6,7},{7,6},{8,9},{9,8},{10,11... | collective-permute-start | bytes 4718600 | tf_op jit(solution)/shard_map/ppermute | solution.py:296
  89.9 14.0 %collective-permute-start.6 = (bf16[256,512]{1,0:T(8,128)(2,1)S(1)}, bf16[256,512]{1,0:T(8,128)(2,1)S(1)}, u32[]{:S(2)}, u32[]{:S(2)}) collective-permute-start(bf16[256,512]{1,0:T(8,128)(2,1)S(1)} %get-tuple-element.81), channel_id=1, source_target_pairs={{1,0},{2,1},{3,2},{4,3},{5,4},{6,5},{7,6},{8,7},{9,8},{10,9},{11,1... | collective-permute-start | bytes 786440 | tf_op jit(solution)/shard_map/ppermute | solution.py:319
  91.2 12.7 %collective-permute-start.7 = (bf16[256,512]{1,0:T(8,128)(2,1)S(1)}, bf16[256,512]{1,0:T(8,128)(2,1)S(1)}, u32[]{:S(2)}, u32[]{:S(2)}) collective-permute-start(bf16[256,512]{1,0:T(8,128)(2,1)S(1)} %get-tuple-element.82), channel_id=1, source_target_pairs={{0,1},{1,2},{2,3},{3,4},{4,5},{5,6},{6,7},{7,8},{8,9},{9,10},{10,1... | collective-permute-start | bytes 786440 | tf_op jit(solution)/shard_map/ppermute | solution.py:318
  100.9 20.8 %collective-permute-start.13 = (bf16[8,224,512]{2,1,0:T(8,128)(2,1)}, bf16[8,224,512]{2,1,0:T(8,128)(2,1)}, u32[]{:S(2)}, u32[]{:S(2)}) collective-permute-start(bf16[8,224,512]{2,1,0:T(8,128)(2,1)} %get-tuple-element.88), channel_id=1, source_target_pairs={{0,1},{1,0},{2,3},{3,2},{4,5},{5,4},{6,7},{7,6},{8,9},{9,8},{10,11... | collective-permute-start | bytes 5505032 | tf_op jit(solution)/shard_map/ppermute | solution.py:296
  107.7 1.9 %collective-permute-start.8 = (bf16[8,32,512]{2,1,0:T(8,128)(2,1)}, bf16[8,32,512]{2,1,0:T(8,128)(2,1)}, u32[]{:S(2)}, u32[]{:S(2)}) collective-permute-start(bf16[8,32,512]{2,1,0:T(8,128)(2,1)} %get-tuple-element.86), channel_id=1, source_target_pairs={{0,1},{1,0},{2,3},{3,2},{4,5},{5,4},{6,7},{7,6},{8,9},{9,8},{10,11... | collective-permute-start | bytes 786440 | tf_op jit(solution)/shard_map/ppermute | solution.py:296
  110.7 6.4 %collective-permute-start.9 = (bf16[4,32,512]{2,1,0:T(8,128)(2,1)S(1)}, bf16[4,32,512]{2,1,0:T(8,128)(2,1)S(1)}, u32[]{:S(2)}, u32[]{:S(2)}) collective-permute-start(bf16[4,32,512]{2,1,0:T(8,128)(2,1)S(1)} %dynamic-slice_bitcast_fusion.8), channel_id=1, source_target_pairs={{0,2},{1,3},{2,0},{3,1},{4,6},{5,7},{6,4},{7,5},{8,10},{9,11},{10,... | collective-permute-start | bytes 393224 | tf_op jit(solution)/shard_map/ppermute | solution.py:296
  115.3 20.5 %collective-permute-start.19 = (bf16[4,192,512]{2,1,0:T(8,128)(2,1)S(1)}, bf16[4,192,512]{2,1,0:T(8,128)(2,1)S(1)}, u32[]{:S(2)}, u32[]{:S(2)}) collective-permute-start(bf16[4,192,512]{2,1,0:T(8,128)(2,1)S(1)} %dynamic-slice_bitcast_fusion.1), channel_id=1, source_target_pairs={{0,2},{1,3},{2,0},{3,1},{4,6},{5,7},{6,4},{7,5},{8,10},{9,11},{10,... | collective-permute-start | bytes 2359304 | tf_op jit(solution)/shard_map/ppermute | solution.py:296
  117.2 20.4 %collective-permute-start.10 = (bf16[32,512]{1,0:T(8,128)(2,1)S(1)}, bf16[32,512]{1,0:T(8,128)(2,1)S(1)}, u32[]{:S(2)}, u32[]{:S(2)}) collective-permute-start(bf16[32,512]{1,0:T(8,128)(2,1)S(1)} %get-tuple-element.101), channel_id=1, source_target_pairs={{0,4},{1,5},{2,6},{3,7},{4,0},{5,1},{6,2},{7,3},{8,12},{9,13},{10,... | collective-permute-start | bytes 98312 | tf_op jit(solution)/shard_map/ppermute | solution.py:296
  118.9 19.9 %collective-permute-start.11 = (bf16[32,512]{1,0:T(8,128)(2,1)S(1)}, bf16[32,512]{1,0:T(8,128)(2,1)S(1)}, u32[]{:S(2)}, u32[]{:S(2)}) collective-permute-start(bf16[32,512]{1,0:T(8,128)(2,1)S(1)} %get-tuple-element.103), channel_id=1, source_target_pairs={{0,8},{1,9},{2,10},{3,11},{4,12},{5,13},{6,14},{7,15},{8,0},{9,1},... | collective-permute-start | bytes 98312 | tf_op jit(solution)/shard_map/ppermute | solution.py:296
  121.0 19.5 %collective-permute-start.12 = (bf16[32,512]{1,0:T(8,128)(2,1)S(1)}, bf16[32,512]{1,0:T(8,128)(2,1)S(1)}, u32[]{:S(2)}, u32[]{:S(2)}) collective-permute-start(bf16[32,512]{1,0:T(8,128)(2,1)S(1)} %get-tuple-element.102), channel_id=1, source_target_pairs={{0,12},{1,13},{2,14},{3,15},{4,8},{5,9},{6,10},{7,11},{8,4},{9,5},... | collective-permute-start | bytes 98312 | tf_op jit(solution)/shard_map/ppermute | solution.py:296
  123.8 30.5 %collective-permute-start.14 = (bf16[4,224,512]{2,1,0:T(8,128)(2,1)S(1)}, bf16[4,224,512]{2,1,0:T(8,128)(2,1)S(1)}, u32[]{:S(2)}, u32[]{:S(2)}) collective-permute-start(bf16[4,224,512]{2,1,0:T(8,128)(2,1)S(1)} %dynamic-slice_bitcast_fusion), channel_id=1, source_target_pairs={{0,2},{1,3},{2,0},{3,1},{4,6},{5,7},{6,4},{7,5},{8,10},{9,11},{10,... | collective-permute-start | bytes 2752520 | tf_op jit(solution)/shard_map/ppermute | solution.py:296
  136.0 7.2 %collective-permute-start.20 = (bf16[192,512]{1,0:T(8,128)(2,1)S(1)}, bf16[192,512]{1,0:T(8,128)(2,1)S(1)}, u32[]{:S(2)}, u32[]{:S(2)}) collective-permute-start(bf16[192,512]{1,0:T(8,128)(2,1)S(1)} %get-tuple-element.94), channel_id=1, source_target_pairs={{0,4},{1,5},{2,6},{3,7},{4,0},{5,1},{6,2},{7,3},{8,12},{9,13},{10,... | collective-permute-start | bytes 589832 | tf_op jit(solution)/shard_map/ppermute | solution.py:296
  137.7 15.8 %collective-permute-start.21 = (bf16[192,512]{1,0:T(8,128)(2,1)S(1)}, bf16[192,512]{1,0:T(8,128)(2,1)S(1)}, u32[]{:S(2)}, u32[]{:S(2)}) collective-permute-start(bf16[192,512]{1,0:T(8,128)(2,1)S(1)} %get-tuple-element.96), channel_id=1, source_target_pairs={{0,8},{1,9},{2,10},{3,11},{4,12},{5,13},{6,14},{7,15},{8,0},{9,1},... | collective-permute-start | bytes 589832 | tf_op jit(solution)/shard_map/ppermute | solution.py:296
  138.8 14.7 %collective-permute-start.22 = (bf16[192,512]{1,0:T(8,128)(2,1)S(1)}, bf16[192,512]{1,0:T(8,128)(2,1)S(1)}, u32[]{:S(2)}, u32[]{:S(2)}) collective-permute-start(bf16[192,512]{1,0:T(8,128)(2,1)S(1)} %get-tuple-element.95), channel_id=1, source_target_pairs={{0,12},{1,13},{2,14},{3,15},{4,8},{5,9},{6,10},{7,11},{8,4},{9,5},... | collective-permute-start | bytes 589832 | tf_op jit(solution)/shard_map/ppermute | solution.py:296
  154.6 9.8 %collective-permute-start.15 = (bf16[224,512]{1,0:T(8,128)(2,1)S(1)}, bf16[224,512]{1,0:T(8,128)(2,1)S(1)}, u32[]{:S(2)}, u32[]{:S(2)}) collective-permute-start(bf16[224,512]{1,0:T(8,128)(2,1)S(1)} %get-tuple-element.91), channel_id=1, source_target_pairs={{0,4},{1,5},{2,6},{3,7},{4,0},{5,1},{6,2},{7,3},{8,12},{9,13},{10,... | collective-permute-start | bytes 688136 | tf_op jit(solution)/shard_map/ppermute | solution.py:296
  156.8 18.9 %collective-permute-start.16 = (bf16[224,512]{1,0:T(8,128)(2,1)S(1)}, bf16[224,512]{1,0:T(8,128)(2,1)S(1)}, u32[]{:S(2)}, u32[]{:S(2)}) collective-permute-start(bf16[224,512]{1,0:T(8,128)(2,1)S(1)} %get-tuple-element.93), channel_id=1, source_target_pairs={{0,8},{1,9},{2,10},{3,11},{4,12},{5,13},{6,14},{7,15},{8,0},{9,1},... | collective-permute-start | bytes 688136 | tf_op jit(solution)/shard_map/ppermute | solution.py:296
  157.9 17.8 %collective-permute-start.17 = (bf16[224,512]{1,0:T(8,128)(2,1)S(1)}, bf16[224,512]{1,0:T(8,128)(2,1)S(1)}, u32[]{:S(2)}, u32[]{:S(2)}) collective-permute-start(bf16[224,512]{1,0:T(8,128)(2,1)S(1)} %get-tuple-element.92), channel_id=1, source_target_pairs={{0,12},{1,13},{2,14},{3,15},{4,8},{5,9},{6,10},{7,11},{8,4},{9,5},... | collective-permute-start | bytes 688136 | tf_op jit(solution)/shard_map/ppermute | solution.py:296
  (33 other events, 78.7 us)
where the time goes:
time: 179 us; the launch traced here: 178 us
  Pallas kernels  49.1 us (27%)
  starting transfers between devices  44.9 us (25%)
  waiting for transfers between devices  43.1 us (24%)
  local copies, waits for them, and re-layouts  31.3 us (17%)
  other arithmetic  8 us (4%)
  between operations  1.8 us (1%)
    pallas_call x9, Pallas kernels, run(): pl.pallas_call(kernel, in_specs=where, out_specs=[VMEM] * len(outs), out_...  49.1 us
    ppermute x15, waiting for transfers between devices, swap(): return lax.ppermute(x, 'slab', [(i, i ^ bit) for i in range(slabs)])  43.1 us
    unnamed x85, local copies, waits for them, and re-layouts  31 us
    ppermute x15, starting transfers between devices, swap(): return lax.ppermute(x, 'slab', [(i, i ^ bit) for i in range(slabs)])  23.5 us
    ppermute x4, starting transfers between devices, trade(): lower = lax.ppermute(up, 'slab', up_pairs)  16 us
    ppermute x4, starting transfers between devices, trade(): upper = lax.ppermute(down, 'slab', down_pairs)  5.35 us
    convert_element_type x3, other arithmetic, reduce_rows(): mine = (keep.astype(F32) + swap(give, 1).astype(F32)).astype(BF16)  4.96 us
  transfers between devices with their start and end apart: 23, of which 8 were waited for; matrix products, arithmetic and copies ran while one was open for 4% of the time, Pallas kernels for 18%

commit v1 on v0

v1 whole, which is shorter than its diff:
```python
import functools
import math

import jax
import jax.numpy as jnp
from jax import lax
from jax.experimental import pallas as pl
from jax.experimental.pallas import tpu as pltpu
from jax.sharding import PartitionSpec as P


TILE = 128
HALO = 256
GEO = 16
BLOCK = 256
LIMIT = 16
WHOLE = 50
GHOST_TILES = HALO // TILE
F32 = jnp.float32
BF16 = jnp.bfloat16


def dg(a, b, ca, cb):
    return lax.dot_general(a, b, (((ca,), (cb,)), ((), ())), preferred_element_type=F32)


def blocks(n):
    return [slice(r, r + BLOCK) for r in range(0, n, BLOCK)]


def alive_rows(count, rows, start=0):
    index = lax.broadcasted_iota(jnp.int32, (rows, 1), 0) + start
    return jnp.where(index < count[0], 1.0, 0.0).astype(F32)


def picks(rows, d, n):
    index = lax.broadcasted_iota(jnp.int32, (n, HALO), 0)
    return jnp.where(index == rows[pl.ds(d, 1), :], 1.0, 0.0).astype(BF16)


def send_kernel(scalars, count, core, rows, latents_far, positions_far, w_msg, w_in, *refs):
    near, far, latents, positions, wm, wi, geo, sems = refs[scalars:]
    n = latents.shape[0]
    moves = ((positions_far, positions), (latents_far, latents), (w_msg.at[0], wm), (w_in.at[0, 0], wi))
    copies = [pltpu.make_async_copy(src, dst, sems.at[i]) for i, (src, dst) in enumerate(moves)]
    for copy in copies:
        copy.start()
    copies[0].wait()
    x = positions[...]
    high = x.astype(BF16).astype(F32)
    rest = x - high
    middle = rest.astype(BF16).astype(F32)
    geo[...] = jnp.zeros_like(geo)
    geo[0:3, :] = high
    geo[3:6, :] = middle
    geo[6:9, :] = rest - middle
    lane = lax.broadcasted_iota(jnp.int32, (1, n), 1)
    geo[9:10, :] = jnp.where(lane < count[0], 1.0, 0.0).astype(F32)
    fields = geo[...].astype(BF16)
    copies[1].wait()
    for d, out in ((1 - core[0], near), (core[0], far)):
        pick = picks(rows, d, n)
        out[0:HALO, :] = dg(pick, latents[...], 0, 0).astype(BF16)
        out[HALO : HALO + GEO, :] = jnp.zeros((GEO, out.shape[1]), BF16)
        out[HALO : HALO + GEO, 0:HALO] = dg(fields, pick, 1, 0).astype(BF16)
    copies[2].wait()
    copies[3].wait()


def pair_weight(x_column, geo):
    total = None
    for c in range(3):
        offset = x_column[:, c : c + 1] - geo[c : c + 1, :]
        total = offset * offset if total is None else total + offset * offset
    return geo[3:4, :] / (1.0 + total)


def own_kernel(
    count, tiles, latents, positions, wm, wi,
    a_own, squares, columns, update, partial, pre_part,
    wide, geo,
):
    n = latents.shape[0]
    tile_count = n // TILE
    wide[...] = jnp.zeros_like(wide)
    wide[0:3, :] = positions[...]
    lane = lax.broadcasted_iota(jnp.int32, (1, n), 1)
    wide[3:4, :] = jnp.where(lane < count[0], 1.0, 0.0).astype(F32)
    for t in range(tile_count):
        part = wide[:, t * TILE : (t + 1) * TILE]
        geo[t] = part[0:8]
        columns[t * TILE : (t + 1) * TILE, :] = part.T
    a_own[...] = jnp.zeros_like(a_own)
    squares[...] = jnp.zeros_like(squares)

    def tile_step(t, _):
        rows = pl.ds(pl.multiple_of(t * TILE, TILE), TILE)
        for k in range(tiles.shape[2]):
            tile = tiles[0, t, k] - GHOST_TILES

            @pl.when((tile >= 0) & (tile < tile_count))
            def _():
                weight = pair_weight(columns[rows, :], geo[tile])
                squares[rows, :] += weight * weight
                a_own[rows, pl.ds(pl.multiple_of(tile * TILE, TILE), TILE)] = weight.astype(BF16)

        return 0

    lax.fori_loop(0, tile_count, tile_step, 0)
    update[...] = dg(latents[...], wm[...], 1, 0).astype(BF16)
    partial[...] = dg(a_own[...], update[...], 1, 0)
    pre_part[...] = dg(latents[...], wi[...], 1, 0).astype(BF16)


def first_kernel(
    count, core, tiles, rows, latents, near, far, squares, columns, partial, pre_part, wm, w_in, w_out, w_msg,
    a_ghost, inverse, message, hidden, slope, current, update, send_near, send_far,
    geo, sums,
):
    n = latents.shape[0]
    tile_count = n // TILE
    for side, ghost in enumerate((near, far)):
        fields = ghost[HALO : HALO + GEO, :].astype(F32)
        place = fields[0:3] + fields[3:6] + fields[6:9]
        for g in range(GHOST_TILES):
            cut = slice(g * TILE, (g + 1) * TILE)
            geo[side * GHOST_TILES + g, 0:3, :] = place[:, cut]
            geo[side * GHOST_TILES + g, 3:4, :] = fields[9:10, cut]
    a_ghost[...] = jnp.zeros_like(a_ghost)
    sums[...] = squares[...]
    below = GHOST_TILES * (1 - core[0])
    above = GHOST_TILES * core[0] - (GHOST_TILES + tile_count)

    def tile_step(t, _):
        own = pl.ds(pl.multiple_of(t * TILE, TILE), TILE)
        for k in range(tiles.shape[2]):
            index = tiles[0, t, k]
            tile = jnp.where(index < GHOST_TILES, index + below, index + above)

            @pl.when((index < GHOST_TILES) | (index >= GHOST_TILES + tile_count))
            def _():
                weight = pair_weight(columns[own, :], geo[tile])
                sums[own, :] += weight * weight
                a_ghost[own, pl.ds(pl.multiple_of(tile * TILE, TILE), TILE)] = weight.astype(BF16)

        return 0

    lax.fori_loop(0, tile_count, tile_step, 0)
    update_near = dg(near[0:HALO, :], wm[...], 1, 0).astype(BF16)
    update_far = dg(far[0:HALO, :], wm[...], 1, 0).astype(BF16)
    for r in blocks(n):
        inv = 1.0 / jnp.sqrt(1.0 + jnp.sum(sums[r, :], axis=1, keepdims=True))
        inverse[r, :] = jnp.broadcast_to(inv, (BLOCK, TILE))
        total = partial[r, :] + dg(a_ghost[r, 0:HALO], update_near, 1, 0)
        total = total + dg(a_ghost[r, HALO : 2 * HALO], update_far, 1, 0)
        mess = (total * inv).astype(BF16)
        message[r, :] = mess
        pre = pre_part[r, :].astype(F32) + dg(mess, w_in[0, 1], 1, 0)
        sigma = 1.0 / (1.0 + jnp.exp(-pre))
        hid = (pre * sigma).astype(BF16)
        hidden[r, :] = hid
        slope[r, :] = (sigma * (1.0 + pre * (1.0 - sigma))).astype(BF16)
        delta = dg(hid, w_out[0], 1, 0)
        live = alive_rows(count, BLOCK, r.start)
        cur = (latents[r, :].astype(F32) + live * delta).astype(BF16)
        current[r, :] = cur
        update[r, :] = dg(cur, w_msg[1], 1, 0).astype(BF16)
    send_near[...] = dg(picks(rows, 1 - core[0], n), update[...], 0, 0).astype(BF16)
    send_far[...] = dg(picks(rows, core[0], n), update[...], 0, 0).astype(BF16)


def middle_kernel(
    count, current, update, a_own, cot, w_in, w_out,
    partial, pre_part, grad_delta, grad_hidden,
):
    n = current.shape[0]
    partial[...] = dg(a_own[...], update[...], 1, 0)
    pre_part[...] = dg(current[...], w_in[1, 0], 1, 0).astype(BF16)
    grad_delta[...] = (cot[...].astype(F32) * alive_rows(count, n)).astype(BF16)
    grad_hidden[...] = dg(grad_delta[...], w_out[1], 1, 1).astype(BF16)


def last_kernel(
    near, far, a_ghost, inverse, partial, pre_part, grad_hidden, w_in,
    message, hidden, grad_pre, scaled, back_near, back_far,
):
    n = partial.shape[0]
    for r in blocks(n):
        inv = inverse[r, 0:1]
        total = partial[r, :] + dg(a_ghost[r, 0:HALO], near[...], 1, 0)
        total = total + dg(a_ghost[r, HALO : 2 * HALO], far[...], 1, 0)
        mess = (total * inv).astype(BF16)
        message[r, :] = mess
        pre = pre_part[r, :].astype(F32) + dg(mess, w_in[1, 1], 1, 0)
        sigma = 1.0 / (1.0 + jnp.exp(-pre))
        hidden[r, :] = (pre * sigma).astype(BF16)
        slope = sigma * (1.0 + pre * (1.0 - sigma))
        gpre = (grad_hidden[r, :].astype(F32) * slope).astype(BF16)
        grad_pre[r, :] = gpre
        scaled[r, :] = (dg(gpre, w_in[1, 1], 1, 1) * inv).astype(BF16)
    back_near[...] = dg(a_ghost[:, 0:HALO], scaled[...], 0, 0).astype(BF16)
    back_far[...] = dg(a_ghost[:, HALO : 2 * HALO], scaled[...], 0, 0).astype(BF16)


def pack_rows(core, stage, value, keep, give, at, slabs):
    height, columns = value.shape
    rows, width, bits = height // slabs, keep.shape[-1], slabs.bit_length() - 2
    stage[0:height, 0:columns] = value
    for h in range(columns // width):
        for pair in range(slabs // 2):
            place = sum(((pair >> b) & 1) << (bits - 1 - b) for b in range(bits))
            for out, which in ((keep, core), (give, 1 - core)):
                source = pl.ds(pl.multiple_of((pair * 2 + which) * rows, rows), rows)
                out[place, at : at + rows, :] = stage[source, h * width : (h + 1) * width]
        at += rows
    return at


def terms_kernel(plan, slabs, norm, core, *refs):
    wide, tall = refs[-2:]
    outs = refs[len(refs) - 2 - 2 * len(plan) : -2]
    for c, chunk in enumerate(plan):
        at = 0
        for a, b in chunk:
            value = (dg(refs[a][...], refs[b][...], 0, 0) * norm).astype(BF16)
            stage = tall if value.shape[1] == tall.shape[1] else wide
            at = pack_rows(core[0], stage, value, outs[2 * c], outs[2 * c + 1], at, slabs)


def flow1_kernel(
    count, before, hidden, grad_pre, scaled, a_own, cot, w_in, w_out,
    grad_own, direct, final,
):
    grad_own[...] = dg(a_own[...], scaled[...], 0, 0)
    direct[...] = cot[...].astype(F32) + dg(grad_pre[...], w_in[1, 0], 1, 1)
    delta = dg(hidden[...], w_out[1], 1, 0)
    live = alive_rows(count, before.shape[0])
    final[...] = (before[...].astype(F32) + live * delta).astype(BF16)


def flow0_kernel(gradient, grad_pre, scaled, a_own, w_in, grad_own, direct):
    grad_own[...] = dg(a_own[...], scaled[...], 0, 0)
    direct[...] = gradient[...] + dg(grad_pre[...], w_in[0, 0], 1, 1)


def turn_kernel(
    count, core, rows, grad_own, near, far, direct, slope, inverse, a_ghost, w_msg, w_in, w_out,
    grad_update, gradient, grad_delta, grad_pre, scaled, back_near, back_far,
):
    n = direct.shape[0]
    pick_near = picks(rows, 1 - core[0], n)
    pick_far = picks(rows, core[0], n)
    for r in blocks(n):
        total = grad_own[r, :] + dg(pick_near[r, :], near[...], 1, 0)
        total = total + dg(pick_far[r, :], far[...], 1, 0)
        gup = total.astype(BF16)
        grad_update[r, :] = gup
        grad = direct[r, :] + dg(gup, w_msg[1], 1, 1)
        gradient[r, :] = grad
        gdelta = (grad * alive_rows(count, BLOCK, r.start)).astype(BF16)
        grad_delta[r, :] = gdelta
        gpre = (dg(gdelta, w_out[0], 1, 1) * slope[r, :].astype(F32)).astype(BF16)
        grad_pre[r, :] = gpre
        scaled[r, :] = (dg(gpre, w_in[0, 1], 1, 1) * inverse[r, 0:1]).astype(BF16)
    back_near[...] = dg(a_ghost[:, 0:HALO], scaled[...], 0, 0).astype(BF16)
    back_far[...] = dg(a_ghost[:, HALO : 2 * HALO], scaled[...], 0, 0).astype(BF16)


def end_kernel(
    slabs, norm, core, rows, grad_own, near, far, direct, latents, w_msg,
    gradient, keep, give,
    gup_all, tall,
):
    n = direct.shape[0]
    total = grad_own[...] + dg(picks(rows, 1 - core[0], n), near[...], 1, 0)
    total = total + dg(picks(rows, core[0], n), far[...], 1, 0)
    gup_all[...] = total.astype(BF16)
    value = dg(latents[...], gup_all[...], 0, 0)
    pack_rows(core[0], tall, (value * norm).astype(BF16), keep, give, 0, slabs)
    gradient[...] = direct[...] + dg(gup_all[...], w_msg[0], 1, 1)


VMEM = pl.BlockSpec(memory_space=pltpu.VMEM)
SMEM = pl.BlockSpec(memory_space=pltpu.SMEM)
HBM = pl.BlockSpec(memory_space=pltpu.HBM)


def call(kernel, where, outs, scratch, gflops, limit=LIMIT):
    def run(*args):
        return pl.pallas_call(
            kernel,
            in_specs=where,
            out_specs=[VMEM] * len(outs),
            out_shape=[jax.ShapeDtypeStruct(s, d) for s, d in outs],
            scratch_shapes=scratch,
            compiler_params=pltpu.CompilerParams(vmem_limit_bytes=limit << 20),
            cost_estimate=pl.CostEstimate(
                flops=int(gflops * 1e9), transcendentals=0, bytes_accessed=int(gflops * 2e6)
            ),
        )(*args)

    return run


def reduce_rows(keep, give, slabs, bits):
    mine = keep
    for step, (here, there) in enumerate(((None, None), *bits)):
        if step:
            half = mine.reshape(2, mine.shape[0] // 2, *mine.shape[1:])
            mine, give = (
                lax.dynamic_index_in_dim(half, i, 0, keepdims=False, allow_negative_indices=False)
                for i in (here, there)
            )
        got = lax.ppermute(give, "slab", [(i, i ^ (1 << step)) for i in range(slabs)])
        mine = mine.astype(F32) + got.astype(F32)
        if step < len(bits):
            mine = mine.astype(BF16)
    return mine[0]


def body(latents, positions, counts, send_rows, tiles, w_msg, w_in, w_out, cotangent):
    n, width = latents.shape
    hidden_width = w_out.shape[1]
    slabs = lax.axis_size("slab")
    norm = 1.0 / math.sqrt(slabs * n)
    rows = send_rows[0]
    me = lax.axis_index("slab").astype(jnp.int32)
    core = (me & 1).reshape(1)
    place = [((me >> b) & 1, 1 - ((me >> b) & 1)) for b in range(1, slabs.bit_length() - 1)]
    ready = [x.reshape(1) for pair in place for x in pair] + [tiles]
    near_pairs = [(i, i ^ 1) for i in range(slabs)]
    far_pairs = [(i, i + 1 if i % 2 else i - 1) for i in range(1, slabs - 1)]

    def trade(near, far):
        far = lax.ppermute(far, "slab", far_pairs)
        near = lax.ppermute(near, "slab", near_pairs)
        return near, far

    row_b, row_f = ((n, width), BF16), ((n, width), F32)
    hid_b = ((n, hidden_width), BF16)
    halo_b = ((HALO, width), BF16)
    w_in_b = pltpu.VMEM((width, hidden_width), BF16)
    w_out_b = pltpu.VMEM((hidden_width, width), BF16)
    row_buf = pltpu.VMEM((n, width), BF16)

    near, far, latents, positions, w_msg0, w_in00 = call(
        functools.partial(send_kernel, len(ready)), [SMEM] * 2 + [VMEM] + [HBM] * 4 + [SMEM] * len(ready),
        [((HALO + GEO, width), BF16)] * 2
        + [row_b, (positions.shape, F32), ((width, width), BF16), ((width, hidden_width), BF16)],
        [pltpu.VMEM((GEO, n), F32), pltpu.SemaphoreType.DMA((4,))], 0.5, WHOLE,
    )(counts, core, rows, latents, positions, w_msg, w_in, *ready)
    near, far = trade(near, far)

    a_own, squares, columns, _, partial, pre_part = call(
        own_kernel, [SMEM] * 2 + [VMEM] * 4,
        [((n, n), BF16), ((n, TILE), F32), ((n, TILE), F32), row_b, row_f, hid_b],
        [pltpu.VMEM((TILE, n), F32), pltpu.VMEM((n // TILE, 8, TILE), F32)], 5,
    )(counts, tiles, latents, positions, w_msg0, w_in00)

    a_ghost, inverse, message0, hidden0, slope0, current1, update1, near, far = call(
        first_kernel, [SMEM] * 3 + [VMEM] * 12,
        [((n, 2 * HALO), BF16), ((n, TILE), F32), row_b, hid_b, hid_b, row_b, row_b, halo_b, halo_b],
        [pltpu.VMEM((2 * GHOST_TILES, 8, TILE), F32), pltpu.VMEM((n, TILE), F32)], 5,
    )(counts, core, tiles, rows, latents, near, far, squares, columns, partial, pre_part,
      w_msg0, w_in, w_out, w_msg)
    near, far = trade(near, far)

    partial, pre_part, grad_delta1, grad_hidden = call(
        middle_kernel, [SMEM] + [VMEM] * 6, [row_f, hid_b, row_b, hid_b], [], 3,
    )(counts, current1, update1, a_own, cotangent, w_in, w_out)

    message1, hidden1, grad_pre1, scaled1, near, far = call(
        last_kernel, [VMEM] * 8, [row_b, hid_b, hid_b, row_b, halo_b, halo_b], [], 4,
    )(near, far, a_ghost, inverse, partial, pre_part, grad_hidden, w_in)
    near, far = trade(near, far)

    out_rows, msg_rows = hidden_width // slabs, width // slabs
    in_rows = 2 * msg_rows * (hidden_width // width)

    def half(r):
        return [((slabs // 2, r, width), BF16)] * 2

    def terms(plan, heights, args):
        return call(
            functools.partial(terms_kernel, plan, slabs, norm), [SMEM] + [VMEM] * len(args),
            [o for h in heights for o in half(h)], [w_in_b, w_out_b], 4,
        )(core, *args)

    out1 = terms((((0, 1),),), (out_rows,), (hidden1, grad_delta1))
    in1 = terms((((0, 2), (1, 2)),), (in_rows,), (current1, message1, grad_pre1))
    grad_own, direct, final = call(
        flow1_kernel, [SMEM] + [VMEM] * 8, [row_f, row_f, row_b], [], 4,
    )(counts, current1, hidden1, grad_pre1, scaled1, a_own, cotangent, w_in, w_out)
    share_out1 = reduce_rows(*out1, slabs, place)
    share_in1 = reduce_rows(*in1, slabs, place)

    grad_update1, gradient1, grad_delta0, grad_pre0, scaled0, near, far = call(
        turn_kernel, [SMEM] * 2 + [VMEM] * 11,
        [row_b, row_f, row_b, hid_b, row_b, halo_b, halo_b], [], 4,
    )(counts, core, rows, grad_own, near, far, direct, slope0, inverse, a_ghost, w_msg, w_in, w_out)
    near, far = trade(near, far)

    out0 = terms((((2, 4), (3, 4)), ((5, 6), (0, 1))), (in_rows, msg_rows + out_rows),
                 (hidden0, grad_delta0, latents, message0, grad_pre0, current1, grad_update1))
    grad_own, direct = call(
        flow0_kernel, [VMEM] * 5, [row_f, row_f], [], 3,
    )(gradient1, grad_pre0, scaled0, a_own, w_in)
    share_in0 = reduce_rows(out0[0], out0[1], slabs, place)
    share_mix = reduce_rows(out0[2], out0[3], slabs, place)

    gradient, keep, give = call(
        functools.partial(end_kernel, slabs, norm), [SMEM] + [VMEM] * 7,
        [row_f] + half(msg_rows), [row_buf, w_out_b], 2,
    )(core, rows, grad_own, near, far, direct, latents, w_msg)
    share_msg0 = reduce_rows(keep, give, slabs, place)

    def unpack_in(share):
        parts = share.reshape(2, hidden_width // width, msg_rows, width)
        return jnp.concatenate([parts[:, h] for h in range(hidden_width // width)], axis=-1)

    grad_msg = jnp.stack([share_msg0, share_mix[:msg_rows]])
    grad_out = jnp.stack([share_mix[msg_rows:], share_out1])
    grad_in = jnp.stack([unpack_in(share_in0), unpack_in(share_in1)])
    return (final, gradient, grad_msg, grad_in, grad_out)


def solution(mesh):
    placed = (
        P(("groups", "slab"), None),
        P(None, ("groups", "slab")),
        P(("groups", "slab")),
        P(("groups", "slab"), None, None),
        P(("groups", "slab"), None, None),
        P(),
        P(),
        P(),
        P(("groups", "slab"), None),
    )
    return jax.shard_map(
        body,
        mesh=mesh,
        in_specs=placed,
        out_specs=(
            P(("groups", "slab"), None),
            P(("groups", "slab"), None),
            P("groups", "slab", None),
            P("groups", None, "slab", None),
            P("groups", "slab", None),
        ),
        check_vma=False,
    )
```

time: 179 us -> 157 us (0.88)
  local copies, waits for them, and re-layouts: 31.3 us -> 2.58 us
  waiting for transfers between devices: 43.1 us -> 56 us
  other arithmetic: 8 us -> 4.22 us
  starting transfers between devices: 44.9 us -> 42.1 us
    unnamed x85 -> x15, local copies, waits for them, and re-layouts: 31 us -> 2.19 us
    ppermute x23 -> x28, waiting for transfers between devices: 43.1 us -> 56 us  [the longest x20 55.9 us: reduce_rows(): got = lax.ppermute(give, 'slab', [(i, i ^ 1 << step) for i in range(slabs)])]
    convert_element_type x6 -> x15, other arithmetic: 5.51 us -> 1.85 us  [reduce_rows(): mine = mine.astype(BF16)]
    ppermute x23 -> x28, starting transfers between devices: 44.9 us -> 42.1 us  [the longest x20 28.4 us: reduce_rows(): got = lax.ppermute(give, 'slab', [(i, i ^ 1 << step) for i in range(slabs)])]
    pallas_call x9 -> x12, Pallas kernels: 49.1 us -> 49.7 us  [run(): pl.pallas_call(kernel, in_specs=where, out_specs=[VMEM] * len(outs), out_...]
  transfers between devices with their start and end apart: 23 -> 28, of which waited for: 8 -> 12; matrix products, arithmetic and copies ran while one was open for 4% -> 2% of each run, Pallas kernels for 18% -> 21%
where the time goes in v1:
time: 157 us; the launch traced here: 156 us
  waiting for transfers between devices  56 us (36%)
  Pallas kernels  49.7 us (32%)
  starting transfers between devices  42.1 us (27%)
  other arithmetic  4.22 us (3%)
  local copies, waits for them, and re-layouts  2.58 us (2%)
  between operations  1.79 us (1%)
    ppermute x20, waiting for transfers between devices, reduce_rows(): got = lax.ppermute(give, 'slab', [(i, i ^ 1 << step) for i in range(slabs)])  55.9 us
    pallas_call x12, Pallas kernels, run(): pl.pallas_call(kernel, in_specs=where, out_specs=[VMEM] * len(outs), out_...  49.7 us
    ppermute x20, starting transfers between devices, reduce_rows(): got = lax.ppermute(give, 'slab', [(i, i ^ 1 << step) for i in range(slabs)])  28.4 us
    ppermute x4, starting transfers between devices, trade(): near = lax.ppermute(near, 'slab', near_pairs)  10.4 us
    ppermute x4, starting transfers between devices, trade(): far = lax.ppermute(far, 'slab', far_pairs)  3.32 us
  transfers between devices with their start and end apart: 28, of which 12 were waited for; matrix products, arithmetic and copies ran while one was open for 2% of the time, Pallas kernels for 21%

profile of v1, /device:TPU:0, one launch (start us, length us, event | category | flops | bytes accessed | tf_op | source)
XLA Modules:
  0.0 156.4 jit_solution(17432969405454539955)
XLA Ops:
  3.4 2.8 %shard_map.128 = (bf16[272,512]{1,0:T(8,128)(2,1)S(1)}, bf16[272,512]{1,0:T(8,128)(2,1)S(1)}, bf16[1024,512]{1,0:T(8,128)(2,1)S(1)}, f32[3,1024]{1,0:T(4,128)S(1...) custom-call(s32[1]{0:T(128)S(6)} %copy.26.count, s32[1]{0:T(128)} %bitcast.core, s32[2,256]{1,0:T(2,128)S(1)} %bitcast.88, ...), custom_call_target="tpu_custom_call" | custom-call | flops 500000000 | bytes 1000000 | tf_op jit(solution)/shard_map/pallas_call | solution.py:290
  7.6 7.4 %shard_map.129 = (bf16[1024,1024]{1,0:T(8,128)(2,1)S(1)}, f32[1024,128]{1,0:T(8,128)S(1)}, f32[1024,128]{1,0:T(8,128)S(1)}, bf16[1024,512]{1,0:T(8,128)(2,1)}, f...) custom-call(s32[1]{0:T(128)S(6)} %copy.26.count, s32[1,8,4]{2,1,0:T(8,128)S(1)} %copy.19.refs_6_.tiles, ...), custom_call_target="tpu_custom_call" | custom-call | flops 5000000000 | bytes 10000000 | tf_op jit(solution)/shard_map/pallas_call | solution.py:290
  15.0 8.0 %shard_map.130 = (bf16[1024,512]{1,0:T(8,128)(2,1)S(1)}, f32[1024,128]{1,0:T(8,128)S(1)}, bf16[1024,512]{1,0:T(8,128)(2,1)S(1)}, bf16[1024,1024]{1,0:T(8,128)(2,...) custom-call(s32[1]{0:T(128)S(6)} %copy.26.count, ...), custom_call_target="tpu_custom_call" | custom-call | flops 5000000000 | bytes 10000000 | tf_op jit(solution)/shard_map/pallas_call | solution.py:290
  23.1 3.9 %collective-permute-start.2 = (bf16[256,512]{1,0:T(8,128)(2,1)S(1)}, bf16[256,512]{1,0:T(8,128)(2,1)S(1)}, u32[]{:S(2)}, u32[]{:S(2)}) collective-permute-start(bf16[256,512]{1,0:T(8,128)(2,1)S(1)} %get-tuple-element.69), channel_id=1, source_target_pairs={{0,1},{1,0},{2,3},{3,2},{4,5},{5,4},{6,7},{7,6},{8,9},{9,8},{10,11... | collective-permute-start | bytes 786440 | tf_op jit(solution)/shard_map/ppermute | solution.py:336
  27.9 3.4 %shard_map.131 = (f32[1024,512]{1,0:T(8,128)S(1)}, bf16[1024,1024]{1,0:T(8,128)(2,1)S(1)}, bf16[1024,512]{1,0:T(8,128)(2,1)S(1)}, bf16[1024,1024]{1,0:T(8,128)(2,1)S(1)}) custom-call(s32[1]{0:T(128)S(6)} %copy.26.count, bf16[1024,512]{1,0:T(8,128)(2,1)S(1)} %get-tuple-element.68.current.before.refs_5_.refs_0_, ...), custom_call_target="tpu_custom_call" | custom-call | flops 3000000000 | bytes 6000000 | tf_op jit(solution)/shard_map/pallas_call | solution.py:290
  31.3 5.3 %shard_map.132 = (bf16[1024,512]{1,0:T(8,128)(2,1)S(1)}, bf16[1024,1024]{1,0:T(8,128)(2,1)S(1)}, bf16[1024,1024]{1,0:T(8,128)(2,1)S(1)}, bf16[1024,512]{1,0:T(8,...) custom-call(bf16[256,512]{1,0:T(8,128)(2,1)S(1)} %collective-permute-done.2.near, ...), custom_call_target="tpu_custom_call" | custom-call | flops 4000000000 | bytes 8000000 | tf_op jit(solution)/shard_map/pallas_call | solution.py:290
  36.6 5.4 %collective-permute-start.4 = (bf16[256,512]{1,0:T(8,128)(2,1)S(1)}, bf16[256,512]{1,0:T(8,128)(2,1)S(1)}, u32[]{:S(2)}, u32[]{:S(2)}) collective-permute-start(bf16[256,512]{1,0:T(8,128)(2,1)S(1)} %get-tuple-element.83), channel_id=1, source_target_pairs={{0,1},{1,0},{2,3},{3,2},{4,5},{5,4},{6,7},{7,6},{8,9},{9,8},{10,11... | collective-permute-start | bytes 786440 | tf_op jit(solution)/shard_map/ppermute | solution.py:336
  44.2 3.8 %collective-permute-start.24 = (bf16[8,64,512]{2,1,0:T(8,128)(2,1)S(1)}, bf16[8,64,512]{2,1,0:T(8,128)(2,1)S(1)}, u32[]{:S(2)}, u32[]{:S(2)}) collective-permute-start(bf16[8,64,512]{2,1,0:T(8,128)(2,1)S(1)} %get-tuple-element.110), channel_id=1, source_target_pairs={{0,1},{1,0},{2,3},{3,2},{4,5},{5,4},{6,7},{7,6},{8,9},{9,8},{10,11... | collective-permute-start | bytes 1572872 | tf_op jit(solution)/shard_map/ppermute | solution.py:314
  48.0 2.5 %shard_map.138 = (bf16[8,128,512]{2,1,0:T(8,128)(2,1)S(1)}, bf16[8,128,512]{2,1,0:T(8,128)(2,1)S(1)}) custom-call(s32[1]{0:T(128)} %bitcast.core, bf16[1024,512]{1,0:T(8,128)(2,1)S(1)} %get-tuple-element.68.current.before.refs_5_.refs_0_, bf16[1024,512]{1,0:T(8,128)(2,1)S(1)} %get-tuple-element.105.refs_1_, ...), custom_call_target="tpu_custom_call" | custom-call | flops 4000000000 | bytes 8000000 | tf_op jit(solution)/shard_map/pallas_call | solution.py:290
  50.6 4.5 %shard_map.133 = (f32[1024,512]{1,0:T(8,128)S(1)}, f32[1024,512]{1,0:T(8,128)S(1)}, bf16[1024,512]{1,0:T(8,128)(2,1)}) custom-call(s32[1]{0:T(128)S(6)} %copy.26.count, bf16[1024,512]{1,0:T(8,128)(2,1)S(1)} %get-tuple-element.68.current.before.refs_5_.refs_0_, bf16[1024,1024]{1,0:T(8,128)(2,1)S(1)} %get-tuple-element.78.hidden.refs_0_, ...), custom_call_target="tpu_custom_call" | custom-call | flops 4000000000 | bytes 8000000 | tf_op jit(solution)/shard_map/pallas_call | solution.py:290
  55.1 4.7 %shard_map.134 = (bf16[1024,512]{1,0:T(8,128)(2,1)S(1)}, f32[1024,512]{1,0:T(8,128)S(1)}, bf16[1024,512]{1,0:T(8,128)(2,1)S(1)}, bf16[1024,1024]{1,0:T(8,128)(2,...) custom-call(s32[1]{0:T(128)S(6)} %copy.26.count, s32[1]{0:T(128)} %bitcast.core, ...), custom_call_target="tpu_custom_call" | custom-call | flops 4000000000 | bytes 8000000 | tf_op jit(solution)/shard_map/pallas_call | solution.py:290
  61.4 4.2 %shard_map.137 = (bf16[8,128,512]{2,1,0:T(8,128)(2,1)S(1)}, bf16[8,128,512]{2,1,0:T(8,128)(2,1)S(1)}, bf16[8,96,512]{2,1,0:T(8,128)(2,1)S(1)}, bf16[8,96,512]{2,1,0:T(8,128)(2,1)S(1)}) custom-call(s32[1]{0:T(128)} %bitcast.core, bf16[1024,1024]{1,0:T(8,128)(2,1)S(1)} %get-tuple-element.97.refs_0_, bf16[1024,512]{1,0:T(8,128)(2,1)S(1)} %get-tuple-element.98.refs_1_, ...), custom_call_target="tpu_custom_call" | custom-call | flops 4000000000 | bytes 8000000 | tf_op jit(solution)/shard_map/pallas_call | solution.py:290
  65.6 3.3 %collective-permute-start.12 = (bf16[8,96,512]{2,1,0:T(8,128)(2,1)S(1)}, bf16[8,96,512]{2,1,0:T(8,128)(2,1)S(1)}, u32[]{:S(2)}, u32[]{:S(2)}) collective-permute-start(bf16[8,96,512]{2,1,0:T(8,128)(2,1)S(1)} %get-tuple-element.102), channel_id=1, source_target_pairs={{0,1},{1,0},{2,3},{3,2},{4,5},{5,4},{6,7},{7,6},{8,9},{9,8},{10,11... | collective-permute-start | bytes 2359304 | tf_op jit(solution)/shard_map/ppermute | solution.py:314
  68.8 2.4 %shard_map.135 = (f32[1024,512]{1,0:T(8,128)S(1)}, f32[1024,512]{1,0:T(8,128)S(1)}) custom-call(f32[1024,512]{1,0:T(8,128)S(1)} %get-tuple-element.87.gradient, bf16[1024,1024]{1,0:T(8,128)(2,1)S(1)} %get-tuple-element.88.grad_pre.refs_4_, bf16[1024,512]{1,0:T(8,128)(2,1)S(1)} %get-tuple-element.89.scaled, bf16[1024,1024]{1,0:T(8,128)(2,1)S(1)} %get-tuple-element.74.a_own, ...), custom_call_target="tpu_custom_call" | custom-call | flops 3000000000 | bytes 6000000 | tf_op jit(solution)/shard_map/pallas_call | solution.py:290
  71.3 3.1 %shard_map.136 = (f32[1024,512]{1,0:T(8,128)}, bf16[8,32,512]{2,1,0:T(8,128)(2,1)S(1)}, bf16[8,32,512]{2,1,0:T(8,128)(2,1)S(1)}) custom-call(s32[1]{0:T(128)} %bitcast.core, s32[2,256]{1,0:T(2,128)S(1)} %bitcast.91, f32[1024,512]{1,0:T(8,128)S(1)} %get-tuple-element.90.grad_own, bf16[256,512]{1,0:T(8,128)(2,1)S(1)} %collective-permute-done.6.near, ...), custom_call_target="tpu_custom_call" | custom-call | flops 2000000000 | bytes 4000000 | tf_op jit(solution)/shard_map/pallas_call | solution.py:290
  77.6 6.8 %collective-permute-done.25 = bf16[4,64,512]{2,1,0:T(8,128)(2,1)S(1)} collective-permute-done((bf16[4,64,512]{2,1,0:T(8,128)(2,1)S(1)}, bf16[4,64,512]{2,1,0:T(8,128)(2,1)S(1)}, u32[]{:S(2)}, u32[]{:S(2)}) %collective-permute-start.25) | collective-permute-done | bytes 262176 | tf_op jit(solution)/shard_map/ppermute | solution.py:314
  84.5 1.6 %collective-permute-start.26 = (bf16[2,64,512]{2,1,0:T(8,128)(2,1)S(1)}, bf16[2,64,512]{2,1,0:T(8,128)(2,1)S(1)}, u32[]{:S(2)}, u32[]{:S(2)}) collective-permute-start(bf16[2,64,512]{2,1,0:T(8,128)(2,1)S(1)} %dynamic-slice_bitcast_fusion.7), channel_id=1, source_target_pairs={{0,4},{1,5},{2,6},{3,7},{4,0},{5,1},{6,2},{7,3},{8,12},{9,13},{10,... | collective-permute-start | bytes 393224 | tf_op jit(solution)/shard_map/ppermute | solution.py:314
  86.3 1.6 %collective-permute-start.10 = (bf16[2,32,512]{2,1,0:T(8,128)(2,1)S(1)}, bf16[2,32,512]{2,1,0:T(8,128)(2,1)S(1)}, u32[]{:S(2)}, u32[]{:S(2)}) collective-permute-start(bf16[2,32,512]{2,1,0:T(8,128)(2,1)S(1)} %dynamic-slice_bitcast_fusion.9), channel_id=1, source_target_pairs={{0,4},{1,5},{2,6},{3,7},{4,0},{5,1},{6,2},{7,3},{8,12},{9,13},{10,... | collective-permute-start | bytes 196616 | tf_op jit(solution)/shard_map/ppermute | solution.py:314
  87.9 2.3 %collective-permute-done.26 = bf16[2,64,512]{2,1,0:T(8,128)(2,1)S(1)} collective-permute-done((bf16[2,64,512]{2,1,0:T(8,128)(2,1)S(1)}, bf16[2,64,512]{2,1,0:T(8,128)(2,1)S(1)}, u32[]{:S(2)}, u32[]{:S(2)}) %collective-permute-start.26) | collective-permute-done | bytes 131104 | tf_op jit(solution)/shard_map/ppermute | solution.py:314
  90.2 3.2 %collective-permute-start.27 = (bf16[1,64,512]{2,1,0:T(8,128)(2,1)S(1)}, bf16[1,64,512]{2,1,0:T(8,128)(2,1)S(1)}, u32[]{:S(2)}, u32[]{:S(2)}) collective-permute-start(bf16[1,64,512]{2,1,0:T(8,128)(2,1)S(1)} %constant_dynamic-slice_fusion), channel_id=1, source_target_pairs={{0,8},{1,9},{2,10},{3,11},{4,12},{5,13},{6,14},{7,15},{8,0},{9,1},... | collective-permute-start | bytes 196616 | tf_op jit(solution)/shard_map/ppermute | solution.py:314
  95.7 2.8 %collective-permute-done.11 = bf16[1,32,512]{2,1,0:T(8,128)(2,1)S(1)} collective-permute-done((bf16[1,32,512]{2,1,0:T(8,128)(2,1)S(1)}, bf16[1,32,512]{2,1,0:T(8,128)(2,1)S(1)}, u32[]{:S(2)}, u32[]{:S(2)}) %collective-permute-start.11) | collective-permute-done | bytes 32800 | tf_op jit(solution)/shard_map/ppermute | solution.py:314
  99.8 1.7 %collective-permute-start.13 = (bf16[4,96,512]{2,1,0:T(8,128)(2,1)S(1)}, bf16[4,96,512]{2,1,0:T(8,128)(2,1)S(1)}, u32[]{:S(2)}, u32[]{:S(2)}) collective-permute-start(bf16[4,96,512]{2,1,0:T(8,128)(2,1)S(1)} %dynamic-slice_bitcast_fusion.2), channel_id=1, source_target_pairs={{0,2},{1,3},{2,0},{3,1},{4,6},{5,7},{6,4},{7,5},{8,10},{9,11},{10,... | collective-permute-start | bytes 1179656 | tf_op jit(solution)/shard_map/ppermute | solution.py:314
  102.3 19.5 %collective-permute-done.13 = bf16[4,96,512]{2,1,0:T(8,128)(2,1)S(1)} collective-permute-done((bf16[4,96,512]{2,1,0:T(8,128)(2,1)S(1)}, bf16[4,96,512]{2,1,0:T(8,128)(2,1)S(1)}, u32[]{:S(2)}, u32[]{:S(2)}) %collective-permute-start.13) | collective-permute-done | bytes 393248 | tf_op jit(solution)/shard_map/ppermute | solution.py:314
  122.9 4.8 %collective-permute-done.14 = bf16[2,96,512]{2,1,0:T(8,128)(2,1)S(1)} collective-permute-done((bf16[2,96,512]{2,1,0:T(8,128)(2,1)S(1)}, bf16[2,96,512]{2,1,0:T(8,128)(2,1)S(1)}, u32[]{:S(2)}, u32[]{:S(2)}) %collective-permute-start.14) | collective-permute-done | bytes 196640 | tf_op jit(solution)/shard_map/ppermute | solution.py:314
  129.1 1.9 %collective-permute-start.22 = (bf16[2,128,512]{2,1,0:T(8,128)(2,1)S(1)}, bf16[2,128,512]{2,1,0:T(8,128)(2,1)S(1)}, u32[]{:S(2)}, u32[]{:S(2)}) collective-permute-start(bf16[2,128,512]{2,1,0:T(8,128)(2,1)S(1)} %dynamic-slice_bitcast_fusion.4), channel_id=1, source_target_pairs={{0,4},{1,5},{2,6},{3,7},{4,0},{5,1},{6,2},{7,3},{8,12},{9,13},{10,... | collective-permute-start | bytes 786440 | tf_op jit(solution)/shard_map/ppermute | solution.py:314
  131.0 3.5 %collective-permute-done.15 = bf16[1,96,512]{2,1,0:T(8,128)(2,1)S(1)} collective-permute-done((bf16[1,96,512]{2,1,0:T(8,128)(2,1)S(1)}, bf16[1,96,512]{2,1,0:T(8,128)(2,1)S(1)}, u32[]{:S(2)}, u32[]{:S(2)}) %collective-permute-start.15) | collective-permute-done | bytes 98336 | tf_op jit(solution)/shard_map/ppermute | solution.py:314
  135.3 2.4 %collective-permute-done.22 = bf16[2,128,512]{2,1,0:T(8,128)(2,1)S(1)} collective-permute-done((bf16[2,128,512]{2,1,0:T(8,128)(2,1)S(1)}, bf16[2,128,512]{2,1,0:T(8,128)(2,1)S(1)}, u32[]{:S(2)}, u32[]{:S(2)}) %collective-permute-start.22) | collective-permute-done | bytes 262176 | tf_op jit(solution)/shard_map/ppermute | solution.py:314
  137.8 2.5 %collective-permute-start.23 = (bf16[1,128,512]{2,1,0:T(8,128)(2,1)S(1)}, bf16[1,128,512]{2,1,0:T(8,128)(2,1)S(1)}, u32[]{:S(2)}, u32[]{:S(2)}) collective-permute-start(bf16[1,128,512]{2,1,0:T(8,128)(2,1)S(1)} %constant_dynamic-slice_fusion.1), channel_id=1, source_target_pairs={{0,8},{1,9},{2,10},{3,11},{4,12},{5,13},{6,14},{7,15},{8,0},{9,1},... | collective-permute-start | bytes 393224 | tf_op jit(solution)/shard_map/ppermute | solution.py:314
  140.5 1.6 %collective-permute-start.18 = (bf16[2,128,512]{2,1,0:T(8,128)(2,1)S(1)}, bf16[2,128,512]{2,1,0:T(8,128)(2,1)S(1)}, u32[]{:S(2)}, u32[]{:S(2)}) collective-permute-start(bf16[2,128,512]{2,1,0:T(8,128)(2,1)S(1)} %dynamic-slice_bitcast_fusion.5), channel_id=1, source_target_pairs={{0,4},{1,5},{2,6},{3,7},{4,0},{5,1},{6,2},{7,3},{8,12},{9,13},{10,... | collective-permute-start | bytes 786440 | tf_op jit(solution)/shard_map/ppermute | solution.py:314
  142.9 3.1 %collective-permute-done.23 = bf16[1,128,512]{2,1,0:T(8,128)(2,1)S(1)} collective-permute-done((bf16[1,128,512]{2,1,0:T(8,128)(2,1)S(1)}, bf16[1,128,512]{2,1,0:T(8,128)(2,1)S(1)}, u32[]{:S(2)}, u32[]{:S(2)}) %collective-permute-start.23) | collective-permute-done | bytes 131104 | tf_op jit(solution)/shard_map/ppermute | solution.py:314
  146.0 2.3 %collective-permute-done.18 = bf16[2,128,512]{2,1,0:T(8,128)(2,1)S(1)} collective-permute-done((bf16[2,128,512]{2,1,0:T(8,128)(2,1)S(1)}, bf16[2,128,512]{2,1,0:T(8,128)(2,1)S(1)}, u32[]{:S(2)}, u32[]{:S(2)}) %collective-permute-start.18) | collective-permute-done | bytes 262176 | tf_op jit(solution)/shard_map/ppermute | solution.py:314
  148.6 6.8 %collective-permute-done.19 = bf16[1,128,512]{2,1,0:T(8,128)(2,1)S(1)} collective-permute-done((bf16[1,128,512]{2,1,0:T(8,128)(2,1)S(1)}, bf16[1,128,512]{2,1,0:T(8,128)(2,1)S(1)}, u32[]{:S(2)}, u32[]{:S(2)}) %collective-permute-start.19) | collective-permute-done | bytes 131104 | tf_op jit(solution)/shard_map/ppermute | solution.py:314
  (94 shorter events, 21.2 us)
Async XLA Ops:
  6.3 8.7 %collective-permute-start = (bf16[272,512]{1,0:T(8,128)(2,1)S(1)}, bf16[272,512]{1,0:T(8,128)(2,1)S(1)}, u32[]{:S(2)}, u32[]{:S(2)}) collective-permute-start(bf16[272,512]{1,0:T(8,128)(2,1)S(1)} %get-tuple-element.59), channel_id=1, source_target_pairs={{0,1},{1,0},{2,3},{3,2},{4,5},{5,4},{6,7},{7,6},{8,9},{9,8},{10,11... | collective-permute-start | bytes 835592 | tf_op jit(solution)/shard_map/ppermute | solution.py:336
  6.9 8.1 %collective-permute-start.1 = (bf16[272,512]{1,0:T(8,128)(2,1)S(1)}, bf16[272,512]{1,0:T(8,128)(2,1)S(1)}, u32[]{:S(2)}, u32[]{:S(2)}) collective-permute-start(bf16[272,512]{1,0:T(8,128)(2,1)S(1)} %get-tuple-element.60), channel_id=1, source_target_pairs={{1,2},{2,1},{3,4},{4,3},{5,6},{6,5},{7,8},{8,7},{9,10},{10,9},{11,... | collective-permute-start | bytes 835592 | tf_op jit(solution)/shard_map/ppermute | solution.py:335
  7.5 7.4 %copy-start = (bf16[2,2,512,1024]{3,2,1,0:T(8,128)(2,1)S(1)}, bf16[2,2,512,1024]{3,2,1,0:T(8,128)(2,1)}, u32[]{:S(2)}) copy-start(bf16[2,2,512,1024]{3,2,1,0:T(8,128)(2,1)} %w_in.13) | copy-start | bytes 12582916
  7.5 7.4 %copy-start.1 = (bf16[2,1024,512]{2,1,0:T(8,128)(2,1)S(1)}, bf16[2,1024,512]{2,1,0:T(8,128)(2,1)}, u32[]{:S(2)}) copy-start(bf16[2,1024,512]{2,1,0:T(8,128)(2,1)} %w_out.7) | copy-start | bytes 6291460
  7.6 7.4 %copy-start.3 = (bf16[2,512,512]{2,1,0:T(8,128)(2,1)S(1)}, bf16[2,512,512]{2,1,0:T(8,128)(2,1)}, u32[]{:S(2)}) copy-start(bf16[2,512,512]{2,1,0:T(8,128)(2,1)} %w_msg.7) | copy-start | bytes 3145732
  15.0 12.8 %copy-start.2 = (bf16[1024,512]{1,0:T(8,128)(2,1)S(1)}, bf16[1024,512]{1,0:T(8,128)(2,1)}, u32[]{:S(2)}) copy-start(bf16[1024,512]{1,0:T(8,128)(2,1)} %cot.3) | copy-start | bytes 3145732
  23.1 8.2 %collective-permute-start.2 = (bf16[256,512]{1,0:T(8,128)(2,1)S(1)}, bf16[256,512]{1,0:T(8,128)(2,1)S(1)}, u32[]{:S(2)}, u32[]{:S(2)}) collective-permute-start(bf16[256,512]{1,0:T(8,128)(2,1)S(1)} %get-tuple-element.69), channel_id=1, source_target_pairs={{0,1},{1,0},{2,3},{3,2},{4,5},{5,4},{6,7},{7,6},{8,9},{9,8},{10,11... | collective-permute-start | bytes 786440 | tf_op jit(solution)/shard_map/ppermute | solution.py:336
  27.0 4.3 %collective-permute-start.3 = (bf16[256,512]{1,0:T(8,128)(2,1)S(1)}, bf16[256,512]{1,0:T(8,128)(2,1)S(1)}, u32[]{:S(2)}, u32[]{:S(2)}) collective-permute-start(bf16[256,512]{1,0:T(8,128)(2,1)S(1)} %get-tuple-element.70), channel_id=1, source_target_pairs={{1,2},{2,1},{3,4},{4,3},{5,6},{6,5},{7,8},{8,7},{9,10},{10,9},{11,... | collective-permute-start | bytes 786440 | tf_op jit(solution)/shard_map/ppermute | solution.py:335
  36.6 18.6 %collective-permute-start.4 = (bf16[256,512]{1,0:T(8,128)(2,1)S(1)}, bf16[256,512]{1,0:T(8,128)(2,1)S(1)}, u32[]{:S(2)}, u32[]{:S(2)}) collective-permute-start(bf16[256,512]{1,0:T(8,128)(2,1)S(1)} %get-tuple-element.83), channel_id=1, source_target_pairs={{0,1},{1,0},{2,3},{3,2},{4,5},{5,4},{6,7},{7,6},{8,9},{9,8},{10,11... | collective-permute-start | bytes 786440 | tf_op jit(solution)/shard_map/ppermute | solution.py:336
  42.0 13.2 %collective-permute-start.5 = (bf16[256,512]{1,0:T(8,128)(2,1)S(1)}, bf16[256,512]{1,0:T(8,128)(2,1)S(1)}, u32[]{:S(2)}, u32[]{:S(2)}) collective-permute-start(bf16[256,512]{1,0:T(8,128)(2,1)S(1)} %get-tuple-element.84), channel_id=1, source_target_pairs={{1,2},{2,1},{3,4},{4,3},{5,6},{6,5},{7,8},{8,7},{9,10},{10,9},{11,... | collective-permute-start | bytes 786440 | tf_op jit(solution)/shard_map/ppermute | solution.py:335
  44.2 30.7 %collective-permute-start.24 = (bf16[8,64,512]{2,1,0:T(8,128)(2,1)S(1)}, bf16[8,64,512]{2,1,0:T(8,128)(2,1)S(1)}, u32[]{:S(2)}, u32[]{:S(2)}) collective-permute-start(bf16[8,64,512]{2,1,0:T(8,128)(2,1)S(1)} %get-tuple-element.110), channel_id=1, source_target_pairs={{0,1},{1,0},{2,3},{3,2},{4,5},{5,4},{6,7},{7,6},{8,9},{9,8},{10,11... | collective-permute-start | bytes 1572872 | tf_op jit(solution)/shard_map/ppermute | solution.py:314
  50.6 48.0 %collective-permute-start.20 = (bf16[8,128,512]{2,1,0:T(8,128)(2,1)S(1)}, bf16[8,128,512]{2,1,0:T(8,128)(2,1)S(1)}, u32[]{:S(2)}, u32[]{:S(2)}) collective-permute-start(bf16[8,128,512]{2,1,0:T(8,128)(2,1)S(1)} %get-tuple-element.107), channel_id=1, source_target_pairs={{0,1},{1,0},{2,3},{3,2},{4,5},{5,4},{6,7},{7,6},{8,9},{9,8},{10,11... | collective-permute-start | bytes 3145736 | tf_op jit(solution)/shard_map/ppermute | solution.py:314
  59.9 11.3 %collective-permute-start.6 = (bf16[256,512]{1,0:T(8,128)(2,1)S(1)}, bf16[256,512]{1,0:T(8,128)(2,1)S(1)}, u32[]{:S(2)}, u32[]{:S(2)}) collective-permute-start(bf16[256,512]{1,0:T(8,128)(2,1)S(1)} %get-tuple-element.91), channel_id=1, source_target_pairs={{0,1},{1,0},{2,3},{3,2},{4,5},{5,4},{6,7},{7,6},{8,9},{9,8},{10,11... | collective-permute-start | bytes 786440 | tf_op jit(solution)/shard_map/ppermute | solution.py:336
  60.4 10.9 %collective-permute-start.7 = (bf16[256,512]{1,0:T(8,128)(2,1)S(1)}, bf16[256,512]{1,0:T(8,128)(2,1)S(1)}, u32[]{:S(2)}, u32[]{:S(2)}) collective-permute-start(bf16[256,512]{1,0:T(8,128)(2,1)S(1)} %get-tuple-element.92), channel_id=1, source_target_pairs={{1,2},{2,1},{3,4},{4,3},{5,6},{6,5},{7,8},{8,7},{9,10},{10,9},{11,... | collective-permute-start | bytes 786440 | tf_op jit(solution)/shard_map/ppermute | solution.py:335
  65.6 33.9 %collective-permute-start.12 = (bf16[8,96,512]{2,1,0:T(8,128)(2,1)S(1)}, bf16[8,96,512]{2,1,0:T(8,128)(2,1)S(1)}, u32[]{:S(2)}, u32[]{:S(2)}) collective-permute-start(bf16[8,96,512]{2,1,0:T(8,128)(2,1)S(1)} %get-tuple-element.102), channel_id=1, source_target_pairs={{0,1},{1,0},{2,3},{3,2},{4,5},{5,4},{6,7},{7,6},{8,9},{9,8},{10,11... | collective-permute-start | bytes 2359304 | tf_op jit(solution)/shard_map/ppermute | solution.py:314
  71.2 30.2 %collective-permute-start.16 = (bf16[8,128,512]{2,1,0:T(8,128)(2,1)S(1)}, bf16[8,128,512]{2,1,0:T(8,128)(2,1)S(1)}, u32[]{:S(2)}, u32[]{:S(2)}) collective-permute-start(bf16[8,128,512]{2,1,0:T(8,128)(2,1)S(1)} %get-tuple-element.104), channel_id=1, source_target_pairs={{0,1},{1,0},{2,3},{3,2},{4,5},{5,4},{6,7},{7,6},{8,9},{9,8},{10,11... | collective-permute-start | bytes 3145736 | tf_op jit(solution)/shard_map/ppermute | solution.py:314
  74.4 1.9 %collective-permute-start.8 = (bf16[8,32,512]{2,1,0:T(8,128)(2,1)S(1)}, bf16[8,32,512]{2,1,0:T(8,128)(2,1)S(1)}, u32[]{:S(2)}, u32[]{:S(2)}) collective-permute-start(bf16[8,32,512]{2,1,0:T(8,128)(2,1)S(1)} %get-tuple-element.96), channel_id=1, source_target_pairs={{0,1},{1,0},{2,3},{3,2},{4,5},{5,4},{6,7},{7,6},{8,9},{9,8},{10,11... | collective-permute-start | bytes 786440 | tf_op jit(solution)/shard_map/ppermute | solution.py:314
  75.1 9.2 %collective-permute-start.25 = (bf16[4,64,512]{2,1,0:T(8,128)(2,1)S(1)}, bf16[4,64,512]{2,1,0:T(8,128)(2,1)S(1)}, u32[]{:S(2)}, u32[]{:S(2)}) collective-permute-start(bf16[4,64,512]{2,1,0:T(8,128)(2,1)S(1)} %dynamic-slice_bitcast_fusion.3), channel_id=1, source_target_pairs={{0,2},{1,3},{2,0},{3,1},{4,6},{5,7},{6,4},{7,5},{8,10},{9,11},{10,... | collective-permute-start | bytes 786440 | tf_op jit(solution)/shard_map/ppermute | solution.py:314
  76.5 9.7 %collective-permute-start.9 = (bf16[4,32,512]{2,1,0:T(8,128)(2,1)S(1)}, bf16[4,32,512]{2,1,0:T(8,128)(2,1)S(1)}, u32[]{:S(2)}, u32[]{:S(2)}) collective-permute-start(bf16[4,32,512]{2,1,0:T(8,128)(2,1)S(1)} %dynamic-slice_bitcast_fusion.8), channel_id=1, source_target_pairs={{0,2},{1,3},{2,0},{3,1},{4,6},{5,7},{6,4},{7,5},{8,10},{9,11},{10,... | collective-permute-start | bytes 393224 | tf_op jit(solution)/shard_map/ppermute | solution.py:314
  84.5 5.7 %collective-permute-start.26 = (bf16[2,64,512]{2,1,0:T(8,128)(2,1)S(1)}, bf16[2,64,512]{2,1,0:T(8,128)(2,1)S(1)}, u32[]{:S(2)}, u32[]{:S(2)}) collective-permute-start(bf16[2,64,512]{2,1,0:T(8,128)(2,1)S(1)} %dynamic-slice_bitcast_fusion.7), channel_id=1, source_target_pairs={{0,4},{1,5},{2,6},{3,7},{4,0},{5,1},{6,2},{7,3},{8,12},{9,13},{10,... | collective-permute-start | bytes 393224 | tf_op jit(solution)/shard_map/ppermute | solution.py:314
  86.3 7.2 %collective-permute-start.10 = (bf16[2,32,512]{2,1,0:T(8,128)(2,1)S(1)}, bf16[2,32,512]{2,1,0:T(8,128)(2,1)S(1)}, u32[]{:S(2)}, u32[]{:S(2)}) collective-permute-start(bf16[2,32,512]{2,1,0:T(8,128)(2,1)S(1)} %dynamic-slice_bitcast_fusion.9), channel_id=1, source_target_pairs={{0,4},{1,5},{2,6},{3,7},{4,0},{5,1},{6,2},{7,3},{8,12},{9,13},{10,... | collective-permute-start | bytes 196616 | tf_op jit(solution)/shard_map/ppermute | solution.py:314
  90.2 5.5 %collective-permute-start.27 = (bf16[1,64,512]{2,1,0:T(8,128)(2,1)S(1)}, bf16[1,64,512]{2,1,0:T(8,128)(2,1)S(1)}, u32[]{:S(2)}, u32[]{:S(2)}) collective-permute-start(bf16[1,64,512]{2,1,0:T(8,128)(2,1)S(1)} %constant_dynamic-slice_fusion), channel_id=1, source_target_pairs={{0,8},{1,9},{2,10},{3,11},{4,12},{5,13},{6,14},{7,15},{8,0},{9,1},... | collective-permute-start | bytes 196616 | tf_op jit(solution)/shard_map/ppermute | solution.py:314
  93.5 5.1 %collective-permute-start.11 = (bf16[1,32,512]{2,1,0:T(8,128)(2,1)S(1)}, bf16[1,32,512]{2,1,0:T(8,128)(2,1)S(1)}, u32[]{:S(2)}, u32[]{:S(2)}) collective-permute-start(bf16[1,32,512]{2,1,0:T(8,128)(2,1)S(1)} %constant_dynamic-slice_fusion.4), channel_id=1, source_target_pairs={{0,8},{1,9},{2,10},{3,11},{4,12},{5,13},{6,14},{7,15},{8,0},{9,1},... | collective-permute-start | bytes 98312 | tf_op jit(solution)/shard_map/ppermute | solution.py:314
  99.0 23.7 %collective-permute-start.21 = (bf16[4,128,512]{2,1,0:T(8,128)(2,1)S(1)}, bf16[4,128,512]{2,1,0:T(8,128)(2,1)S(1)}, u32[]{:S(2)}, u32[]{:S(2)}) collective-permute-start(bf16[4,128,512]{2,1,0:T(8,128)(2,1)S(1)} %dynamic-slice_bitcast_fusion), channel_id=1, source_target_pairs={{0,2},{1,3},{2,0},{3,1},{4,6},{5,7},{6,4},{7,5},{8,10},{9,11},{10,... | collective-permute-start | bytes 1572872 | tf_op jit(solution)/shard_map/ppermute | solution.py:314
  99.8 22.1 %collective-permute-start.13 = (bf16[4,96,512]{2,1,0:T(8,128)(2,1)S(1)}, bf16[4,96,512]{2,1,0:T(8,128)(2,1)S(1)}, u32[]{:S(2)}, u32[]{:S(2)}) collective-permute-start(bf16[4,96,512]{2,1,0:T(8,128)(2,1)S(1)} %dynamic-slice_bitcast_fusion.2), channel_id=1, source_target_pairs={{0,2},{1,3},{2,0},{3,1},{4,6},{5,7},{6,4},{7,5},{8,10},{9,11},{10,... | collective-permute-start | bytes 1179656 | tf_op jit(solution)/shard_map/ppermute | solution.py:314
  101.8 38.6 %collective-permute-start.17 = (bf16[4,128,512]{2,1,0:T(8,128)(2,1)S(1)}, bf16[4,128,512]{2,1,0:T(8,128)(2,1)S(1)}, u32[]{:S(2)}, u32[]{:S(2)}) collective-permute-start(bf16[4,128,512]{2,1,0:T(8,128)(2,1)S(1)} %dynamic-slice_bitcast_fusion.1), channel_id=1, source_target_pairs={{0,2},{1,3},{2,0},{3,1},{4,6},{5,7},{6,4},{7,5},{8,10},{9,11},{10,... | collective-permute-start | bytes 1572872 | tf_op jit(solution)/shard_map/ppermute | solution.py:314
  122.0 5.7 %collective-permute-start.14 = (bf16[2,96,512]{2,1,0:T(8,128)(2,1)S(1)}, bf16[2,96,512]{2,1,0:T(8,128)(2,1)S(1)}, u32[]{:S(2)}, u32[]{:S(2)}) collective-permute-start(bf16[2,96,512]{2,1,0:T(8,128)(2,1)S(1)} %dynamic-slice_bitcast_fusion.6), channel_id=1, source_target_pairs={{0,4},{1,5},{2,6},{3,7},{4,0},{5,1},{6,2},{7,3},{8,12},{9,13},{10,... | collective-permute-start | bytes 589832 | tf_op jit(solution)/shard_map/ppermute | solution.py:314
  127.8 6.8 %collective-permute-start.15 = (bf16[1,96,512]{2,1,0:T(8,128)(2,1)S(1)}, bf16[1,96,512]{2,1,0:T(8,128)(2,1)S(1)}, u32[]{:S(2)}, u32[]{:S(2)}) collective-permute-start(bf16[1,96,512]{2,1,0:T(8,128)(2,1)S(1)} %constant_dynamic-slice_fusion.3), channel_id=1, source_target_pairs={{0,8},{1,9},{2,10},{3,11},{4,12},{5,13},{6,14},{7,15},{8,0},{9,1},... | collective-permute-start | bytes 294920 | tf_op jit(solution)/shard_map/ppermute | solution.py:314
  129.1 8.6 %collective-permute-start.22 = (bf16[2,128,512]{2,1,0:T(8,128)(2,1)S(1)}, bf16[2,128,512]{2,1,0:T(8,128)(2,1)S(1)}, u32[]{:S(2)}, u32[]{:S(2)}) collective-permute-start(bf16[2,128,512]{2,1,0:T(8,128)(2,1)S(1)} %dynamic-slice_bitcast_fusion.4), channel_id=1, source_target_pairs={{0,4},{1,5},{2,6},{3,7},{4,0},{5,1},{6,2},{7,3},{8,12},{9,13},{10,... | collective-permute-start | bytes 786440 | tf_op jit(solution)/shard_map/ppermute | solution.py:314
  137.8 8.2 %collective-permute-start.23 = (bf16[1,128,512]{2,1,0:T(8,128)(2,1)S(1)}, bf16[1,128,512]{2,1,0:T(8,128)(2,1)S(1)}, u32[]{:S(2)}, u32[]{:S(2)}) collective-permute-start(bf16[1,128,512]{2,1,0:T(8,128)(2,1)S(1)} %constant_dynamic-slice_fusion.1), channel_id=1, source_target_pairs={{0,8},{1,9},{2,10},{3,11},{4,12},{5,13},{6,14},{7,15},{8,0},{9,1},... | collective-permute-start | bytes 393224 | tf_op jit(solution)/shard_map/ppermute | solution.py:314
  140.5 7.7 %collective-permute-start.18 = (bf16[2,128,512]{2,1,0:T(8,128)(2,1)S(1)}, bf16[2,128,512]{2,1,0:T(8,128)(2,1)S(1)}, u32[]{:S(2)}, u32[]{:S(2)}) collective-permute-start(bf16[2,128,512]{2,1,0:T(8,128)(2,1)S(1)} %dynamic-slice_bitcast_fusion.5), channel_id=1, source_target_pairs={{0,4},{1,5},{2,6},{3,7},{4,0},{5,1},{6,2},{7,3},{8,12},{9,13},{10,... | collective-permute-start | bytes 786440 | tf_op jit(solution)/shard_map/ppermute | solution.py:314
  148.4 7.0 %collective-permute-start.19 = (bf16[1,128,512]{2,1,0:T(8,128)(2,1)S(1)}, bf16[1,128,512]{2,1,0:T(8,128)(2,1)S(1)}, u32[]{:S(2)}, u32[]{:S(2)}) collective-permute-start(bf16[1,128,512]{2,1,0:T(8,128)(2,1)S(1)} %constant_dynamic-slice_fusion.2), channel_id=1, source_target_pairs={{0,8},{1,9},{2,10},{3,11},{4,12},{5,13},{6,14},{7,15},{8,0},{9,1},... | collective-permute-start | bytes 393224 | tf_op jit(solution)/shard_map/ppermute | solution.py:314
  (3 other events, 8.8 us)

commit v2 on v1

--- a/solution.py
+++ b/solution.py
@@ -38,10 +38,12 @@
     return jnp.where(index == rows[pl.ds(d, 1), :], 1.0, 0.0).astype(BF16)
 
 
-def send_kernel(scalars, count, core, rows, latents_far, positions_far, w_msg, w_in, *refs):
-    near, far, latents, positions, wm, wi, geo, sems = refs[scalars:]
+def send_kernel(scalars, count, core, rows_far, latents_far, positions_far, w_msg, w_in, *refs):
+    near, far, rows, latents, positions, wm, wi, geo, sems = refs[scalars:]
     n = latents.shape[0]
-    moves = ((positions_far, positions), (latents_far, latents), (w_msg.at[0], wm), (w_in.at[0, 0], wi))
+    moves = (
+        (positions_far, positions), (rows_far, rows), (latents_far, latents), (w_msg.at[0], wm), (w_in.at[0, 0], wi)
+    )
     copies = [pltpu.make_async_copy(src, dst, sems.at[i]) for i, (src, dst) in enumerate(moves)]
     for copy in copies:
         copy.start()
@@ -58,13 +60,14 @@
     geo[9:10, :] = jnp.where(lane < count[0], 1.0, 0.0).astype(F32)
     fields = geo[...].astype(BF16)
     copies[1].wait()
+    copies[2].wait()
     for d, out in ((1 - core[0], near), (core[0], far)):
         pick = picks(rows, d, n)
         out[0:HALO, :] = dg(pick, latents[...], 0, 0).astype(BF16)
         out[HALO : HALO + GEO, :] = jnp.zeros((GEO, out.shape[1]), BF16)
         out[HALO : HALO + GEO, 0:HALO] = dg(fields, pick, 1, 0).astype(BF16)
-    copies[2].wait()
     copies[3].wait()
+    copies[4].wait()
 
 
 def pair_weight(x_column, geo):
@@ -95,8 +98,8 @@
 
     def tile_step(t, _):
         rows = pl.ds(pl.multiple_of(t * TILE, TILE), TILE)
-        for k in range(tiles.shape[2]):
-            tile = tiles[0, t, k] - GHOST_TILES
+        for k in range(tiles.shape[1]):
+            tile = tiles[0, k, t] - GHOST_TILES
 
             @pl.when((tile >= 0) & (tile < tile_count))
             def _():
@@ -133,8 +136,8 @@
 
     def tile_step(t, _):
         own = pl.ds(pl.multiple_of(t * TILE, TILE), TILE)
-        for k in range(tiles.shape[2]):
-            index = tiles[0, t, k]
+        for k in range(tiles.shape[1]):
+            index = tiles[0, k, t]
             tile = jnp.where(index < GHOST_TILES, index + below, index + above)
 
             @pl.when((index < GHOST_TILES) | (index >= GHOST_TILES + tile_count))
@@ -202,13 +205,15 @@
     back_far[...] = dg(a_ghost[:, HALO : 2 * HALO], scaled[...], 0, 0).astype(BF16)
 
 
-def pack_rows(core, stage, value, keep, give, at, slabs):
+def pack_rows(core, stage, value, keep, give, at, slabs, order):
     height, columns = value.shape
-    rows, width, bits = height // slabs, keep.shape[-1], slabs.bit_length() - 2
+    rows, width = height // slabs, keep.shape[-1]
     stage[0:height, 0:columns] = value
     for h in range(columns // width):
         for pair in range(slabs // 2):
-            place = sum(((pair >> b) & 1) << (bits - 1 - b) for b in range(bits))
+            place = 0
+            for b in order:
+                place = place * 2 + ((pair * 2 >> b) & 1)
             for out, which in ((keep, core), (give, 1 - core)):
                 source = pl.ds(pl.multiple_of((pair * 2 + which) * rows, rows), rows)
                 out[place, at : at + rows, :] = stage[source, h * width : (h + 1) * width]
@@ -219,28 +224,21 @@
 def terms_kernel(plan, slabs, norm, core, *refs):
     wide, tall = refs[-2:]
     outs = refs[len(refs) - 2 - 2 * len(plan) : -2]
-    for c, chunk in enumerate(plan):
+    for c, (order, chunk) in enumerate(plan):
         at = 0
         for a, b in chunk:
             value = (dg(refs[a][...], refs[b][...], 0, 0) * norm).astype(BF16)
             stage = tall if value.shape[1] == tall.shape[1] else wide
-            at = pack_rows(core[0], stage, value, outs[2 * c], outs[2 * c + 1], at, slabs)
-
-
-def flow1_kernel(
-    count, before, hidden, grad_pre, scaled, a_own, cot, w_in, w_out,
-    grad_own, direct, final,
-):
+            at = pack_rows(core[0], stage, value, outs[2 * c], outs[2 * c + 1], at, slabs, order)
+
+
+def flow1_kernel(grad_pre, scaled, a_own, cot, w_in, grad_own, direct):
     grad_own[...] = dg(a_own[...], scaled[...], 0, 0)
     direct[...] = cot[...].astype(F32) + dg(grad_pre[...], w_in[1, 0], 1, 1)
-    delta = dg(hidden[...], w_out[1], 1, 0)
-    live = alive_rows(count, before.shape[0])
-    final[...] = (before[...].astype(F32) + live * delta).astype(BF16)
-
-
-def flow0_kernel(gradient, grad_pre, scaled, a_own, w_in, grad_own, direct):
+
+
+def flow0_kernel(scaled, a_own, grad_own):
     grad_own[...] = dg(a_own[...], scaled[...], 0, 0)
-    direct[...] = gradient[...] + dg(grad_pre[...], w_in[0, 0], 1, 1)
 
 
 def turn_kernel(
@@ -267,17 +265,40 @@
 
 
 def end_kernel(
-    slabs, norm, core, rows, grad_own, near, far, direct, latents, w_msg,
-    gradient, keep, give,
-    gup_all, tall,
-):
-    n = direct.shape[0]
+    slabs, norm, order, core, rows, grad_own, near, far, latents,
+    gup_all, keep, give,
+    tall,
+):
+    n = latents.shape[0]
     total = grad_own[...] + dg(picks(rows, 1 - core[0], n), near[...], 1, 0)
     total = total + dg(picks(rows, core[0], n), far[...], 1, 0)
     gup_all[...] = total.astype(BF16)
     value = dg(latents[...], gup_all[...], 0, 0)
-    pack_rows(core[0], tall, (value * norm).astype(BF16), keep, give, 0, slabs)
-    gradient[...] = direct[...] + dg(gup_all[...], w_msg[0], 1, 1)
+    pack_rows(core[0], tall, (value * norm).astype(BF16), keep, give, 0, slabs, order)
+
+
+def share_kernel(plan, *refs):
+    outs = refs[-3:]
+    for c, pieces in enumerate(plan):
+        half, here, got = refs[3 * c : 3 * c + 3]
+        total = half[here[0], 0].astype(F32) + got[0].astype(F32)
+        at = 0
+        for o, layer, parts in pieces:
+            out = outs[o]
+            rows, width = out.shape[-2], total.shape[-1]
+            for p in range(parts):
+                for h in range(out.shape[-1] // width):
+                    block = (layer, p) if len(out.shape) == 4 else (layer,)
+                    out[(*block, slice(None), slice(h * width, (h + 1) * width))] = total[at : at + rows]
+                    at += rows
+
+
+def tail_kernel(count, gradient1, grad_pre, grad_update, current, hidden, w_msg, w_in, w_out, gradient, final):
+    direct = gradient1[...] + dg(grad_pre[...], w_in[0, 0], 1, 1)
+    gradient[...] = direct + dg(grad_update[...], w_msg[0], 1, 1)
+    delta = dg(hidden[...], w_out[1], 1, 0)
+    live = alive_rows(count, current.shape[0])
+    final[...] = (current[...].astype(F32) + live * delta).astype(BF16)
 
 
 VMEM = pl.BlockSpec(memory_space=pltpu.VMEM)
@@ -294,28 +315,25 @@
             out_shape=[jax.ShapeDtypeStruct(s, d) for s, d in outs],
             scratch_shapes=scratch,
             compiler_params=pltpu.CompilerParams(vmem_limit_bytes=limit << 20),
-            cost_estimate=pl.CostEstimate(
-                flops=int(gflops * 1e9), transcendentals=0, bytes_accessed=int(gflops * 2e6)
-            ),
+            cost_estimate=pl.CostEstimate(flops=int(gflops * 1e9), transcendentals=0, bytes_accessed=int(gflops * 2e6)),
         )(*args)
 
     return run
 
 
-def reduce_rows(keep, give, slabs, bits):
+def reduce_rows(keep, give, slabs, place, order):
     mine = keep
-    for step, (here, there) in enumerate(((None, None), *bits)):
+    for step, bit in enumerate((0, *order)):
         if step:
+            here, there = place[bit - 1]
             half = mine.reshape(2, mine.shape[0] // 2, *mine.shape[1:])
-            mine, give = (
-                lax.dynamic_index_in_dim(half, i, 0, keepdims=False, allow_negative_indices=False)
-                for i in (here, there)
-            )
-        got = lax.ppermute(give, "slab", [(i, i ^ (1 << step)) for i in range(slabs)])
-        mine = mine.astype(F32) + got.astype(F32)
-        if step < len(bits):
-            mine = mine.astype(BF16)
-    return mine[0]
+            take = functools.partial(lax.dynamic_index_in_dim, keepdims=False, allow_negative_indices=False)
+            give = take(half, there, 0)
+            mine = take(half, here, 0)
+        got = lax.ppermute(give, "slab", [(i, i ^ (1 << bit)) for i in range(slabs)])
+        if step == len(order):
+            return half, here.reshape(1), got
+        mine = (mine.astype(F32) + got.astype(F32)).astype(BF16)
 
 
 def body(latents, positions, counts, send_rows, tiles, w_msg, w_in, w_out, cotangent):
@@ -324,10 +342,11 @@
     slabs = lax.axis_size("slab")
     norm = 1.0 / math.sqrt(slabs * n)
     rows = send_rows[0]
+    tiles = tiles.transpose(0, 2, 1)
     me = lax.axis_index("slab").astype(jnp.int32)
     core = (me & 1).reshape(1)
     place = [((me >> b) & 1, 1 - ((me >> b) & 1)) for b in range(1, slabs.bit_length() - 1)]
-    ready = [x.reshape(1) for pair in place for x in pair] + [tiles]
+    ready = [x.reshape(1) for pair in place for x in pair]
     near_pairs = [(i, i ^ 1) for i in range(slabs)]
     far_pairs = [(i, i + 1 if i % 2 else i - 1) for i in range(1, slabs - 1)]
 
@@ -341,13 +360,12 @@
     halo_b = ((HALO, width), BF16)
     w_in_b = pltpu.VMEM((width, hidden_width), BF16)
     w_out_b = pltpu.VMEM((hidden_width, width), BF16)
-    row_buf = pltpu.VMEM((n, width), BF16)
-
-    near, far, latents, positions, w_msg0, w_in00 = call(
-        functools.partial(send_kernel, len(ready)), [SMEM] * 2 + [VMEM] + [HBM] * 4 + [SMEM] * len(ready),
+
+    near, far, rows, latents, positions, w_msg0, w_in00 = call(
+        functools.partial(send_kernel, len(ready)), [SMEM] * 2 + [HBM] * 5 + [SMEM] * len(ready),
         [((HALO + GEO, width), BF16)] * 2
-        + [row_b, (positions.shape, F32), ((width, width), BF16), ((width, hidden_width), BF16)],
-        [pltpu.VMEM((GEO, n), F32), pltpu.SemaphoreType.DMA((4,))], 0.5, WHOLE,
+        + [(rows.shape, jnp.int32), row_b, (positions.shape, F32), ((width, width), BF16), ((width, hidden_width), BF16)],
+        [pltpu.VMEM((GEO, n), F32), pltpu.SemaphoreType.DMA((5,))], 0.5, WHOLE,
     )(counts, core, rows, latents, positions, w_msg, w_in, *ready)
     near, far = trade(near, far)
 
@@ -386,13 +404,14 @@
             [o for h in heights for o in half(h)], [w_in_b, w_out_b], 4,
         )(core, *args)
 
-    out1 = terms((((0, 1),),), (out_rows,), (hidden1, grad_delta1))
-    in1 = terms((((0, 2), (1, 2)),), (in_rows,), (current1, message1, grad_pre1))
-    grad_own, direct, final = call(
-        flow1_kernel, [SMEM] + [VMEM] * 8, [row_f, row_f, row_b], [], 4,
-    )(counts, current1, hidden1, grad_pre1, scaled1, a_own, cotangent, w_in, w_out)
-    share_out1 = reduce_rows(*out1, slabs, place)
-    share_in1 = reduce_rows(*in1, slabs, place)
+    bits = list(range(1, slabs.bit_length() - 1))
+    plain = tuple(bits)
+    swapped = (2, 1, *bits[2:])
+    out1 = terms(((plain, ((0, 1),)),), (out_rows,), (hidden1, grad_delta1))
+    in1 = terms(((swapped, ((0, 2), (1, 2))),), (in_rows,), (current1, message1, grad_pre1))
+    grad_own, direct = call(flow1_kernel, [VMEM] * 5, [row_f, row_f], [], 3)(grad_pre1, scaled1, a_own, cotangent, w_in)
+    share_out1 = reduce_rows(*out1, slabs, place, plain)
+    share_in1 = reduce_rows(*in1, slabs, place, swapped)
 
     grad_update1, gradient1, grad_delta0, grad_pre0, scaled0, near, far = call(
         turn_kernel, [SMEM] * 2 + [VMEM] * 11,
@@ -400,27 +419,27 @@
     )(counts, core, rows, grad_own, near, far, direct, slope0, inverse, a_ghost, w_msg, w_in, w_out)
     near, far = trade(near, far)
 
-    out0 = terms((((2, 4), (3, 4)), ((5, 6), (0, 1))), (in_rows, msg_rows + out_rows),
+    out0 = terms(((plain, ((2, 4), (3, 4))), (swapped, ((5, 6), (0, 1)))), (in_rows, msg_rows + out_rows),
                  (hidden0, grad_delta0, latents, message0, grad_pre0, current1, grad_update1))
-    grad_own, direct = call(
-        flow0_kernel, [VMEM] * 5, [row_f, row_f], [], 3,
-    )(gradient1, grad_pre0, scaled0, a_own, w_in)
-    share_in0 = reduce_rows(out0[0], out0[1], slabs, place)
-    share_mix = reduce_rows(out0[2], out0[3], slabs, place)
-
-    gradient, keep, give = call(
-        functools.partial(end_kernel, slabs, norm), [SMEM] + [VMEM] * 7,
-        [row_f] + half(msg_rows), [row_buf, w_out_b], 2,
-    )(core, rows, grad_own, near, far, direct, latents, w_msg)
-    share_msg0 = reduce_rows(keep, give, slabs, place)
-
-    def unpack_in(share):
-        parts = share.reshape(2, hidden_width // width, msg_rows, width)
-        return jnp.concatenate([parts[:, h] for h in range(hidden_width // width)], axis=-1)
-
-    grad_msg = jnp.stack([share_msg0, share_mix[:msg_rows]])
-    grad_out = jnp.stack([share_mix[msg_rows:], share_out1])
-    grad_in = jnp.stack([unpack_in(share_in0), unpack_in(share_in1)])
+    (grad_own,) = call(flow0_kernel, [VMEM] * 2, [row_f], [], 2)(scaled0, a_own)
+    share_in0 = reduce_rows(*out0[:2], slabs, place, plain)
+    share_mix = reduce_rows(*out0[2:], slabs, place, swapped)
+
+    grad_update0, keep, give = call(
+        functools.partial(end_kernel, slabs, norm, plain), [SMEM] + [VMEM] * 5,
+        [row_b] + half(msg_rows), [w_out_b], 2,
+    )(core, rows, grad_own, near, far, latents)
+    share_msg0 = reduce_rows(keep, give, slabs, place, plain)
+
+    gradient, final = call(
+        tail_kernel, [SMEM] + [VMEM] * 8, [row_f, row_b], [], 4,
+    )(counts, gradient1, grad_pre0, grad_update0, current1, hidden1, w_msg, w_in, w_out)
+
+    plan = (((2, 1, 1),), ((1, 1, 2),), ((1, 0, 2),), ((0, 1, 1), (2, 0, 1)), ((0, 0, 1),))
+    grad_msg, grad_in, grad_out = call(
+        functools.partial(share_kernel, plan), [VMEM, SMEM, VMEM] * len(plan),
+        [((2, msg_rows, width), F32), ((2, 2, msg_rows, hidden_width), F32), ((2, out_rows, width), F32)], [], 0.1,
+    )(*share_out1, *share_in1, *share_in0, *share_mix, *share_msg0)
     return (final, gradient, grad_msg, grad_in, grad_out)
 
 

time: 157 us -> 131 us (0.83)
  waiting for transfers between devices: 56 us -> 32.4 us
  other arithmetic: 4.22 us -> 1.84 us
  starting transfers between devices: 42.1 us -> 43.7 us
    ppermute x20, waiting for transfers between devices: 55.9 us -> 32.4 us  [reduce_rows(): got = lax.ppermute(give, 'slab', [(i, i ^ 1 << bit) for i in range(slabs)])]
    another operation x4 -> x0, other arithmetic: 2.26 us -> none  [the longest x2 0.87 us: body(): grad_in = jnp.stack([unpack_in(share_in0), unpack_in(share_in1)])]
    pallas_call x12 -> x14, Pallas kernels: 49.7 us -> 49.5 us  [run(): pl.pallas_call(kernel, in_specs=where, out_specs=[VMEM] * len(outs), out_...]
  transfers between devices with their start and end apart: 28 -> 28, of which waited for: 12 -> 8; matrix products, arithmetic and copies ran while one was open for 2% -> 2% of each run, Pallas kernels for 21% -> 25%
where the time goes in v2:
time: 131 us
  Pallas kernels  49.5 us (38%)
  starting transfers between devices  43.7 us (33%)
  waiting for transfers between devices  32.4 us (25%)
  other arithmetic  1.84 us (1%)
  local copies, waits for them, and re-layouts  1.77 us (1%)
  between operations  1.77 us (1%)
    pallas_call x14, Pallas kernels, run(): pl.pallas_call(kernel, in_specs=where, out_specs=[VMEM] * len(outs), out_...  49.5 us
    ppermute x20, waiting for transfers between devices, reduce_rows(): got = lax.ppermute(give, 'slab', [(i, i ^ 1 << bit) for i in range(slabs)])  32.4 us
    ppermute x20, starting transfers between devices, reduce_rows(): got = lax.ppermute(give, 'slab', [(i, i ^ 1 << bit) for i in range(slabs)])  29.9 us
    ppermute x4, starting transfers between devices, trade(): near = lax.ppermute(near, 'slab', near_pairs)  10.4 us
    ppermute x4, starting transfers between devices, trade(): far = lax.ppermute(far, 'slab', far_pairs)  3.32 us
  transfers between devices with their start and end apart: 28, of which 8 were waited for; matrix products, arithmetic and copies ran while one was open for 2% of the time, Pallas kernels for 25%

profile of v2, /device:TPU:0, one launch (start us, length us, event | category | flops | bytes accessed | tf_op | source)
XLA Modules:
  0.0 130.9 jit_solution(10970860198141902794)
XLA Ops:
  2.7 2.2 %shard_map.128 = (bf16[272,512]{1,0:T(8,128)(2,1)S(1)}, bf16[272,512]{1,0:T(8,128)(2,1)S(1)}, s32[2,256]{1,0:T(2,128)S(1)}, bf16[1024,512]{1,0:T(8,128)(2,1)S(1)...) custom-call(s32[1]{0:T(128)S(6)} %copy.19.count, s32[1]{0:T(128)} %bitcast.core, ...), custom_call_target="tpu_custom_call" | custom-call | flops 500000000 | bytes 1000000 | tf_op jit(solution)/shard_map/pallas_call | solution.py:311
  6.2 7.4 %shard_map.129 = (bf16[1024,1024]{1,0:T(8,128)(2,1)S(1)}, f32[1024,128]{1,0:T(8,128)S(1)}, f32[1024,128]{1,0:T(8,128)S(1)}, bf16[1024,512]{1,0:T(8,128)(2,1)}, f...) custom-call(s32[1]{0:T(128)S(6)} %copy.19.count, s32[1,4,8]{2,1,0:T(4,128)S(1)} %bitcast.90, ...), custom_call_target="tpu_custom_call" | custom-call | flops 5000000000 | bytes 10000000 | tf_op jit(solution)/shard_map/pallas_call | solution.py:311
  13.6 8.0 %shard_map.130 = (bf16[1024,512]{1,0:T(8,128)(2,1)S(1)}, f32[1024,128]{1,0:T(8,128)S(1)}, bf16[1024,512]{1,0:T(8,128)(2,1)S(1)}, bf16[1024,1024]{1,0:T(8,128)(2,...) custom-call(s32[1]{0:T(128)S(6)} %copy.19.count, ...), custom_call_target="tpu_custom_call" | custom-call | flops 5000000000 | bytes 10000000 | tf_op jit(solution)/shard_map/pallas_call | solution.py:311
  21.7 3.9 %collective-permute-start.2 = (bf16[256,512]{1,0:T(8,128)(2,1)S(1)}, bf16[256,512]{1,0:T(8,128)(2,1)S(1)}, u32[]{:S(2)}, u32[]{:S(2)}) collective-permute-start(bf16[256,512]{1,0:T(8,128)(2,1)S(1)} %get-tuple-element.72), channel_id=1, source_target_pairs={{0,1},{1,0},{2,3},{3,2},{4,5},{5,4},{6,7},{7,6},{8,9},{9,8},{10,11... | collective-permute-start | bytes 786440 | tf_op jit(solution)/shard_map/ppermute | solution.py:355
  26.5 3.4 %shard_map.131 = (f32[1024,512]{1,0:T(8,128)S(1)}, bf16[1024,1024]{1,0:T(8,128)(2,1)S(1)}, bf16[1024,512]{1,0:T(8,128)(2,1)S(1)}, bf16[1024,1024]{1,0:T(8,128)(2,1)S(1)}) custom-call(s32[1]{0:T(128)S(6)} %copy.19.count, bf16[1024,512]{1,0:T(8,128)(2,1)S(1)} %get-tuple-element.76.current.refs_0_.refs_5_, bf16[1024,512]{1,0:T(8,128)(2,1)S(1)} %get-tuple-element.77.update, ...), custom_call_target="tpu_custom_call" | custom-call | flops 3000000000 | bytes 6000000 | tf_op jit(solution)/shard_map/pallas_call | solution.py:311
  29.9 5.3 %shard_map.132 = (bf16[1024,512]{1,0:T(8,128)(2,1)S(1)}, bf16[1024,1024]{1,0:T(8,128)(2,1)S(1)}, bf16[1024,1024]{1,0:T(8,128)(2,1)S(1)}, bf16[1024,512]{1,0:T(8,...) custom-call(bf16[256,512]{1,0:T(8,128)(2,1)S(1)} %collective-permute-done.2.near, ...), custom_call_target="tpu_custom_call" | custom-call | flops 4000000000 | bytes 8000000 | tf_op jit(solution)/shard_map/pallas_call | solution.py:311
  35.2 5.4 %collective-permute-start.4 = (bf16[256,512]{1,0:T(8,128)(2,1)S(1)}, bf16[256,512]{1,0:T(8,128)(2,1)S(1)}, u32[]{:S(2)}, u32[]{:S(2)}) collective-permute-start(bf16[256,512]{1,0:T(8,128)(2,1)S(1)} %get-tuple-element.85), channel_id=1, source_target_pairs={{0,1},{1,0},{2,3},{3,2},{4,5},{5,4},{6,7},{7,6},{8,9},{9,8},{10,11... | collective-permute-start | bytes 786440 | tf_op jit(solution)/shard_map/ppermute | solution.py:355
  41.5 1.4 %shard_map.138 = (bf16[8,64,512]{2,1,0:T(8,128)(2,1)S(1)}, bf16[8,64,512]{2,1,0:T(8,128)(2,1)S(1)}) custom-call(s32[1]{0:T(128)} %bitcast.core, bf16[1024,1024]{1,0:T(8,128)(2,1)S(1)} %get-tuple-element.95.hidden.refs_0_, bf16[1024,512]{1,0:T(8,128)(2,1)S(1)} %get-tuple-element.98.refs_1_), custom_call_target="tpu_custom_call" | custom-call | flops 4000000000 | bytes 8000000 | tf_op jit(solution)/shard_map/pallas_call | solution.py:311
  42.8 3.8 %collective-permute-start.8 = (bf16[8,64,512]{2,1,0:T(8,128)(2,1)S(1)}, bf16[8,64,512]{2,1,0:T(8,128)(2,1)S(1)}, u32[]{:S(2)}, u32[]{:S(2)}) collective-permute-start(bf16[8,64,512]{2,1,0:T(8,128)(2,1)S(1)} %get-tuple-element.100), channel_id=1, source_target_pairs={{0,1},{1,0},{2,3},{3,2},{4,5},{5,4},{6,7},{7,6},{8,9},{9,8},{10,11... | collective-permute-start | bytes 1572872 | tf_op jit(solution)/shard_map/ppermute | solution.py:333
  46.6 2.5 %shard_map.139 = (bf16[8,128,512]{2,1,0:T(8,128)(2,1)S(1)}, bf16[8,128,512]{2,1,0:T(8,128)(2,1)S(1)}) custom-call(s32[1]{0:T(128)} %bitcast.core, bf16[1024,512]{1,0:T(8,128)(2,1)S(1)} %get-tuple-element.76.current.refs_0_.refs_5_, bf16[1024,512]{1,0:T(8,128)(2,1)S(1)} %get-tuple-element.101.refs_1_, bf16[1024,1024]{1,0:T(8,128)(2,1)S(1)} %get-tuple-element.82.grad_pre.refs_2_), custom_call_target="tpu_custom_call" | custom-call | flops 4000000000 | bytes 8000000 | tf_op jit(solution)/shard_map/pallas_call | solution.py:311
  49.2 2.4 %shard_map.133 = (f32[1024,512]{1,0:T(8,128)S(1)}, f32[1024,512]{1,0:T(8,128)S(1)}) custom-call(bf16[1024,1024]{1,0:T(8,128)(2,1)S(1)} %get-tuple-element.82.grad_pre.refs_2_, bf16[1024,512]{1,0:T(8,128)(2,1)S(1)} %get-tuple-element.83.scaled, bf16[1024,1024]{1,0:T(8,128)(2,1)S(1)} %get-tuple-element.78.a_own, bf16[1024,512]{1,0:T(8,128)(2,1)S(1)} %copy-done.3, ...), custom_call_target="tpu_custom_call" | custom-call | flops 3000000000 | bytes 6000000 | tf_op jit(solution)/shard_map/pallas_call | solution.py:311
  51.6 4.7 %shard_map.134 = (bf16[1024,512]{1,0:T(8,128)(2,1)S(1)}, f32[1024,512]{1,0:T(8,128)S(1)}, bf16[1024,512]{1,0:T(8,128)(2,1)S(1)}, bf16[1024,1024]{1,0:T(8,128)(2,...) custom-call(s32[1]{0:T(128)S(6)} %copy.19.count, s32[1]{0:T(128)} %bitcast.core, ...), custom_call_target="tpu_custom_call" | custom-call | flops 4000000000 | bytes 8000000 | tf_op jit(solution)/shard_map/pallas_call | solution.py:311
  57.8 4.2 %shard_map.140 = (bf16[8,128,512]{2,1,0:T(8,128)(2,1)S(1)}, bf16[8,128,512]{2,1,0:T(8,128)(2,1)S(1)}, bf16[8,96,512]{2,1,0:T(8,128)(2,1)S(1)}, bf16[8,96,512]{2,1,0:T(8,128)(2,1)S(1)}) custom-call(s32[1]{0:T(128)} %bitcast.core, bf16[1024,1024]{1,0:T(8,128)(2,1)S(1)} %get-tuple-element.104.refs_0_, bf16[1024,512]{1,0:T(8,128)(2,1)S(1)} %get-tuple-element.105.refs_1_, ...), custom_call_target="tpu_custom_call" | custom-call | flops 4000000000 | bytes 8000000 | tf_op jit(solution)/shard_map/pallas_call | solution.py:311
  62.0 3.3 %collective-permute-start.20 = (bf16[8,96,512]{2,1,0:T(8,128)(2,1)S(1)}, bf16[8,96,512]{2,1,0:T(8,128)(2,1)S(1)}, u32[]{:S(2)}, u32[]{:S(2)}) collective-permute-start(bf16[8,96,512]{2,1,0:T(8,128)(2,1)S(1)} %get-tuple-element.111), channel_id=1, source_target_pairs={{0,1},{1,0},{2,3},{3,2},{4,5},{5,4},{6,7},{7,6},{8,9},{9,8},{10,11... | collective-permute-start | bytes 2359304 | tf_op jit(solution)/shard_map/ppermute | solution.py:333
  65.3 1.3 shard_map.135.grad_own
  66.7 1.3 %shard_map.136 = (bf16[1024,512]{1,0:T(8,128)(2,1)S(1)}, bf16[8,32,512]{2,1,0:T(8,128)(2,1)S(1)}, bf16[8,32,512]{2,1,0:T(8,128)(2,1)S(1)}) custom-call(s32[1]{0:T(128)} %bitcast.core, s32[2,256]{1,0:T(2,128)S(1)} %get-tuple-element.61.rows, f32[1024,512]{1,0:T(8,128)S(1)} %shard_map.135.grad_own, bf16[256,512]{1,0:T(8,128)(2,1)S(1)} %collective-permute-done.6.near, ...), custom_call_target="tpu_custom_call" | custom-call | flops 2000000000 | bytes 4000000 | tf_op jit(solution)/shard_map/pallas_call | solution.py:311
  68.8 2.2 %collective-permute-start.9 = (bf16[4,64,512]{2,1,0:T(8,128)(2,1)S(1)}, bf16[4,64,512]{2,1,0:T(8,128)(2,1)S(1)}, u32[]{:S(2)}, u32[]{:S(2)}) collective-permute-start(bf16[4,64,512]{2,1,0:T(8,128)(2,1)S(1)} %dynamic-slice_bitcast_fusion.5), channel_id=1, source_target_pairs={{0,2},{1,3},{2,0},{3,1},{4,6},{5,7},{6,4},{7,5},{8,10},{9,11},{10,... | collective-permute-start | bytes 786440 | tf_op jit(solution)/shard_map/ppermute | solution.py:333
  71.0 1.3 %collective-permute-start.25 = (bf16[4,32,512]{2,1,0:T(8,128)(2,1)S(1)}, bf16[4,32,512]{2,1,0:T(8,128)(2,1)S(1)}, u32[]{:S(2)}, u32[]{:S(2)}) collective-permute-start(bf16[4,32,512]{2,1,0:T(8,128)(2,1)S(1)} %dynamic-slice_bitcast_fusion.7), channel_id=1, source_target_pairs={{0,2},{1,3},{2,0},{3,1},{4,6},{5,7},{6,4},{7,5},{8,10},{9,11},{10,... | collective-permute-start | bytes 393224 | tf_op jit(solution)/shard_map/ppermute | solution.py:333
  72.3 5.7 %collective-permute-done.9 = bf16[4,64,512]{2,1,0:T(8,128)(2,1)S(1)} collective-permute-done((bf16[4,64,512]{2,1,0:T(8,128)(2,1)S(1)}, bf16[4,64,512]{2,1,0:T(8,128)(2,1)S(1)}, u32[]{:S(2)}, u32[]{:S(2)}) %collective-permute-start.9) | collective-permute-done | bytes 262176 | tf_op jit(solution)/shard_map/ppermute | solution.py:333
  78.2 2.1 %collective-permute-start.10 = (bf16[2,64,512]{2,1,0:T(8,128)(2,1)S(1)}, bf16[2,64,512]{2,1,0:T(8,128)(2,1)S(1)}, u32[]{:S(2)}, u32[]{:S(2)}) collective-permute-start(bf16[2,64,512]{2,1,0:T(8,128)(2,1)S(1)} %dynamic-slice_bitcast_fusion.8), channel_id=1, source_target_pairs={{0,4},{1,5},{2,6},{3,7},{4,0},{5,1},{6,2},{7,3},{8,12},{9,13},{10,... | collective-permute-start | bytes 393224 | tf_op jit(solution)/shard_map/ppermute | solution.py:333
  80.7 1.6 %collective-permute-start.26 = (bf16[2,32,512]{2,1,0:T(8,128)(2,1)S(1)}, bf16[2,32,512]{2,1,0:T(8,128)(2,1)S(1)}, u32[]{:S(2)}, u32[]{:S(2)}) collective-permute-start(bf16[2,32,512]{2,1,0:T(8,128)(2,1)S(1)} %dynamic-slice_bitcast_fusion.9), channel_id=1, source_target_pairs={{0,4},{1,5},{2,6},{3,7},{4,0},{5,1},{6,2},{7,3},{8,12},{9,13},{10,... | collective-permute-start | bytes 196616 | tf_op jit(solution)/shard_map/ppermute | solution.py:333
  83.6 3.8 %collective-permute-start.11 = (bf16[1,64,512]{2,1,0:T(8,128)(2,1)S(1)}, bf16[1,64,512]{2,1,0:T(8,128)(2,1)S(1)}, u32[]{:S(2)}, u32[]{:S(2)}) collective-permute-start(bf16[1,64,512]{2,1,0:T(8,128)(2,1)S(1)} %constant_dynamic-slice_fusion.4), channel_id=1, source_target_pairs={{0,8},{1,9},{2,10},{3,11},{4,12},{5,13},{6,14},{7,15},{8,0},{9,1},... | collective-permute-start | bytes 196616 | tf_op jit(solution)/shard_map/ppermute | solution.py:333
  88.8 1.5 %collective-permute-start.21 = (bf16[4,96,512]{2,1,0:T(8,128)(2,1)S(1)}, bf16[4,96,512]{2,1,0:T(8,128)(2,1)S(1)}, u32[]{:S(2)}, u32[]{:S(2)}) collective-permute-start(bf16[4,96,512]{2,1,0:T(8,128)(2,1)S(1)} %dynamic-slice_bitcast_fusion.2), channel_id=1, source_target_pairs={{0,4},{1,5},{2,6},{3,7},{4,0},{5,1},{6,2},{7,3},{8,12},{9,13},{10,... | collective-permute-start | bytes 1179656 | tf_op jit(solution)/shard_map/ppermute | solution.py:333
  91.7 1.6 %collective-permute-start.17 = (bf16[4,128,512]{2,1,0:T(8,128)(2,1)S(1)}, bf16[4,128,512]{2,1,0:T(8,128)(2,1)S(1)}, u32[]{:S(2)}, u32[]{:S(2)}) collective-permute-start(bf16[4,128,512]{2,1,0:T(8,128)(2,1)S(1)} %dynamic-slice_bitcast_fusion), channel_id=1, source_target_pairs={{0,2},{1,3},{2,0},{3,1},{4,6},{5,7},{6,4},{7,5},{8,10},{9,11},{10,... | collective-permute-start | bytes 1572872 | tf_op jit(solution)/shard_map/ppermute | solution.py:333
  93.3 7.6 %collective-permute-done.21 = bf16[4,96,512]{2,1,0:T(8,128)(2,1)S(1)} collective-permute-done((bf16[4,96,512]{2,1,0:T(8,128)(2,1)S(1)}, bf16[4,96,512]{2,1,0:T(8,128)(2,1)S(1)}, u32[]{:S(2)}, u32[]{:S(2)}) %collective-permute-start.21) | collective-permute-done | bytes 393248 | tf_op jit(solution)/shard_map/ppermute | solution.py:333
  101.0 1.6 %collective-permute-start.22 = (bf16[2,96,512]{2,1,0:T(8,128)(2,1)S(1)}, bf16[2,96,512]{2,1,0:T(8,128)(2,1)S(1)}, u32[]{:S(2)}, u32[]{:S(2)}) collective-permute-start(bf16[2,96,512]{2,1,0:T(8,128)(2,1)S(1)} %dynamic-slice_bitcast_fusion.6), channel_id=1, source_target_pairs={{0,2},{1,3},{2,0},{3,1},{4,6},{5,7},{6,4},{7,5},{8,10},{9,11},{10,... | collective-permute-start | bytes 589832 | tf_op jit(solution)/shard_map/ppermute | solution.py:333
  102.6 7.3 %collective-permute-done.13 = bf16[4,128,512]{2,1,0:T(8,128)(2,1)S(1)} collective-permute-done((bf16[4,128,512]{2,1,0:T(8,128)(2,1)S(1)}, bf16[4,128,512]{2,1,0:T(8,128)(2,1)S(1)}, u32[]{:S(2)}, u32[]{:S(2)}) %collective-permute-start.13) | collective-permute-done | bytes 524320 | tf_op jit(solution)/shard_map/ppermute | solution.py:333
  110.1 1.5 %collective-permute-start.14 = (bf16[2,128,512]{2,1,0:T(8,128)(2,1)S(1)}, bf16[2,128,512]{2,1,0:T(8,128)(2,1)S(1)}, u32[]{:S(2)}, u32[]{:S(2)}) collective-permute-start(bf16[2,128,512]{2,1,0:T(8,128)(2,1)S(1)} %dynamic-slice_bitcast_fusion.4), channel_id=1, source_target_pairs={{0,2},{1,3},{2,0},{3,1},{4,6},{5,7},{6,4},{7,5},{8,10},{9,11},{10,... | collective-permute-start | bytes 786440 | tf_op jit(solution)/shard_map/ppermute | solution.py:333
  114.1 2.5 %collective-permute-done.14 = bf16[2,128,512]{2,1,0:T(8,128)(2,1)S(1)} collective-permute-done((bf16[2,128,512]{2,1,0:T(8,128)(2,1)S(1)}, bf16[2,128,512]{2,1,0:T(8,128)(2,1)S(1)}, u32[]{:S(2)}, u32[]{:S(2)}) %collective-permute-start.14) | collective-permute-done | bytes 262176 | tf_op jit(solution)/shard_map/ppermute | solution.py:333
  117.5 6.0 %collective-permute-done.18 = bf16[2,128,512]{2,1,0:T(8,128)(2,1)S(1)} collective-permute-done((bf16[2,128,512]{2,1,0:T(8,128)(2,1)S(1)}, bf16[2,128,512]{2,1,0:T(8,128)(2,1)S(1)}, u32[]{:S(2)}, u32[]{:S(2)}) %collective-permute-start.18) | collective-permute-done | bytes 262176 | tf_op jit(solution)/shard_map/ppermute | solution.py:333
  123.7 4.5 %shard_map.137 = (f32[1024,512]{1,0:T(8,128)}, bf16[1024,512]{1,0:T(8,128)(2,1)}) custom-call(s32[1]{0:T(128)S(6)} %copy.19.count, f32[1024,512]{1,0:T(8,128)S(1)} %get-tuple-element.89.gradient1, bf16[1024,1024]{1,0:T(8,128)(2,1)S(1)} %get-tuple-element.90.grad_pre.refs_4_, bf16[1024,512]{1,0:T(8,128)(2,1)S(1)} %get-tuple-element.94.grad_update, ...), custom_call_target="tpu_custom_call" | custom-call | flops 4000000000 | bytes 8000000 | tf_op jit(solution)/shard_map/pallas_call | solution.py:311
  128.2 1.7 %collective-permute-done.19.refs_8_ = bf16[1,128,512]{2,1,0:T(8,128)(2,1)S(1)} collective-permute-done((bf16[1,128,512]{2,1,0:T(8,128)(2,1)S(1)}, bf16[1,128,512]{2,1,0:T(8,128)(2,1)S(1)}, u32[]{:S(2)}, u32[]{:S(2)}) %collective-permute-start.19) | collective-permute-done | bytes 131104 | tf_op jit(solution)/shard_map/ppermute | solution.py:333
  (82 shorter events, 16.2 us)
Async XLA Ops:
  4.9 8.6 %collective-permute-start = (bf16[272,512]{1,0:T(8,128)(2,1)S(1)}, bf16[272,512]{1,0:T(8,128)(2,1)S(1)}, u32[]{:S(2)}, u32[]{:S(2)}) collective-permute-start(bf16[272,512]{1,0:T(8,128)(2,1)S(1)} %get-tuple-element.63), channel_id=1, source_target_pairs={{0,1},{1,0},{2,3},{3,2},{4,5},{5,4},{6,7},{7,6},{8,9},{9,8},{10,11... | collective-permute-start | bytes 835592 | tf_op jit(solution)/shard_map/ppermute | solution.py:355
  5.5 8.1 %collective-permute-start.1 = (bf16[272,512]{1,0:T(8,128)(2,1)S(1)}, bf16[272,512]{1,0:T(8,128)(2,1)S(1)}, u32[]{:S(2)}, u32[]{:S(2)}) collective-permute-start(bf16[272,512]{1,0:T(8,128)(2,1)S(1)} %get-tuple-element.64), channel_id=1, source_target_pairs={{1,2},{2,1},{3,4},{4,3},{5,6},{6,5},{7,8},{8,7},{9,10},{10,9},{11,... | collective-permute-start | bytes 835592 | tf_op jit(solution)/shard_map/ppermute | solution.py:354
  6.2 7.4 %copy-start = (bf16[2,2,512,1024]{3,2,1,0:T(8,128)(2,1)S(1)}, bf16[2,2,512,1024]{3,2,1,0:T(8,128)(2,1)}, u32[]{:S(2)}) copy-start(bf16[2,2,512,1024]{3,2,1,0:T(8,128)(2,1)} %w_in.13) | copy-start | bytes 12582916
  6.2 7.4 %copy-start.1 = (bf16[2,1024,512]{2,1,0:T(8,128)(2,1)S(1)}, bf16[2,1024,512]{2,1,0:T(8,128)(2,1)}, u32[]{:S(2)}) copy-start(bf16[2,1024,512]{2,1,0:T(8,128)(2,1)} %w_out.7) | copy-start | bytes 6291460
  6.2 7.4 %copy-start.2 = (bf16[2,512,512]{2,1,0:T(8,128)(2,1)S(1)}, bf16[2,512,512]{2,1,0:T(8,128)(2,1)}, u32[]{:S(2)}) copy-start(bf16[2,512,512]{2,1,0:T(8,128)(2,1)} %w_msg.7) | copy-start | bytes 3145732
  13.6 12.8 %copy-start.3 = (bf16[1024,512]{1,0:T(8,128)(2,1)S(1)}, bf16[1024,512]{1,0:T(8,128)(2,1)}, u32[]{:S(2)}) copy-start(bf16[1024,512]{1,0:T(8,128)(2,1)} %cot.3) | copy-start | bytes 3145732
  21.7 8.2 %collective-permute-start.2 = (bf16[256,512]{1,0:T(8,128)(2,1)S(1)}, bf16[256,512]{1,0:T(8,128)(2,1)S(1)}, u32[]{:S(2)}, u32[]{:S(2)}) collective-permute-start(bf16[256,512]{1,0:T(8,128)(2,1)S(1)} %get-tuple-element.72), channel_id=1, source_target_pairs={{0,1},{1,0},{2,3},{3,2},{4,5},{5,4},{6,7},{7,6},{8,9},{9,8},{10,11... | collective-permute-start | bytes 786440 | tf_op jit(solution)/shard_map/ppermute | solution.py:355
  25.6 4.3 %collective-permute-start.3 = (bf16[256,512]{1,0:T(8,128)(2,1)S(1)}, bf16[256,512]{1,0:T(8,128)(2,1)S(1)}, u32[]{:S(2)}, u32[]{:S(2)}) collective-permute-start(bf16[256,512]{1,0:T(8,128)(2,1)S(1)} %get-tuple-element.73), channel_id=1, source_target_pairs={{1,2},{2,1},{3,4},{4,3},{5,6},{6,5},{7,8},{8,7},{9,10},{10,9},{11,... | collective-permute-start | bytes 786440 | tf_op jit(solution)/shard_map/ppermute | solution.py:354
  35.2 16.4 %collective-permute-start.4 = (bf16[256,512]{1,0:T(8,128)(2,1)S(1)}, bf16[256,512]{1,0:T(8,128)(2,1)S(1)}, u32[]{:S(2)}, u32[]{:S(2)}) collective-permute-start(bf16[256,512]{1,0:T(8,128)(2,1)S(1)} %get-tuple-element.85), channel_id=1, source_target_pairs={{0,1},{1,0},{2,3},{3,2},{4,5},{5,4},{6,7},{7,6},{8,9},{9,8},{10,11... | collective-permute-start | bytes 786440 | tf_op jit(solution)/shard_map/ppermute | solution.py:355
  40.6 11.0 %collective-permute-start.5 = (bf16[256,512]{1,0:T(8,128)(2,1)S(1)}, bf16[256,512]{1,0:T(8,128)(2,1)S(1)}, u32[]{:S(2)}, u32[]{:S(2)}) collective-permute-start(bf16[256,512]{1,0:T(8,128)(2,1)S(1)} %get-tuple-element.86), channel_id=1, source_target_pairs={{1,2},{2,1},{3,4},{4,3},{5,6},{6,5},{7,8},{8,7},{9,10},{10,9},{11,... | collective-permute-start | bytes 786440 | tf_op jit(solution)/shard_map/ppermute | solution.py:354
  42.8 25.8 %collective-permute-start.8 = (bf16[8,64,512]{2,1,0:T(8,128)(2,1)S(1)}, bf16[8,64,512]{2,1,0:T(8,128)(2,1)S(1)}, u32[]{:S(2)}, u32[]{:S(2)}) collective-permute-start(bf16[8,64,512]{2,1,0:T(8,128)(2,1)S(1)} %get-tuple-element.100), channel_id=1, source_target_pairs={{0,1},{1,0},{2,3},{3,2},{4,5},{5,4},{6,7},{7,6},{8,9},{9,8},{10,11... | collective-permute-start | bytes 1572872 | tf_op jit(solution)/shard_map/ppermute | solution.py:333
  49.1 41.2 %collective-permute-start.12 = (bf16[8,128,512]{2,1,0:T(8,128)(2,1)S(1)}, bf16[8,128,512]{2,1,0:T(8,128)(2,1)S(1)}, u32[]{:S(2)}, u32[]{:S(2)}) collective-permute-start(bf16[8,128,512]{2,1,0:T(8,128)(2,1)S(1)} %get-tuple-element.103), channel_id=1, source_target_pairs={{0,1},{1,0},{2,3},{3,2},{4,5},{5,4},{6,7},{7,6},{8,9},{9,8},{10,11... | collective-permute-start | bytes 3145736 | tf_op jit(solution)/shard_map/ppermute | solution.py:333
  56.3 10.3 %collective-permute-start.6 = (bf16[256,512]{1,0:T(8,128)(2,1)S(1)}, bf16[256,512]{1,0:T(8,128)(2,1)S(1)}, u32[]{:S(2)}, u32[]{:S(2)}) collective-permute-start(bf16[256,512]{1,0:T(8,128)(2,1)S(1)} %get-tuple-element.92), channel_id=1, source_target_pairs={{0,1},{1,0},{2,3},{3,2},{4,5},{5,4},{6,7},{7,6},{8,9},{9,8},{10,11... | collective-permute-start | bytes 786440 | tf_op jit(solution)/shard_map/ppermute | solution.py:355
  56.9 9.8 %collective-permute-start.7 = (bf16[256,512]{1,0:T(8,128)(2,1)S(1)}, bf16[256,512]{1,0:T(8,128)(2,1)S(1)}, u32[]{:S(2)}, u32[]{:S(2)}) collective-permute-start(bf16[256,512]{1,0:T(8,128)(2,1)S(1)} %get-tuple-element.93), channel_id=1, source_target_pairs={{1,2},{2,1},{3,4},{4,3},{5,6},{6,5},{7,8},{8,7},{9,10},{10,9},{11,... | collective-permute-start | bytes 786440 | tf_op jit(solution)/shard_map/ppermute | solution.py:354
  62.0 26.5 %collective-permute-start.20 = (bf16[8,96,512]{2,1,0:T(8,128)(2,1)S(1)}, bf16[8,96,512]{2,1,0:T(8,128)(2,1)S(1)}, u32[]{:S(2)}, u32[]{:S(2)}) collective-permute-start(bf16[8,96,512]{2,1,0:T(8,128)(2,1)S(1)} %get-tuple-element.111), channel_id=1, source_target_pairs={{0,1},{1,0},{2,3},{3,2},{4,5},{5,4},{6,7},{7,6},{8,9},{9,8},{10,11... | collective-permute-start | bytes 2359304 | tf_op jit(solution)/shard_map/ppermute | solution.py:333
  66.6 24.7 %collective-permute-start.16 = (bf16[8,128,512]{2,1,0:T(8,128)(2,1)S(1)}, bf16[8,128,512]{2,1,0:T(8,128)(2,1)S(1)}, u32[]{:S(2)}, u32[]{:S(2)}) collective-permute-start(bf16[8,128,512]{2,1,0:T(8,128)(2,1)S(1)} %get-tuple-element.109), channel_id=1, source_target_pairs={{0,1},{1,0},{2,3},{3,2},{4,5},{5,4},{6,7},{7,6},{8,9},{9,8},{10,11... | collective-permute-start | bytes 3145736 | tf_op jit(solution)/shard_map/ppermute | solution.py:333
  68.0 2.9 %collective-permute-start.24 = (bf16[8,32,512]{2,1,0:T(8,128)(2,1)S(1)}, bf16[8,32,512]{2,1,0:T(8,128)(2,1)S(1)}, u32[]{:S(2)}, u32[]{:S(2)}) collective-permute-start(bf16[8,32,512]{2,1,0:T(8,128)(2,1)S(1)} %get-tuple-element.113), channel_id=1, source_target_pairs={{0,1},{1,0},{2,3},{3,2},{4,5},{5,4},{6,7},{7,6},{8,9},{9,8},{10,11... | collective-permute-start | bytes 786440 | tf_op jit(solution)/shard_map/ppermute | solution.py:333
  68.8 9.3 %collective-permute-start.9 = (bf16[4,64,512]{2,1,0:T(8,128)(2,1)S(1)}, bf16[4,64,512]{2,1,0:T(8,128)(2,1)S(1)}, u32[]{:S(2)}, u32[]{:S(2)}) collective-permute-start(bf16[4,64,512]{2,1,0:T(8,128)(2,1)S(1)} %dynamic-slice_bitcast_fusion.5), channel_id=1, source_target_pairs={{0,2},{1,3},{2,0},{3,1},{4,6},{5,7},{6,4},{7,5},{8,10},{9,11},{10,... | collective-permute-start | bytes 786440 | tf_op jit(solution)/shard_map/ppermute | solution.py:333
  71.0 9.7 %collective-permute-start.25 = (bf16[4,32,512]{2,1,0:T(8,128)(2,1)S(1)}, bf16[4,32,512]{2,1,0:T(8,128)(2,1)S(1)}, u32[]{:S(2)}, u32[]{:S(2)}) collective-permute-start(bf16[4,32,512]{2,1,0:T(8,128)(2,1)S(1)} %dynamic-slice_bitcast_fusion.7), channel_id=1, source_target_pairs={{0,2},{1,3},{2,0},{3,1},{4,6},{5,7},{6,4},{7,5},{8,10},{9,11},{10,... | collective-permute-start | bytes 393224 | tf_op jit(solution)/shard_map/ppermute | solution.py:333
  78.2 5.3 %collective-permute-start.10 = (bf16[2,64,512]{2,1,0:T(8,128)(2,1)S(1)}, bf16[2,64,512]{2,1,0:T(8,128)(2,1)S(1)}, u32[]{:S(2)}, u32[]{:S(2)}) collective-permute-start(bf16[2,64,512]{2,1,0:T(8,128)(2,1)S(1)} %dynamic-slice_bitcast_fusion.8), channel_id=1, source_target_pairs={{0,4},{1,5},{2,6},{3,7},{4,0},{5,1},{6,2},{7,3},{8,12},{9,13},{10,... | collective-permute-start | bytes 393224 | tf_op jit(solution)/shard_map/ppermute | solution.py:333
  80.7 6.6 %collective-permute-start.26 = (bf16[2,32,512]{2,1,0:T(8,128)(2,1)S(1)}, bf16[2,32,512]{2,1,0:T(8,128)(2,1)S(1)}, u32[]{:S(2)}, u32[]{:S(2)}) collective-permute-start(bf16[2,32,512]{2,1,0:T(8,128)(2,1)S(1)} %dynamic-slice_bitcast_fusion.9), channel_id=1, source_target_pairs={{0,4},{1,5},{2,6},{3,7},{4,0},{5,1},{6,2},{7,3},{8,12},{9,13},{10,... | collective-permute-start | bytes 196616 | tf_op jit(solution)/shard_map/ppermute | solution.py:333
  83.6 44.6 %collective-permute-start.11 = (bf16[1,64,512]{2,1,0:T(8,128)(2,1)S(1)}, bf16[1,64,512]{2,1,0:T(8,128)(2,1)S(1)}, u32[]{:S(2)}, u32[]{:S(2)}) collective-permute-start(bf16[1,64,512]{2,1,0:T(8,128)(2,1)S(1)} %constant_dynamic-slice_fusion.4), channel_id=1, source_target_pairs={{0,8},{1,9},{2,10},{3,11},{4,12},{5,13},{6,14},{7,15},{8,0},{9,1},... | collective-permute-start | bytes 196616 | tf_op jit(solution)/shard_map/ppermute | solution.py:333
  87.4 40.8 %collective-permute-start.27 = (bf16[1,32,512]{2,1,0:T(8,128)(2,1)S(1)}, bf16[1,32,512]{2,1,0:T(8,128)(2,1)S(1)}, u32[]{:S(2)}, u32[]{:S(2)}) collective-permute-start(bf16[1,32,512]{2,1,0:T(8,128)(2,1)S(1)} %constant_dynamic-slice_fusion), channel_id=1, source_target_pairs={{0,8},{1,9},{2,10},{3,11},{4,12},{5,13},{6,14},{7,15},{8,0},{9,1},... | collective-permute-start | bytes 98312 | tf_op jit(solution)/shard_map/ppermute | solution.py:333
  88.8 12.1 %collective-permute-start.21 = (bf16[4,96,512]{2,1,0:T(8,128)(2,1)S(1)}, bf16[4,96,512]{2,1,0:T(8,128)(2,1)S(1)}, u32[]{:S(2)}, u32[]{:S(2)}) collective-permute-start(bf16[4,96,512]{2,1,0:T(8,128)(2,1)S(1)} %dynamic-slice_bitcast_fusion.2), channel_id=1, source_target_pairs={{0,4},{1,5},{2,6},{3,7},{4,0},{5,1},{6,2},{7,3},{8,12},{9,13},{10,... | collective-permute-start | bytes 1179656 | tf_op jit(solution)/shard_map/ppermute | solution.py:333
  90.7 19.2 %collective-permute-start.13 = (bf16[4,128,512]{2,1,0:T(8,128)(2,1)S(1)}, bf16[4,128,512]{2,1,0:T(8,128)(2,1)S(1)}, u32[]{:S(2)}, u32[]{:S(2)}) collective-permute-start(bf16[4,128,512]{2,1,0:T(8,128)(2,1)S(1)} %dynamic-slice_bitcast_fusion.1), channel_id=1, source_target_pairs={{0,4},{1,5},{2,6},{3,7},{4,0},{5,1},{6,2},{7,3},{8,12},{9,13},{10,... | collective-permute-start | bytes 1572872 | tf_op jit(solution)/shard_map/ppermute | solution.py:333
  91.7 20.9 %collective-permute-start.17 = (bf16[4,128,512]{2,1,0:T(8,128)(2,1)S(1)}, bf16[4,128,512]{2,1,0:T(8,128)(2,1)S(1)}, u32[]{:S(2)}, u32[]{:S(2)}) collective-permute-start(bf16[4,128,512]{2,1,0:T(8,128)(2,1)S(1)} %dynamic-slice_bitcast_fusion), channel_id=1, source_target_pairs={{0,2},{1,3},{2,0},{3,1},{4,6},{5,7},{6,4},{7,5},{8,10},{9,11},{10,... | collective-permute-start | bytes 1572872 | tf_op jit(solution)/shard_map/ppermute | solution.py:333
  101.0 10.6 %collective-permute-start.22 = (bf16[2,96,512]{2,1,0:T(8,128)(2,1)S(1)}, bf16[2,96,512]{2,1,0:T(8,128)(2,1)S(1)}, u32[]{:S(2)}, u32[]{:S(2)}) collective-permute-start(bf16[2,96,512]{2,1,0:T(8,128)(2,1)S(1)} %dynamic-slice_bitcast_fusion.6), channel_id=1, source_target_pairs={{0,2},{1,3},{2,0},{3,1},{4,6},{5,7},{6,4},{7,5},{8,10},{9,11},{10,... | collective-permute-start | bytes 589832 | tf_op jit(solution)/shard_map/ppermute | solution.py:333
  110.1 6.4 %collective-permute-start.14 = (bf16[2,128,512]{2,1,0:T(8,128)(2,1)S(1)}, bf16[2,128,512]{2,1,0:T(8,128)(2,1)S(1)}, u32[]{:S(2)}, u32[]{:S(2)}) collective-permute-start(bf16[2,128,512]{2,1,0:T(8,128)(2,1)S(1)} %dynamic-slice_bitcast_fusion.4), channel_id=1, source_target_pairs={{0,2},{1,3},{2,0},{3,1},{4,6},{5,7},{6,4},{7,5},{8,10},{9,11},{10,... | collective-permute-start | bytes 786440 | tf_op jit(solution)/shard_map/ppermute | solution.py:333
  111.7 16.5 %collective-permute-start.23 = (bf16[1,96,512]{2,1,0:T(8,128)(2,1)S(1)}, bf16[1,96,512]{2,1,0:T(8,128)(2,1)S(1)}, u32[]{:S(2)}, u32[]{:S(2)}) collective-permute-start(bf16[1,96,512]{2,1,0:T(8,128)(2,1)S(1)} %constant_dynamic-slice_fusion.1), channel_id=1, source_target_pairs={{0,8},{1,9},{2,10},{3,11},{4,12},{5,13},{6,14},{7,15},{8,0},{9,1},... | collective-permute-start | bytes 294920 | tf_op jit(solution)/shard_map/ppermute | solution.py:333
  112.8 10.7 %collective-permute-start.18 = (bf16[2,128,512]{2,1,0:T(8,128)(2,1)S(1)}, bf16[2,128,512]{2,1,0:T(8,128)(2,1)S(1)}, u32[]{:S(2)}, u32[]{:S(2)}) collective-permute-start(bf16[2,128,512]{2,1,0:T(8,128)(2,1)S(1)} %dynamic-slice_bitcast_fusion.3), channel_id=1, source_target_pairs={{0,4},{1,5},{2,6},{3,7},{4,0},{5,1},{6,2},{7,3},{8,12},{9,13},{10,... | collective-permute-start | bytes 786440 | tf_op jit(solution)/shard_map/ppermute | solution.py:333
  116.7 11.5 %collective-permute-start.15 = (bf16[1,128,512]{2,1,0:T(8,128)(2,1)S(1)}, bf16[1,128,512]{2,1,0:T(8,128)(2,1)S(1)}, u32[]{:S(2)}, u32[]{:S(2)}) collective-permute-start(bf16[1,128,512]{2,1,0:T(8,128)(2,1)S(1)} %constant_dynamic-slice_fusion.3), channel_id=1, source_target_pairs={{0,8},{1,9},{2,10},{3,11},{4,12},{5,13},{6,14},{7,15},{8,0},{9,1},... | collective-permute-start | bytes 393224 | tf_op jit(solution)/shard_map/ppermute | solution.py:333
  123.6 6.3 %collective-permute-start.19 = (bf16[1,128,512]{2,1,0:T(8,128)(2,1)S(1)}, bf16[1,128,512]{2,1,0:T(8,128)(2,1)S(1)}, u32[]{:S(2)}, u32[]{:S(2)}) collective-permute-start(bf16[1,128,512]{2,1,0:T(8,128)(2,1)S(1)} %constant_dynamic-slice_fusion.2), channel_id=1, source_target_pairs={{0,8},{1,9},{2,10},{3,11},{4,12},{5,13},{6,14},{7,15},{8,0},{9,1},... | collective-permute-start | bytes 393224 | tf_op jit(solution)/shard_map/ppermute | solution.py:333
  (3 other events, 4.9 us)

commit v3 on v2

--- a/solution.py
+++ b/solution.py
@@ -12,7 +12,7 @@
 TILE = 128
 HALO = 256
 GEO = 16
-BLOCK = 256
+BLOCK = 1024
 LIMIT = 16
 WHOLE = 50
 GHOST_TILES = HALO // TILE
@@ -237,10 +237,6 @@
     direct[...] = cot[...].astype(F32) + dg(grad_pre[...], w_in[1, 0], 1, 1)
 
 
-def flow0_kernel(scaled, a_own, grad_own):
-    grad_own[...] = dg(a_own[...], scaled[...], 0, 0)
-
-
 def turn_kernel(
     count, core, rows, grad_own, near, far, direct, slope, inverse, a_ghost, w_msg, w_in, w_out,
     grad_update, gradient, grad_delta, grad_pre, scaled, back_near, back_far,
@@ -264,17 +260,36 @@
     back_far[...] = dg(a_ghost[:, HALO : 2 * HALO], scaled[...], 0, 0).astype(BF16)
 
 
-def end_kernel(
-    slabs, norm, order, core, rows, grad_own, near, far, latents,
-    gup_all, keep, give,
-    tall,
-):
-    n = latents.shape[0]
+def mix_kernel(
+    slabs, norm, order, core, scaled, a_own, latents, ghost_near, ghost_far, back_near, back_far,
+    later, later_update, hidden, grad_delta,
+    grad_own, keep, give,
+    own, tall,
+):
+    grad_own[...] = dg(a_own[...], scaled[...], 0, 0)
+    own[...] = grad_own[...].astype(BF16)
+    value = dg(latents[...], own[...], 0, 0)
+    value = value + dg(ghost_near[0:HALO, :], back_near[...], 0, 0)
+    value = value + dg(ghost_far[0:HALO, :], back_far[...], 0, 0)
+    at = pack_rows(core[0], tall, (value * norm).astype(BF16), keep, give, 0, slabs, order)
+    value = dg(later[...], later_update[...], 0, 0)
+    at = pack_rows(core[0], tall, (value * norm).astype(BF16), keep, give, at, slabs, order)
+    value = dg(hidden[...], grad_delta[...], 0, 0)
+    pack_rows(core[0], tall, (value * norm).astype(BF16), keep, give, at, slabs, order)
+
+
+def rest_kernel(count, gradient1, grad_pre, current, hidden, w_in, w_out, direct, final):
+    direct[...] = gradient1[...] + dg(grad_pre[...], w_in[0, 0], 1, 1)
+    delta = dg(hidden[...], w_out[1], 1, 0)
+    live = alive_rows(count, current.shape[0])
+    final[...] = (current[...].astype(F32) + live * delta).astype(BF16)
+
+
+def end_kernel(core, rows, grad_own, near, far, direct, w_msg, gradient):
+    n = direct.shape[0]
     total = grad_own[...] + dg(picks(rows, 1 - core[0], n), near[...], 1, 0)
     total = total + dg(picks(rows, core[0], n), far[...], 1, 0)
-    gup_all[...] = total.astype(BF16)
-    value = dg(latents[...], gup_all[...], 0, 0)
-    pack_rows(core[0], tall, (value * norm).astype(BF16), keep, give, 0, slabs, order)
+    gradient[...] = direct[...] + dg(total.astype(BF16), w_msg[0], 1, 1)
 
 
 def share_kernel(plan, *refs):
@@ -293,14 +308,6 @@
                     at += rows
 
 
-def tail_kernel(count, gradient1, grad_pre, grad_update, current, hidden, w_msg, w_in, w_out, gradient, final):
-    direct = gradient1[...] + dg(grad_pre[...], w_in[0, 0], 1, 1)
-    gradient[...] = direct + dg(grad_update[...], w_msg[0], 1, 1)
-    delta = dg(hidden[...], w_out[1], 1, 0)
-    live = alive_rows(count, current.shape[0])
-    final[...] = (current[...].astype(F32) + live * delta).astype(BF16)
-
-
 VMEM = pl.BlockSpec(memory_space=pltpu.VMEM)
 SMEM = pl.BlockSpec(memory_space=pltpu.SMEM)
 HBM = pl.BlockSpec(memory_space=pltpu.HBM)
@@ -368,6 +375,7 @@
         [pltpu.VMEM((GEO, n), F32), pltpu.SemaphoreType.DMA((5,))], 0.5, WHOLE,
     )(counts, core, rows, latents, positions, w_msg, w_in, *ready)
     near, far = trade(near, far)
+    ghost_near, ghost_far = near, far
 
     a_own, squares, columns, _, partial, pre_part = call(
         own_kernel, [SMEM] * 2 + [VMEM] * 4,
@@ -417,29 +425,27 @@
         turn_kernel, [SMEM] * 2 + [VMEM] * 11,
         [row_b, row_f, row_b, hid_b, row_b, halo_b, halo_b], [], 4,
     )(counts, core, rows, grad_own, near, far, direct, slope0, inverse, a_ghost, w_msg, w_in, w_out)
+    back_near, back_far = near, far
     near, far = trade(near, far)
 
-    out0 = terms(((plain, ((2, 4), (3, 4))), (swapped, ((5, 6), (0, 1)))), (in_rows, msg_rows + out_rows),
-                 (hidden0, grad_delta0, latents, message0, grad_pre0, current1, grad_update1))
-    (grad_own,) = call(flow0_kernel, [VMEM] * 2, [row_f], [], 2)(scaled0, a_own)
-    share_in0 = reduce_rows(*out0[:2], slabs, place, plain)
-    share_mix = reduce_rows(*out0[2:], slabs, place, swapped)
-
-    grad_update0, keep, give = call(
-        functools.partial(end_kernel, slabs, norm, plain), [SMEM] + [VMEM] * 5,
-        [row_b] + half(msg_rows), [w_out_b], 2,
-    )(core, rows, grad_own, near, far, latents)
-    share_msg0 = reduce_rows(keep, give, slabs, place, plain)
-
-    gradient, final = call(
-        tail_kernel, [SMEM] + [VMEM] * 8, [row_f, row_b], [], 4,
-    )(counts, gradient1, grad_pre0, grad_update0, current1, hidden1, w_msg, w_in, w_out)
-
-    plan = (((2, 1, 1),), ((1, 1, 2),), ((1, 0, 2),), ((0, 1, 1), (2, 0, 1)), ((0, 0, 1),))
+    in0 = terms(((plain, ((0, 2), (1, 2))),), (in_rows,), (latents, message0, grad_pre0))
+    grad_own, *mix0 = call(
+        functools.partial(mix_kernel, slabs, norm, swapped), [SMEM] + [VMEM] * 11,
+        [row_f] + half(2 * msg_rows + out_rows), [pltpu.VMEM((n, width), BF16), w_out_b], 5,
+    )(core, scaled0, a_own, latents, ghost_near, ghost_far, back_near, back_far,
+      current1, grad_update1, hidden0, grad_delta0)
+    direct, final = call(
+        rest_kernel, [SMEM] + [VMEM] * 6, [row_f, row_b], [], 3,
+    )(counts, gradient1, grad_pre0, current1, hidden1, w_in, w_out)
+    (gradient,) = call(end_kernel, [SMEM] + [VMEM] * 6, [row_f], [], 2)(core, rows, grad_own, near, far, direct, w_msg)
+    share_in0 = reduce_rows(*in0, slabs, place, plain)
+    share_mix = reduce_rows(*mix0, slabs, place, swapped)
+
+    plan = (((2, 1, 1),), ((1, 1, 2),), ((1, 0, 2),), ((0, 0, 1), (0, 1, 1), (2, 0, 1)))
     grad_msg, grad_in, grad_out = call(
         functools.partial(share_kernel, plan), [VMEM, SMEM, VMEM] * len(plan),
         [((2, msg_rows, width), F32), ((2, 2, msg_rows, hidden_width), F32), ((2, out_rows, width), F32)], [], 0.1,
-    )(*share_out1, *share_in1, *share_in0, *share_mix, *share_msg0)
+    )(*share_out1, *share_in1, *share_in0, *share_mix)
     return (final, gradient, grad_msg, grad_in, grad_out)
 
 

time: 131 us -> 138 us (1.053)
  waiting for transfers between devices: 32.4 us -> 45.4 us
  starting transfers between devices: 43.7 us -> 39.4 us
  Pallas kernels: 49.5 us -> 47.8 us
    ppermute x20 -> x16, waiting for transfers between devices: 32.4 us -> 45.3 us  [reduce_rows(): got = lax.ppermute(give, 'slab', [(i, i ^ 1 << bit) for i in range(slabs)])]
    ppermute x20 -> x16, starting transfers between devices: 29.9 us -> 25.6 us  [reduce_rows(): got = lax.ppermute(give, 'slab', [(i, i ^ 1 << bit) for i in range(slabs)])]
    pallas_call x14, Pallas kernels: 49.5 us -> 47.8 us  [run(): pl.pallas_call(kernel, in_specs=where, out_specs=[VMEM] * len(outs), out_...]
  transfers between devices with their start and end apart: 28 -> 24, of which waited for: 8 -> 10; matrix products, arithmetic and copies ran while one was open for 2% -> 2% of each run, Pallas kernels for 25% -> 24%
where the time goes in v3:
time: 138 us
  Pallas kernels  47.8 us (35%)
  waiting for transfers between devices  45.4 us (33%)
  starting transfers between devices  39.4 us (29%)
  other arithmetic  1.85 us (1%)
  local copies, waits for them, and re-layouts  1.74 us (1%)
  between operations  1.71 us (1%)
    pallas_call x14, Pallas kernels, run(): pl.pallas_call(kernel, in_specs=where, out_specs=[VMEM] * len(outs), out_...  47.8 us
    ppermute x16, waiting for transfers between devices, reduce_rows(): got = lax.ppermute(give, 'slab', [(i, i ^ 1 << bit) for i in range(slabs)])  45.3 us
    ppermute x16, starting transfers between devices, reduce_rows(): got = lax.ppermute(give, 'slab', [(i, i ^ 1 << bit) for i in range(slabs)])  25.6 us
    ppermute x4, starting transfers between devices, trade(): near = lax.ppermute(near, 'slab', near_pairs)  10.5 us
    ppermute x4, starting transfers between devices, trade(): far = lax.ppermute(far, 'slab', far_pairs)  3.32 us
  transfers between devices with their start and end apart: 24, of which 10 were waited for; matrix products, arithmetic and copies ran while one was open for 2% of the time, Pallas kernels for 24%

profile of v3, /device:TPU:0, one launch (start us, length us, event | category | flops | bytes accessed | tf_op | source)
XLA Modules:
  0.0 137.9 jit_solution(3522347462253652156)
XLA Ops:
  2.7 2.2 %shard_map.128 = (bf16[272,512]{1,0:T(8,128)(2,1)S(1)}, bf16[272,512]{1,0:T(8,128)(2,1)S(1)}, s32[2,256]{1,0:T(2,128)S(1)}, bf16[1024,512]{1,0:T(8,128)(2,1)S(1)...) custom-call(s32[1]{0:T(128)S(6)} %copy.18.count, s32[1]{0:T(128)} %bitcast.core, ...), custom_call_target="tpu_custom_call" | custom-call | flops 500000000 | bytes 1000000 | tf_op jit(solution)/shard_map/pallas_call | solution.py:318
  6.2 7.4 %shard_map.129 = (bf16[1024,1024]{1,0:T(8,128)(2,1)S(1)}, f32[1024,128]{1,0:T(8,128)S(1)}, f32[1024,128]{1,0:T(8,128)S(1)}, bf16[1024,512]{1,0:T(8,128)(2,1)}, f...) custom-call(s32[1]{0:T(128)S(6)} %copy.18.count, s32[1,4,8]{2,1,0:T(4,128)S(1)} %bitcast.74, ...), custom_call_target="tpu_custom_call" | custom-call | flops 5000000000 | bytes 10000000 | tf_op jit(solution)/shard_map/pallas_call | solution.py:318
  13.6 7.0 %shard_map.130 = (bf16[1024,512]{1,0:T(8,128)(2,1)S(1)}, f32[1024,128]{1,0:T(8,128)S(1)}, bf16[1024,512]{1,0:T(8,128)(2,1)S(1)}, bf16[1024,1024]{1,0:T(8,128)(2,...) custom-call(s32[1]{0:T(128)S(6)} %copy.18.count, ...), custom_call_target="tpu_custom_call" | custom-call | flops 5000000000 | bytes 10000000 | tf_op jit(solution)/shard_map/pallas_call | solution.py:318
  20.6 3.9 %collective-permute-start.2 = (bf16[256,512]{1,0:T(8,128)(2,1)S(1)}, bf16[256,512]{1,0:T(8,128)(2,1)S(1)}, u32[]{:S(2)}, u32[]{:S(2)}) collective-permute-start(bf16[256,512]{1,0:T(8,128)(2,1)S(1)} %get-tuple-element.70), channel_id=1, source_target_pairs={{0,1},{1,0},{2,3},{3,2},{4,5},{5,4},{6,7},{7,6},{8,9},{9,8},{10,11... | collective-permute-start | bytes 786440 | tf_op jit(solution)/shard_map/ppermute | solution.py:362
  25.5 3.4 %shard_map.131 = (f32[1024,512]{1,0:T(8,128)S(1)}, bf16[1024,1024]{1,0:T(8,128)(2,1)S(1)}, bf16[1024,512]{1,0:T(8,128)(2,1)S(1)}, bf16[1024,1024]{1,0:T(8,128)(2,1)S(1)}) custom-call(s32[1]{0:T(128)S(6)} %copy.18.count, bf16[1024,512]{1,0:T(8,128)(2,1)S(1)} %get-tuple-element.74.current.later.refs_0_, bf16[1024,512]{1,0:T(8,128)(2,1)S(1)} %get-tuple-element.75.update, ...), custom_call_target="tpu_custom_call" | custom-call | flops 3000000000 | bytes 6000000 | tf_op jit(solution)/shard_map/pallas_call | solution.py:318
  28.9 4.3 %shard_map.132 = (bf16[1024,512]{1,0:T(8,128)(2,1)S(1)}, bf16[1024,1024]{1,0:T(8,128)(2,1)S(1)}, bf16[1024,1024]{1,0:T(8,128)(2,1)S(1)}, bf16[1024,512]{1,0:T(8,...) custom-call(bf16[256,512]{1,0:T(8,128)(2,1)S(1)} %collective-permute-done.2.near, ...), custom_call_target="tpu_custom_call" | custom-call | flops 4000000000 | bytes 8000000 | tf_op jit(solution)/shard_map/pallas_call | solution.py:318
  33.2 5.4 %collective-permute-start.4 = (bf16[256,512]{1,0:T(8,128)(2,1)S(1)}, bf16[256,512]{1,0:T(8,128)(2,1)S(1)}, u32[]{:S(2)}, u32[]{:S(2)}) collective-permute-start(bf16[256,512]{1,0:T(8,128)(2,1)S(1)} %get-tuple-element.83), channel_id=1, source_target_pairs={{0,1},{1,0},{2,3},{3,2},{4,5},{5,4},{6,7},{7,6},{8,9},{9,8},{10,11... | collective-permute-start | bytes 786440 | tf_op jit(solution)/shard_map/ppermute | solution.py:362
  40.8 3.8 %collective-permute-start.8 = (bf16[8,64,512]{2,1,0:T(8,128)(2,1)S(1)}, bf16[8,64,512]{2,1,0:T(8,128)(2,1)S(1)}, u32[]{:S(2)}, u32[]{:S(2)}) collective-permute-start(bf16[8,64,512]{2,1,0:T(8,128)(2,1)S(1)} %get-tuple-element.101), channel_id=1, source_target_pairs={{0,1},{1,0},{2,3},{3,2},{4,5},{5,4},{6,7},{7,6},{8,9},{9,8},{10,11... | collective-permute-start | bytes 1572872 | tf_op jit(solution)/shard_map/ppermute | solution.py:340
  44.6 2.5 %shard_map.139 = (bf16[8,128,512]{2,1,0:T(8,128)(2,1)S(1)}, bf16[8,128,512]{2,1,0:T(8,128)(2,1)S(1)}) custom-call(s32[1]{0:T(128)} %bitcast.core, bf16[1024,512]{1,0:T(8,128)(2,1)S(1)} %get-tuple-element.74.current.later.refs_0_, bf16[1024,512]{1,0:T(8,128)(2,1)S(1)} %get-tuple-element.102.refs_1_, bf16[1024,1024]{1,0:T(8,128)(2,1)S(1)} %get-tuple-element.80.grad_pre.refs_2_), custom_call_target="tpu_custom_call" | custom-call | flops 4000000000 | bytes 8000000 | tf_op jit(solution)/shard_map/pallas_call | solution.py:318
  47.2 2.4 %shard_map.133 = (f32[1024,512]{1,0:T(8,128)S(1)}, f32[1024,512]{1,0:T(8,128)S(1)}) custom-call(bf16[1024,1024]{1,0:T(8,128)(2,1)S(1)} %get-tuple-element.80.grad_pre.refs_2_, bf16[1024,512]{1,0:T(8,128)(2,1)S(1)} %get-tuple-element.81.scaled, bf16[1024,1024]{1,0:T(8,128)(2,1)S(1)} %get-tuple-element.76.a_own, bf16[1024,512]{1,0:T(8,128)(2,1)S(1)} %copy-done.3, ...), custom_call_target="tpu_custom_call" | custom-call | flops 3000000000 | bytes 6000000 | tf_op jit(solution)/shard_map/pallas_call | solution.py:318
  49.6 4.1 %shard_map.134 = (bf16[1024,512]{1,0:T(8,128)(2,1)S(1)}, f32[1024,512]{1,0:T(8,128)S(1)}, bf16[1024,512]{1,0:T(8,128)(2,1)S(1)}, bf16[1024,1024]{1,0:T(8,128)(2,...) custom-call(s32[1]{0:T(128)S(6)} %copy.18.count, s32[1]{0:T(128)} %bitcast.core, ...), custom_call_target="tpu_custom_call" | custom-call | flops 4000000000 | bytes 8000000 | tf_op jit(solution)/shard_map/pallas_call | solution.py:318
  55.2 3.9 %shard_map.136 = (f32[1024,512]{1,0:T(8,128)S(1)}, bf16[8,128,512]{2,1,0:T(8,128)(2,1)S(1)}, bf16[8,128,512]{2,1,0:T(8,128)(2,1)S(1)}) custom-call(s32[1]{0:T(128)} %bitcast.core, bf16[1024,512]{1,0:T(8,128)(2,1)S(1)} %get-tuple-element.91.scaled, bf16[1024,1024]{1,0:T(8,128)(2,1)S(1)} %get-tuple-element.76.a_own, ...), custom_call_target="tpu_custom_call" | custom-call | flops 5000000000 | bytes 10000000 | tf_op jit(solution)/shard_map/pallas_call | solution.py:318
  59.0 3.3 %collective-permute-start.20 = (bf16[8,128,512]{2,1,0:T(8,128)(2,1)S(1)}, bf16[8,128,512]{2,1,0:T(8,128)(2,1)S(1)}, u32[]{:S(2)}, u32[]{:S(2)}) collective-permute-start(bf16[8,128,512]{2,1,0:T(8,128)(2,1)S(1)} %get-tuple-element.109), channel_id=1, source_target_pairs={{0,1},{1,0},{2,3},{3,2},{4,5},{5,4},{6,7},{7,6},{8,9},{9,8},{10,11... | collective-permute-start | bytes 3145736 | tf_op jit(solution)/shard_map/ppermute | solution.py:340
  63.9 2.5 %shard_map.140 = (bf16[8,128,512]{2,1,0:T(8,128)(2,1)S(1)}, bf16[8,128,512]{2,1,0:T(8,128)(2,1)S(1)}) custom-call(s32[1]{0:T(128)} %bitcast.core, bf16[1024,512]{1,0:T(8,128)(2,1)S(1)} %get-tuple-element.60.latents.refs_0_, bf16[1024,512]{1,0:T(8,128)(2,1)S(1)} %get-tuple-element.105.refs_1_, bf16[1024,1024]{1,0:T(8,128)(2,1)S(1)} %get-tuple-element.88.grad_pre.refs_2_), custom_call_target="tpu_custom_call" | custom-call | flops 4000000000 | bytes 8000000 | tf_op jit(solution)/shard_map/pallas_call | solution.py:318
  66.4 4.3 %collective-permute-done.9 = bf16[4,64,512]{2,1,0:T(8,128)(2,1)S(1)} collective-permute-done((bf16[4,64,512]{2,1,0:T(8,128)(2,1)S(1)}, bf16[4,64,512]{2,1,0:T(8,128)(2,1)S(1)}, u32[]{:S(2)}, u32[]{:S(2)}) %collective-permute-start.9) | collective-permute-done | bytes 262176 | tf_op jit(solution)/shard_map/ppermute | solution.py:340
  70.9 1.8 %collective-permute-start.10 = (bf16[2,64,512]{2,1,0:T(8,128)(2,1)S(1)}, bf16[2,64,512]{2,1,0:T(8,128)(2,1)S(1)}, u32[]{:S(2)}, u32[]{:S(2)}) collective-permute-start(bf16[2,64,512]{2,1,0:T(8,128)(2,1)S(1)} %dynamic-slice_bitcast_fusion.7), channel_id=1, source_target_pairs={{0,4},{1,5},{2,6},{3,7},{4,0},{5,1},{6,2},{7,3},{8,12},{9,13},{10,... | collective-permute-start | bytes 393224 | tf_op jit(solution)/shard_map/ppermute | solution.py:340
  72.6 3.4 %shard_map.135 = (f32[1024,512]{1,0:T(8,128)S(1)}, bf16[1024,512]{1,0:T(8,128)(2,1)}) custom-call(s32[1]{0:T(128)S(6)} %copy.18.count, f32[1024,512]{1,0:T(8,128)S(1)} %get-tuple-element.87.gradient1, bf16[1024,1024]{1,0:T(8,128)(2,1)S(1)} %get-tuple-element.88.grad_pre.refs_2_, bf16[1024,512]{1,0:T(8,128)(2,1)S(1)} %get-tuple-element.74.current.later.refs_0_, ...), custom_call_target="tpu_custom_call" | custom-call | flops 3000000000 | bytes 6000000 | tf_op jit(solution)/shard_map/pallas_call | solution.py:318
  76.1 2.8 %collective-permute-start.11 = (bf16[1,64,512]{2,1,0:T(8,128)(2,1)S(1)}, bf16[1,64,512]{2,1,0:T(8,128)(2,1)S(1)}, u32[]{:S(2)}, u32[]{:S(2)}) collective-permute-start(bf16[1,64,512]{2,1,0:T(8,128)(2,1)S(1)} %constant_dynamic-slice_fusion.3), channel_id=1, source_target_pairs={{0,8},{1,9},{2,10},{3,11},{4,12},{5,13},{6,14},{7,15},{8,0},{9,1},... | collective-permute-start | bytes 196616 | tf_op jit(solution)/shard_map/ppermute | solution.py:340
  79.3 1.8 %collective-permute-start.13 = (bf16[4,128,512]{2,1,0:T(8,128)(2,1)S(1)}, bf16[4,128,512]{2,1,0:T(8,128)(2,1)S(1)}, u32[]{:S(2)}, u32[]{:S(2)}) collective-permute-start(bf16[4,128,512]{2,1,0:T(8,128)(2,1)S(1)} %dynamic-slice_bitcast_fusion.2), channel_id=1, source_target_pairs={{0,4},{1,5},{2,6},{3,7},{4,0},{5,1},{6,2},{7,3},{8,12},{9,13},{10,... | collective-permute-start | bytes 1572872 | tf_op jit(solution)/shard_map/ppermute | solution.py:340
  82.2 12.1 %collective-permute-done.13 = bf16[4,128,512]{2,1,0:T(8,128)(2,1)S(1)} collective-permute-done((bf16[4,128,512]{2,1,0:T(8,128)(2,1)S(1)}, bf16[4,128,512]{2,1,0:T(8,128)(2,1)S(1)}, u32[]{:S(2)}, u32[]{:S(2)}) %collective-permute-start.13) | collective-permute-done | bytes 524320 | tf_op jit(solution)/shard_map/ppermute | solution.py:340
  95.6 9.2 %collective-permute-done.21 = bf16[4,128,512]{2,1,0:T(8,128)(2,1)S(1)} collective-permute-done((bf16[4,128,512]{2,1,0:T(8,128)(2,1)S(1)}, bf16[4,128,512]{2,1,0:T(8,128)(2,1)S(1)}, u32[]{:S(2)}, u32[]{:S(2)}) %collective-permute-start.21) | collective-permute-done | bytes 524320 | tf_op jit(solution)/shard_map/ppermute | solution.py:340
  106.8 1.5 %collective-permute-start.22 = (bf16[2,128,512]{2,1,0:T(8,128)(2,1)S(1)}, bf16[2,128,512]{2,1,0:T(8,128)(2,1)S(1)}, u32[]{:S(2)}, u32[]{:S(2)}) collective-permute-start(bf16[2,128,512]{2,1,0:T(8,128)(2,1)S(1)} %dynamic-slice_bitcast_fusion.3), channel_id=1, source_target_pairs={{0,2},{1,3},{2,0},{3,1},{4,6},{5,7},{6,4},{7,5},{8,10},{9,11},{10,... | collective-permute-start | bytes 786440 | tf_op jit(solution)/shard_map/ppermute | solution.py:340
  108.5 5.5 %collective-permute-done.14 = bf16[2,128,512]{2,1,0:T(8,128)(2,1)S(1)} collective-permute-done((bf16[2,128,512]{2,1,0:T(8,128)(2,1)S(1)}, bf16[2,128,512]{2,1,0:T(8,128)(2,1)S(1)}, u32[]{:S(2)}, u32[]{:S(2)}) %collective-permute-start.14) | collective-permute-done | bytes 262176 | tf_op jit(solution)/shard_map/ppermute | solution.py:340
  113.9 1.6 %collective-permute-start.18 = (bf16[2,128,512]{2,1,0:T(8,128)(2,1)S(1)}, bf16[2,128,512]{2,1,0:T(8,128)(2,1)S(1)}, u32[]{:S(2)}, u32[]{:S(2)}) collective-permute-start(bf16[2,128,512]{2,1,0:T(8,128)(2,1)S(1)} %dynamic-slice_bitcast_fusion.4), channel_id=1, source_target_pairs={{0,4},{1,5},{2,6},{3,7},{4,0},{5,1},{6,2},{7,3},{8,12},{9,13},{10,... | collective-permute-start | bytes 786440 | tf_op jit(solution)/shard_map/ppermute | solution.py:340
  115.7 2.3 %collective-permute-done.22 = bf16[2,128,512]{2,1,0:T(8,128)(2,1)S(1)} collective-permute-done((bf16[2,128,512]{2,1,0:T(8,128)(2,1)S(1)}, bf16[2,128,512]{2,1,0:T(8,128)(2,1)S(1)}, u32[]{:S(2)}, u32[]{:S(2)}) %collective-permute-start.22) | collective-permute-done | bytes 262176 | tf_op jit(solution)/shard_map/ppermute | solution.py:340
  118.0 1.7 %collective-permute-start.15 = (bf16[1,128,512]{2,1,0:T(8,128)(2,1)S(1)}, bf16[1,128,512]{2,1,0:T(8,128)(2,1)S(1)}, u32[]{:S(2)}, u32[]{:S(2)}) collective-permute-start(bf16[1,128,512]{2,1,0:T(8,128)(2,1)S(1)} %constant_dynamic-slice_fusion.2), channel_id=1, source_target_pairs={{0,8},{1,9},{2,10},{3,11},{4,12},{5,13},{6,14},{7,15},{8,0},{9,1},... | collective-permute-start | bytes 393224 | tf_op jit(solution)/shard_map/ppermute | solution.py:340
  119.8 1.6 %collective-permute-done.18 = bf16[2,128,512]{2,1,0:T(8,128)(2,1)S(1)} collective-permute-done((bf16[2,128,512]{2,1,0:T(8,128)(2,1)S(1)}, bf16[2,128,512]{2,1,0:T(8,128)(2,1)S(1)}, u32[]{:S(2)}, u32[]{:S(2)}) %collective-permute-start.18) | collective-permute-done | bytes 262176 | tf_op jit(solution)/shard_map/ppermute | solution.py:340
  121.8 2.7 %collective-permute-start.19 = (bf16[1,128,512]{2,1,0:T(8,128)(2,1)S(1)}, bf16[1,128,512]{2,1,0:T(8,128)(2,1)S(1)}, u32[]{:S(2)}, u32[]{:S(2)}) collective-permute-start(bf16[1,128,512]{2,1,0:T(8,128)(2,1)S(1)} %constant_dynamic-slice_fusion.1), channel_id=1, source_target_pairs={{0,8},{1,9},{2,10},{3,11},{4,12},{5,13},{6,14},{7,15},{8,0},{9,1},... | collective-permute-start | bytes 393224 | tf_op jit(solution)/shard_map/ppermute | solution.py:340
  124.5 2.6 %shard_map.137 = f32[1024,512]{1,0:T(8,128)} custom-call(s32[1]{0:T(128)} %bitcast.core, s32[2,256]{1,0:T(2,128)S(1)} %get-tuple-element.59.rows, f32[1024,512]{1,0:T(8,128)S(1)} %get-tuple-element.97.grad_own, bf16[256,512]{1,0:T(8,128)(2,1)S(1)} %collective-permute-done.6.near, bf16[256,512]{1,0:T(8,128)(2,1)S(1)} %collective-permute-done.7.far, ...), custom_call_target="tpu_custom_call" | custom-call | flops 2000000000 | bytes 4000000 | tf_op jit(solution)/shard_map/pallas_call | solution.py:318
  127.1 5.3 %collective-permute-done.15.refs_5_ = bf16[1,128,512]{2,1,0:T(8,128)(2,1)S(1)} collective-permute-done((bf16[1,128,512]{2,1,0:T(8,128)(2,1)S(1)}, bf16[1,128,512]{2,1,0:T(8,128)(2,1)S(1)}, u32[]{:S(2)}, u32[]{:S(2)}) %collective-permute-start.15) | collective-permute-done | bytes 131104 | tf_op jit(solution)/shard_map/ppermute | solution.py:340
  132.4 2.8 %collective-permute-done.23.refs_11_ = bf16[1,128,512]{2,1,0:T(8,128)(2,1)S(1)} collective-permute-done((bf16[1,128,512]{2,1,0:T(8,128)(2,1)S(1)}, bf16[1,128,512]{2,1,0:T(8,128)(2,1)S(1)}, u32[]{:S(2)}, u32[]{:S(2)}) %collective-permute-start.23) | collective-permute-done | bytes 131104 | tf_op jit(solution)/shard_map/ppermute | solution.py:340
  135.2 1.7 %collective-permute-done.19.refs_8_ = bf16[1,128,512]{2,1,0:T(8,128)(2,1)S(1)} collective-permute-done((bf16[1,128,512]{2,1,0:T(8,128)(2,1)S(1)}, bf16[1,128,512]{2,1,0:T(8,128)(2,1)S(1)}, u32[]{:S(2)}, u32[]{:S(2)}) %collective-permute-start.19) | collective-permute-done | bytes 131104 | tf_op jit(solution)/shard_map/ppermute | solution.py:340
  (68 shorter events, 15.5 us)
Async XLA Ops:
  1.3 0.7 copy-start.4
  2.0 0.7 copy-start.5
  2.7 3.5 %copy-start.6 = (s32[1,8,4]{1,2,0:T(4,128)S(1)}, s32[1,8,4]{1,2,0:T(4,128)}, u32[]{:S(2)}) copy-start(s32[1,8,4]{1,2,0:T(4,128)} %param.13) | copy-start | bytes 388
  4.9 8.6 %collective-permute-start = (bf16[272,512]{1,0:T(8,128)(2,1)S(1)}, bf16[272,512]{1,0:T(8,128)(2,1)S(1)}, u32[]{:S(2)}, u32[]{:S(2)}) collective-permute-start(bf16[272,512]{1,0:T(8,128)(2,1)S(1)} %get-tuple-element.61), channel_id=1, source_target_pairs={{0,1},{1,0},{2,3},{3,2},{4,5},{5,4},{6,7},{7,6},{8,9},{9,8},{10,11... | collective-permute-start | bytes 835592 | tf_op jit(solution)/shard_map/ppermute | solution.py:362
  5.5 8.1 %collective-permute-start.1 = (bf16[272,512]{1,0:T(8,128)(2,1)S(1)}, bf16[272,512]{1,0:T(8,128)(2,1)S(1)}, u32[]{:S(2)}, u32[]{:S(2)}) collective-permute-start(bf16[272,512]{1,0:T(8,128)(2,1)S(1)} %get-tuple-element.62), channel_id=1, source_target_pairs={{1,2},{2,1},{3,4},{4,3},{5,6},{6,5},{7,8},{8,7},{9,10},{10,9},{11,... | collective-permute-start | bytes 835592 | tf_op jit(solution)/shard_map/ppermute | solution.py:361
  6.2 7.4 %copy-start = (bf16[2,2,512,1024]{3,2,1,0:T(8,128)(2,1)S(1)}, bf16[2,2,512,1024]{3,2,1,0:T(8,128)(2,1)}, u32[]{:S(2)}) copy-start(bf16[2,2,512,1024]{3,2,1,0:T(8,128)(2,1)} %w_in.13) | copy-start | bytes 12582916
  6.2 7.4 %copy-start.1 = (bf16[2,1024,512]{2,1,0:T(8,128)(2,1)S(1)}, bf16[2,1024,512]{2,1,0:T(8,128)(2,1)}, u32[]{:S(2)}) copy-start(bf16[2,1024,512]{2,1,0:T(8,128)(2,1)} %w_out.7) | copy-start | bytes 6291460
  6.2 7.4 %copy-start.2 = (bf16[2,512,512]{2,1,0:T(8,128)(2,1)S(1)}, bf16[2,512,512]{2,1,0:T(8,128)(2,1)}, u32[]{:S(2)}) copy-start(bf16[2,512,512]{2,1,0:T(8,128)(2,1)} %w_msg.7) | copy-start | bytes 3145732
  13.6 11.8 %copy-start.3 = (bf16[1024,512]{1,0:T(8,128)(2,1)S(1)}, bf16[1024,512]{1,0:T(8,128)(2,1)}, u32[]{:S(2)}) copy-start(bf16[1024,512]{1,0:T(8,128)(2,1)} %cot.3) | copy-start | bytes 3145732
  20.6 8.2 %collective-permute-start.2 = (bf16[256,512]{1,0:T(8,128)(2,1)S(1)}, bf16[256,512]{1,0:T(8,128)(2,1)S(1)}, u32[]{:S(2)}, u32[]{:S(2)}) collective-permute-start(bf16[256,512]{1,0:T(8,128)(2,1)S(1)} %get-tuple-element.70), channel_id=1, source_target_pairs={{0,1},{1,0},{2,3},{3,2},{4,5},{5,4},{6,7},{7,6},{8,9},{9,8},{10,11... | collective-permute-start | bytes 786440 | tf_op jit(solution)/shard_map/ppermute | solution.py:362
  24.6 4.3 %collective-permute-start.3 = (bf16[256,512]{1,0:T(8,128)(2,1)S(1)}, bf16[256,512]{1,0:T(8,128)(2,1)S(1)}, u32[]{:S(2)}, u32[]{:S(2)}) collective-permute-start(bf16[256,512]{1,0:T(8,128)(2,1)S(1)} %get-tuple-element.71), channel_id=1, source_target_pairs={{1,2},{2,1},{3,4},{4,3},{5,6},{6,5},{7,8},{8,7},{9,10},{10,9},{11,... | collective-permute-start | bytes 786440 | tf_op jit(solution)/shard_map/ppermute | solution.py:361
  33.2 16.4 %collective-permute-start.4 = (bf16[256,512]{1,0:T(8,128)(2,1)S(1)}, bf16[256,512]{1,0:T(8,128)(2,1)S(1)}, u32[]{:S(2)}, u32[]{:S(2)}) collective-permute-start(bf16[256,512]{1,0:T(8,128)(2,1)S(1)} %get-tuple-element.83), channel_id=1, source_target_pairs={{0,1},{1,0},{2,3},{3,2},{4,5},{5,4},{6,7},{7,6},{8,9},{9,8},{10,11... | collective-permute-start | bytes 786440 | tf_op jit(solution)/shard_map/ppermute | solution.py:362
  38.6 11.0 %collective-permute-start.5 = (bf16[256,512]{1,0:T(8,128)(2,1)S(1)}, bf16[256,512]{1,0:T(8,128)(2,1)S(1)}, u32[]{:S(2)}, u32[]{:S(2)}) collective-permute-start(bf16[256,512]{1,0:T(8,128)(2,1)S(1)} %get-tuple-element.84), channel_id=1, source_target_pairs={{1,2},{2,1},{3,4},{4,3},{5,6},{6,5},{7,8},{8,7},{9,10},{10,9},{11,... | collective-permute-start | bytes 786440 | tf_op jit(solution)/shard_map/ppermute | solution.py:361
  40.8 21.5 %collective-permute-start.8 = (bf16[8,64,512]{2,1,0:T(8,128)(2,1)S(1)}, bf16[8,64,512]{2,1,0:T(8,128)(2,1)S(1)}, u32[]{:S(2)}, u32[]{:S(2)}) collective-permute-start(bf16[8,64,512]{2,1,0:T(8,128)(2,1)S(1)} %get-tuple-element.101), channel_id=1, source_target_pairs={{0,1},{1,0},{2,3},{3,2},{4,5},{5,4},{6,7},{7,6},{8,9},{9,8},{10,11... | collective-permute-start | bytes 1572872 | tf_op jit(solution)/shard_map/ppermute | solution.py:340
  47.1 29.0 %collective-permute-start.12 = (bf16[8,128,512]{2,1,0:T(8,128)(2,1)S(1)}, bf16[8,128,512]{2,1,0:T(8,128)(2,1)S(1)}, u32[]{:S(2)}, u32[]{:S(2)}) collective-permute-start(bf16[8,128,512]{2,1,0:T(8,128)(2,1)S(1)} %get-tuple-element.104), channel_id=1, source_target_pairs={{0,1},{1,0},{2,3},{3,2},{4,5},{5,4},{6,7},{7,6},{8,9},{9,8},{10,11... | collective-permute-start | bytes 3145736 | tf_op jit(solution)/shard_map/ppermute | solution.py:340
  53.7 68.1 %collective-permute-start.6 = (bf16[256,512]{1,0:T(8,128)(2,1)S(1)}, bf16[256,512]{1,0:T(8,128)(2,1)S(1)}, u32[]{:S(2)}, u32[]{:S(2)}) collective-permute-start(bf16[256,512]{1,0:T(8,128)(2,1)S(1)} %get-tuple-element.92.back_near), channel_id=1, source_target_pairs={{0,1},{1,0},{2,3},{3,2},{4,5},{5,4},{6,7},{7,6},{8,9},{9,8},{10,11... | collective-permute-start | bytes 786440 | tf_op jit(solution)/shard_map/ppermute | solution.py:362
  54.2 70.3 %collective-permute-start.7 = (bf16[256,512]{1,0:T(8,128)(2,1)S(1)}, bf16[256,512]{1,0:T(8,128)(2,1)S(1)}, u32[]{:S(2)}, u32[]{:S(2)}) collective-permute-start(bf16[256,512]{1,0:T(8,128)(2,1)S(1)} %get-tuple-element.93.back_far), channel_id=1, source_target_pairs={{1,2},{2,1},{3,4},{4,3},{5,6},{6,5},{7,8},{8,7},{9,10},{10,9},{11,... | collective-permute-start | bytes 786440 | tf_op jit(solution)/shard_map/ppermute | solution.py:361
  59.0 20.2 %collective-permute-start.20 = (bf16[8,128,512]{2,1,0:T(8,128)(2,1)S(1)}, bf16[8,128,512]{2,1,0:T(8,128)(2,1)S(1)}, u32[]{:S(2)}, u32[]{:S(2)}) collective-permute-start(bf16[8,128,512]{2,1,0:T(8,128)(2,1)S(1)} %get-tuple-element.109), channel_id=1, source_target_pairs={{0,1},{1,0},{2,3},{3,2},{4,5},{5,4},{6,7},{7,6},{8,9},{9,8},{10,11... | collective-permute-start | bytes 3145736 | tf_op jit(solution)/shard_map/ppermute | solution.py:340
  62.5 8.3 %collective-permute-start.9 = (bf16[4,64,512]{2,1,0:T(8,128)(2,1)S(1)}, bf16[4,64,512]{2,1,0:T(8,128)(2,1)S(1)}, u32[]{:S(2)}, u32[]{:S(2)}) collective-permute-start(bf16[4,64,512]{2,1,0:T(8,128)(2,1)S(1)} %dynamic-slice_bitcast_fusion.6), channel_id=1, source_target_pairs={{0,2},{1,3},{2,0},{3,1},{4,6},{5,7},{6,4},{7,5},{8,10},{9,11},{10,... | collective-permute-start | bytes 786440 | tf_op jit(solution)/shard_map/ppermute | solution.py:340
  70.9 5.1 %collective-permute-start.10 = (bf16[2,64,512]{2,1,0:T(8,128)(2,1)S(1)}, bf16[2,64,512]{2,1,0:T(8,128)(2,1)S(1)}, u32[]{:S(2)}, u32[]{:S(2)}) collective-permute-start(bf16[2,64,512]{2,1,0:T(8,128)(2,1)S(1)} %dynamic-slice_bitcast_fusion.7), channel_id=1, source_target_pairs={{0,4},{1,5},{2,6},{3,7},{4,0},{5,1},{6,2},{7,3},{8,12},{9,13},{10,... | collective-permute-start | bytes 393224 | tf_op jit(solution)/shard_map/ppermute | solution.py:340
  76.0 5.4 %collective-permute-start.16 = (bf16[8,128,512]{2,1,0:T(8,128)(2,1)S(1)}, bf16[8,128,512]{2,1,0:T(8,128)(2,1)S(1)}, u32[]{:S(2)}, u32[]{:S(2)}) collective-permute-start(bf16[8,128,512]{2,1,0:T(8,128)(2,1)S(1)} %get-tuple-element.107), channel_id=1, source_target_pairs={{0,1},{1,0},{2,3},{3,2},{4,5},{5,4},{6,7},{7,6},{8,9},{9,8},{10,11... | collective-permute-start | bytes 3145736 | tf_op jit(solution)/shard_map/ppermute | solution.py:340
  76.1 51.0 %collective-permute-start.11 = (bf16[1,64,512]{2,1,0:T(8,128)(2,1)S(1)}, bf16[1,64,512]{2,1,0:T(8,128)(2,1)S(1)}, u32[]{:S(2)}, u32[]{:S(2)}) collective-permute-start(bf16[1,64,512]{2,1,0:T(8,128)(2,1)S(1)} %constant_dynamic-slice_fusion.3), channel_id=1, source_target_pairs={{0,8},{1,9},{2,10},{3,11},{4,12},{5,13},{6,14},{7,15},{8,0},{9,1},... | collective-permute-start | bytes 196616 | tf_op jit(solution)/shard_map/ppermute | solution.py:340
  79.3 14.9 %collective-permute-start.13 = (bf16[4,128,512]{2,1,0:T(8,128)(2,1)S(1)}, bf16[4,128,512]{2,1,0:T(8,128)(2,1)S(1)}, u32[]{:S(2)}, u32[]{:S(2)}) collective-permute-start(bf16[4,128,512]{2,1,0:T(8,128)(2,1)S(1)} %dynamic-slice_bitcast_fusion.2), channel_id=1, source_target_pairs={{0,4},{1,5},{2,6},{3,7},{4,0},{5,1},{6,2},{7,3},{8,12},{9,13},{10,... | collective-permute-start | bytes 1572872 | tf_op jit(solution)/shard_map/ppermute | solution.py:340
  81.5 23.3 %collective-permute-start.21 = (bf16[4,128,512]{2,1,0:T(8,128)(2,1)S(1)}, bf16[4,128,512]{2,1,0:T(8,128)(2,1)S(1)}, u32[]{:S(2)}, u32[]{:S(2)}) collective-permute-start(bf16[4,128,512]{2,1,0:T(8,128)(2,1)S(1)} %dynamic-slice_bitcast_fusion), channel_id=1, source_target_pairs={{0,4},{1,5},{2,6},{3,7},{4,0},{5,1},{6,2},{7,3},{8,12},{9,13},{10,... | collective-permute-start | bytes 1572872 | tf_op jit(solution)/shard_map/ppermute | solution.py:340
  94.2 12.6 %collective-permute-start.17 = (bf16[4,128,512]{2,1,0:T(8,128)(2,1)S(1)}, bf16[4,128,512]{2,1,0:T(8,128)(2,1)S(1)}, u32[]{:S(2)}, u32[]{:S(2)}) collective-permute-start(bf16[4,128,512]{2,1,0:T(8,128)(2,1)S(1)} %dynamic-slice_bitcast_fusion.1), channel_id=1, source_target_pairs={{0,2},{1,3},{2,0},{3,1},{4,6},{5,7},{6,4},{7,5},{8,10},{9,11},{10,... | collective-permute-start | bytes 1572872 | tf_op jit(solution)/shard_map/ppermute | solution.py:340
  104.8 9.2 %collective-permute-start.14 = (bf16[2,128,512]{2,1,0:T(8,128)(2,1)S(1)}, bf16[2,128,512]{2,1,0:T(8,128)(2,1)S(1)}, u32[]{:S(2)}, u32[]{:S(2)}) collective-permute-start(bf16[2,128,512]{2,1,0:T(8,128)(2,1)S(1)} %dynamic-slice_bitcast_fusion.5), channel_id=1, source_target_pairs={{0,2},{1,3},{2,0},{3,1},{4,6},{5,7},{6,4},{7,5},{8,10},{9,11},{10,... | collective-permute-start | bytes 786440 | tf_op jit(solution)/shard_map/ppermute | solution.py:340
  106.8 11.2 %collective-permute-start.22 = (bf16[2,128,512]{2,1,0:T(8,128)(2,1)S(1)}, bf16[2,128,512]{2,1,0:T(8,128)(2,1)S(1)}, u32[]{:S(2)}, u32[]{:S(2)}) collective-permute-start(bf16[2,128,512]{2,1,0:T(8,128)(2,1)S(1)} %dynamic-slice_bitcast_fusion.3), channel_id=1, source_target_pairs={{0,2},{1,3},{2,0},{3,1},{4,6},{5,7},{6,4},{7,5},{8,10},{9,11},{10,... | collective-permute-start | bytes 786440 | tf_op jit(solution)/shard_map/ppermute | solution.py:340
  113.9 7.4 %collective-permute-start.18 = (bf16[2,128,512]{2,1,0:T(8,128)(2,1)S(1)}, bf16[2,128,512]{2,1,0:T(8,128)(2,1)S(1)}, u32[]{:S(2)}, u32[]{:S(2)}) collective-permute-start(bf16[2,128,512]{2,1,0:T(8,128)(2,1)S(1)} %dynamic-slice_bitcast_fusion.4), channel_id=1, source_target_pairs={{0,4},{1,5},{2,6},{3,7},{4,0},{5,1},{6,2},{7,3},{8,12},{9,13},{10,... | collective-permute-start | bytes 786440 | tf_op jit(solution)/shard_map/ppermute | solution.py:340
  118.0 14.4 %collective-permute-start.15 = (bf16[1,128,512]{2,1,0:T(8,128)(2,1)S(1)}, bf16[1,128,512]{2,1,0:T(8,128)(2,1)S(1)}, u32[]{:S(2)}, u32[]{:S(2)}) collective-permute-start(bf16[1,128,512]{2,1,0:T(8,128)(2,1)S(1)} %constant_dynamic-slice_fusion.2), channel_id=1, source_target_pairs={{0,8},{1,9},{2,10},{3,11},{4,12},{5,13},{6,14},{7,15},{8,0},{9,1},... | collective-permute-start | bytes 393224 | tf_op jit(solution)/shard_map/ppermute | solution.py:340
  121.4 13.8 %collective-permute-start.23 = (bf16[1,128,512]{2,1,0:T(8,128)(2,1)S(1)}, bf16[1,128,512]{2,1,0:T(8,128)(2,1)S(1)}, u32[]{:S(2)}, u32[]{:S(2)}) collective-permute-start(bf16[1,128,512]{2,1,0:T(8,128)(2,1)S(1)} %constant_dynamic-slice_fusion), channel_id=1, source_target_pairs={{0,8},{1,9},{2,10},{3,11},{4,12},{5,13},{6,14},{7,15},{8,0},{9,1},... | collective-permute-start | bytes 393224 | tf_op jit(solution)/shard_map/ppermute | solution.py:340
  121.8 15.2 %collective-permute-start.19 = (bf16[1,128,512]{2,1,0:T(8,128)(2,1)S(1)}, bf16[1,128,512]{2,1,0:T(8,128)(2,1)S(1)}, u32[]{:S(2)}, u32[]{:S(2)}) collective-permute-start(bf16[1,128,512]{2,1,0:T(8,128)(2,1)S(1)} %constant_dynamic-slice_fusion.1), channel_id=1, source_target_pairs={{0,8},{1,9},{2,10},{3,11},{4,12},{5,13},{6,14},{7,15},{8,0},{9,1},... | collective-permute-start | bytes 393224 | tf_op jit(solution)/shard_map/ppermute | solution.py:340
